TPU v7x, 128 devices: a whole 4x4x4 slice. The times are simulated.
128 devices in a mesh: dp: 8 (over x, y_lo), expert: 16 (over z, y_hi, core).
Axes of the slice: x: 4, y: 4 (y_hi: 2, y_lo: 2; y = y_hi * 2 + y_lo), z: 4, core: 2. Of those that a mesh axis runs over, the one named last changes fastest.
Arguments:
- tokens: bfloat16 [32768, 1536], P(('dp', 'expert')), may hold values from -24 to 24
- cotangent: bfloat16 [32768, 1536], P(('dp', 'expert')), may hold values from -0.59765625 to 0.59765625
- chosen: int32 [512, 16, 8], P(('dp', 'expert')), may hold values from 0 to 63, as said below
- w_router: bfloat16 [1536, 16], replicated, may hold values from -0.15625 to 0.15625
- w_gate: bfloat16 [16, 1536, 1024], P('expert', 'dp'), may hold values from -0.15625 to 0.15625
- w_up: bfloat16 [16, 1536, 1024], P('expert', 'dp'), may hold values from -0.15625 to 0.15625
- w_down: bfloat16 [16, 1024, 1536], P('expert', 'dp'), may hold values from -0.1875 to 0.1875
Outputs:
- mixed: bfloat16 [32768, 1536], P(('dp', 'expert'))
- grad_tokens: bfloat16 [32768, 1536], P(('dp', 'expert'))
- grad_gate: float32 [16, 1536, 1024], P('expert', 'dp')
- grad_up: float32 [16, 1536, 1024], P('expert', 'dp')
- down_weight_gradient: float32 [16, 1024, 1536], P('expert', 'dp')
- grad_router: float32 [1536, 16], replicated
Inputs may be any that keep to these rules, and one draw needn't show every extreme that they name: `chosen`: for each aligned block of 64 token rows and each expert, 8 different row numbers within the block; so every device has exactly 32 slots for each expert.
All inputs are finite; a program needn't handle non-finite values.
Results may differ from a plain program's by a relative error of at most 0.017.
Values may be sent and summed in bfloat16 or wider, within the bound.
A program may use at most 128 MiB of HBM per device.

v0:
```python
import functools

import jax
import jax.numpy as jnp
from jax import lax
from jax.experimental import pallas as pl
from jax.experimental.pallas import tpu as pltpu
from jax.sharding import PartitionSpec as P

MESH = pl.DeviceIdType.MESH


def _gather_kernel(n, *refs):
    count = (len(refs) - 3) // 2
    srcs, dsts = refs[:count], refs[count : 2 * count]
    send_sem, recv_sem, local_sem = refs[2 * count :]
    me = lax.axis_index("dp")
    ex = lax.axis_index("expert")
    barrier = pltpu.get_barrier_semaphore()
    for k in range(1, n):
        pl.semaphore_signal(barrier, inc=1, device_id=(lax.rem(me + k, n), ex), device_id_type=MESH)
    pl.semaphore_wait(barrier, n - 1)
    copies = []
    for a in range(count):
        rows = srcs[a].shape[0]
        slot = dsts[a].at[pl.ds(me * rows, rows)]
        local = pltpu.make_async_copy(srcs[a], slot, local_sem.at[a])
        local.start()
        copies.append(local)
        for k in range(1, n):
            remote = pltpu.make_async_remote_copy(
                src_ref=srcs[a],
                dst_ref=slot,
                send_sem=send_sem.at[a, k],
                recv_sem=recv_sem.at[a, k],
                device_id=(lax.rem(me + k, n), ex),
                device_id_type=MESH,
            )
            remote.start()
            copies.append(remote)
    for c in copies:
        c.wait()


def dp_all_gather(shards, n):
    count = len(shards)
    return pl.pallas_call(
        functools.partial(_gather_kernel, n),
        out_shape=[jax.ShapeDtypeStruct((n * s.shape[0],) + s.shape[1:], s.dtype) for s in shards],
        in_specs=[pl.BlockSpec(memory_space=pl.ANY)] * count,
        out_specs=[pl.BlockSpec(memory_space=pl.ANY)] * count,
        scratch_shapes=[
            pltpu.SemaphoreType.DMA((count, n)),
            pltpu.SemaphoreType.DMA((count, n)),
            pltpu.SemaphoreType.DMA((count,)),
        ],
        compiler_params=pltpu.CompilerParams(collective_id=0, has_side_effects=True),
    )(*shards)


def _exchange_kernel(n, n_scatter, *refs):
    count = (len(refs) - 3) // 2
    srcs, dsts = refs[:count], refs[count : 2 * count]
    send_sem, recv_sem, local_sem = refs[2 * count :]
    me = lax.axis_index("dp")
    ex = lax.axis_index("expert")
    barrier = pltpu.get_barrier_semaphore()
    for k in range(1, n):
        pl.semaphore_signal(barrier, inc=1, device_id=(lax.rem(me + k, n), ex), device_id_type=MESH)
    pl.semaphore_wait(barrier, n - 1)
    copies = []
    for a in range(count):
        rows = dsts[a].shape[1]
        if a < n_scatter:
            mine = srcs[a].at[pl.ds(me * rows, rows)]
        else:
            mine = srcs[a]
        local = pltpu.make_async_copy(mine, dsts[a].at[me], local_sem.at[a])
        local.start()
        copies.append(local)
        for k in range(1, n):
            peer = lax.rem(me + k, n)
            if a < n_scatter:
                part = srcs[a].at[pl.ds(peer * rows, rows)]
            else:
                part = srcs[a]
            remote = pltpu.make_async_remote_copy(
                src_ref=part,
                dst_ref=dsts[a].at[me],
                send_sem=send_sem.at[a, k],
                recv_sem=recv_sem.at[a, k],
                device_id=(peer, ex),
                device_id_type=MESH,
            )
            remote.start()
            copies.append(remote)
    for c in copies:
        c.wait()


def dp_exchange(partials, replicas, n):
    arrays = list(partials) + list(replicas)
    count = len(arrays)
    shapes = [(n, p.shape[0] // n) + p.shape[1:] for p in partials]
    shapes += [(n,) + r.shape for r in replicas]
    received = pl.pallas_call(
        functools.partial(_exchange_kernel, n, len(partials)),
        out_shape=[jax.ShapeDtypeStruct(s, a.dtype) for s, a in zip(shapes, arrays)],
        in_specs=[pl.BlockSpec(memory_space=pl.ANY)] * count,
        out_specs=[pl.BlockSpec(memory_space=pl.ANY)] * count,
        scratch_shapes=[
            pltpu.SemaphoreType.DMA((count, n)),
            pltpu.SemaphoreType.DMA((count, n)),
            pltpu.SemaphoreType.DMA((count,)),
        ],
        compiler_params=pltpu.CompilerParams(collective_id=1, has_side_effects=True),
    )(*arrays)
    return [jnp.sum(r.astype(jnp.float32), axis=0) for r in received]


def _shift_pairs(n, k):
    return [(i, (i + k) % n) for i in range(n)]


def dp_gather_permute(shard, n):
    me = lax.axis_index("dp")
    full = jnp.zeros((n,) + shard.shape, shard.dtype)
    full = lax.dynamic_update_index_in_dim(full, shard, me, 0)
    for k in range(1, n):
        got = lax.ppermute(shard, "dp", perm=_shift_pairs(n, k))
        full = lax.dynamic_update_index_in_dim(full, got, lax.rem(me + n - k, n), 0)
    return full


def dp_scatter_permute(partial, n):
    me = lax.axis_index("dp")
    blocks = partial.reshape((n, partial.shape[0] // n) + partial.shape[1:])
    total = lax.dynamic_index_in_dim(blocks, me, 0, keepdims=False).astype(jnp.float32)
    for k in range(1, n):
        piece = lax.dynamic_index_in_dim(blocks, lax.rem(me + k, n), 0, keepdims=False)
        got = lax.ppermute(piece, "dp", perm=_shift_pairs(n, k))
        total = total + got.astype(jnp.float32)
    return total


def _x_shift(n, d):
    return [(i, (i + 2 * d) % n) for i in range(n)]


def _y_pair(n):
    return [(i, i ^ 1) for i in range(n)]


def x_ring_gather(t, n):
    from_left = lax.ppermute(t, "dp", _x_shift(n, 1))
    from_right = lax.ppermute(t, "dp", _x_shift(n, -1))
    h = t.shape[0] // 2
    first = lax.ppermute(from_left[:h], "dp", _x_shift(n, 1))
    second = lax.ppermute(from_right[h:], "dp", _x_shift(n, -1))
    return [t, from_right, jnp.concatenate([first, second], axis=0), from_left]


def dp_gather_2d(t, n):
    assert n == 8
    me = lax.axis_index("dp")
    x, l, nx = me // 2, me % 2, n // 2
    partner = lax.ppermute(t, "dp", _y_pair(n))
    stacked = jnp.stack(x_ring_gather(t, n) + x_ring_gather(partner, n))
    p = jnp.arange(n, dtype=jnp.int32)
    order = (p // 2 - x) % nx + nx * (p % 2 != l).astype(jnp.int32)
    return jnp.take(stacked, order, axis=0)


def x_ring_scatter(blocks, n):
    h = blocks[0].shape[0] // 2
    low = lax.ppermute(blocks[2][:h].astype(jnp.bfloat16), "dp", _x_shift(n, 1))
    high = lax.ppermute(blocks[2][h:].astype(jnp.bfloat16), "dp", _x_shift(n, -1))
    to_right = jnp.concatenate([blocks[1][:h] + low.astype(jnp.float32), blocks[1][h:]], axis=0)
    to_left = jnp.concatenate([blocks[3][:h], blocks[3][h:] + high.astype(jnp.float32)], axis=0)
    from_left = lax.ppermute(to_right.astype(jnp.bfloat16), "dp", _x_shift(n, 1))
    from_right = lax.ppermute(to_left.astype(jnp.bfloat16), "dp", _x_shift(n, -1))
    return blocks[0] + from_left.astype(jnp.float32) + from_right.astype(jnp.float32)


def dp_scatter_2d(partial, n):
    assert n == 8
    me = lax.axis_index("dp")
    x, l, nx = me // 2, me % 2, n // 2
    blocks = partial.reshape((n, partial.shape[0] // n) + partial.shape[1:])

    def pick(m, side):
        index = 2 * ((x + m) % nx) + side
        return lax.dynamic_index_in_dim(blocks, index, 0, keepdims=False).astype(jnp.float32)

    partner_sum = x_ring_scatter([pick(m, 1 - l) for m in range(nx)], n)
    sent = lax.ppermute(partner_sum.astype(jnp.bfloat16), "dp", _y_pair(n))
    own_sum = x_ring_scatter([pick(m, l) for m in range(nx)], n)
    return own_sum + sent.astype(jnp.float32)


def _ring_gather_kernel(n, shard_ref, out_ref, send_sem, recv_sem, local_sem):
    me = lax.axis_index("dp")
    ex = lax.axis_index("expert")
    right, left, partner = lax.rem(me + 2, n), lax.rem(me + n - 2, n), me + 1 - 2 * lax.rem(me, 2)
    barrier = pltpu.get_barrier_semaphore()
    for peer in (right, left, partner):
        pl.semaphore_signal(barrier, inc=1, device_id=(peer, ex), device_id_type=MESH)
    pl.semaphore_wait(barrier, 3)
    half = shard_ref.shape[0] // 2

    def send(role, src, slot, rows, peer):
        copy = pltpu.make_async_remote_copy(
            src_ref=src,
            dst_ref=out_ref.at[slot, rows],
            send_sem=send_sem.at[role],
            recv_sem=recv_sem.at[role],
            device_id=(peer, ex),
            device_id_type=MESH,
        )
        copy.start()
        return copy

    whole, low, high = pl.ds(0, 2 * half), pl.ds(0, half), pl.ds(half, half)
    local = pltpu.make_async_copy(shard_ref, out_ref.at[me], local_sem.at[0])
    local.start()
    first = [
        send(0, shard_ref, me, whole, right),
        send(1, shard_ref, me, whole, left),
        send(2, shard_ref, me, whole, partner),
    ]
    for copy in first:
        copy.wait_recv()
    mate = partner
    second = [
        send(3, out_ref.at[left, low], left, low, right),
        send(4, out_ref.at[right, high], right, high, left),
        send(5, out_ref.at[mate], mate, whole, right),
        send(6, out_ref.at[mate], mate, whole, left),
    ]
    second[2].wait_recv()
    second[3].wait_recv()
    mate_left, mate_right = lax.rem(mate + n - 2, n), lax.rem(mate + 2, n)
    third = [
        send(7, out_ref.at[mate_left, low], mate_left, low, right),
        send(8, out_ref.at[mate_right, high], mate_right, high, left),
    ]
    for copy in first:
        copy.wait_send()
    for copy in second[:2]:
        copy.wait_recv()
    for copy in second:
        copy.wait_send()
    for copy in third:
        copy.wait_recv()
        copy.wait_send()
    local.wait()


def dp_gather_kernel(shard, n):
    assert n == 8
    return pl.pallas_call(
        functools.partial(_ring_gather_kernel, n),
        out_shape=jax.ShapeDtypeStruct((n,) + shard.shape, shard.dtype),
        in_specs=[pl.BlockSpec(memory_space=pl.ANY)],
        out_specs=pl.BlockSpec(memory_space=pl.ANY),
        scratch_shapes=[
            pltpu.SemaphoreType.DMA((9,)),
            pltpu.SemaphoreType.DMA((9,)),
            pltpu.SemaphoreType.DMA((1,)),
        ],
        compiler_params=pltpu.CompilerParams(collective_id=2, has_side_effects=True),
    )(shard)


def to_blocks(slot_array, num_blocks, pick_count):
    expert_count = slot_array.shape[0]
    trailing = slot_array.shape[2:]
    grouped = slot_array.reshape((expert_count, num_blocks, pick_count) + trailing)
    axis_order = (1, 0, 2) + tuple(range(3, 3 + len(trailing)))
    return jnp.transpose(grouped, axis_order).reshape(
        (num_blocks, expert_count * pick_count) + trailing
    )


def weight_grads(expert_rows, hidden, expert_cot, d_pre_gate, d_pre_up, router_part, n):
    hidden_activations = hidden.shape[2]
    out_part = jnp.einsum(
        "erc,erd->cd", hidden, expert_cot, preferred_element_type=jnp.float32
    ).astype(jnp.bfloat16)
    out_share = dp_scatter_2d(out_part, n)
    both_grads = jnp.concatenate([d_pre_gate, d_pre_up], axis=2)
    in_part = jnp.einsum(
        "erc,erk->ck", expert_rows, both_grads, preferred_element_type=jnp.float32
    ).astype(jnp.bfloat16)
    in_share = dp_scatter_2d(in_part, n)
    grad_router = jnp.sum(
        lax.all_to_all(
            jnp.broadcast_to(router_part[None], (n,) + router_part.shape), "dp", 0, 0, tiled=True
        ),
        axis=0,
    )
    grad_gate = in_share[None, :, :hidden_activations]
    grad_up = in_share[None, :, hidden_activations:]
    down_weight_gradient = out_share[None]
    return (grad_gate, grad_up, down_weight_gradient, grad_router)


def body(tokens, cotangent, chosen, w_router, w_gate, w_up, w_down):
    tok_rows, model_width = tokens.shape
    num_blocks, expert_count, pick_count = chosen.shape
    block_rows = tok_rows // num_blocks
    slot_count = num_blocks * pick_count
    logits = jnp.dot(tokens, w_router, preferred_element_type=jnp.float32)
    gate_values = jax.nn.sigmoid(logits)
    offsets = (jnp.arange(num_blocks, dtype=jnp.int32) * block_rows)[:, None, None]
    slot_rows = jnp.transpose(chosen + offsets, (1, 0, 2)).reshape(expert_count, slot_count)
    picked = tokens[slot_rows]
    slot_gate_values = jnp.take_along_axis(gate_values.T, slot_rows, axis=1)
    cot_rows = cotangent[slot_rows]
    scaled_cot = (slot_gate_values[:, :, None] * cot_rows.astype(jnp.float32)).astype(jnp.bfloat16)
    n = lax.axis_size("dp")
    shard_rows = w_gate.shape[1]
    packed = jnp.concatenate(
        [w_gate[0], w_up[0], w_down[0].reshape(-1, w_gate.shape[2])], axis=0
    )
    full = dp_gather_kernel(packed, n)
    full_gate = full[:, :shard_rows].reshape(1, -1, w_gate.shape[2])
    full_up = full[:, shard_rows : 2 * shard_rows].reshape(1, -1, w_up.shape[2])
    full_down = full[:, 2 * shard_rows :].reshape(1, -1, w_down.shape[2])
    expert_count_axis = lax.axis_size("expert")
    expert_rows = lax.all_to_all(picked, "expert", 0, 0, tiled=True).reshape(1, -1, model_width)
    pre_gate = jnp.einsum(
        "erd,edh->erh", expert_rows, full_gate, preferred_element_type=jnp.float32
    )
    pre_up = jnp.einsum("erd,edh->erh", expert_rows, full_up, preferred_element_type=jnp.float32)
    silu_gate = jax.nn.silu(pre_gate)
    hidden = (silu_gate * pre_up).astype(jnp.bfloat16)
    expert_out = jnp.einsum(
        "erh,ehd->erd", hidden, full_down, preferred_element_type=jnp.float32
    ).astype(jnp.bfloat16)
    returned = lax.all_to_all(
        expert_out.reshape(expert_count_axis, -1, model_width), "expert", 0, 0, tiled=True
    )
    expert_cot = lax.all_to_all(scaled_cot, "expert", 0, 0, tiled=True).reshape(1, -1, model_width)
    back_gate, back_up, back_down = (full_gate, full_up, full_down)
    d_hidden = jnp.einsum("erd,ehd->erh", expert_cot, back_down, preferred_element_type=jnp.float32)
    gate_sigmoid = jax.nn.sigmoid(pre_gate)
    d_pre_gate = (
        d_hidden * pre_up * gate_sigmoid * (1.0 + pre_gate * (1.0 - gate_sigmoid))
    ).astype(jnp.bfloat16)
    d_pre_up = (d_hidden * silu_gate).astype(jnp.bfloat16)
    d_rows = (
        jnp.einsum("erh,edh->erd", d_pre_gate, back_gate, preferred_element_type=jnp.float32)
        + jnp.einsum("erh,edh->erd", d_pre_up, back_up, preferred_element_type=jnp.float32)
    ).astype(jnp.bfloat16)
    row_grads = lax.all_to_all(
        d_rows.reshape(expert_count_axis, -1, model_width), "expert", 0, 0, tiled=True
    )
    position_hits = chosen[:, :, :, None] == jnp.arange(block_rows, dtype=jnp.int32)
    indicator_matrix = position_hits.reshape(num_blocks, expert_count * pick_count, block_rows)
    gate_weighted_rows = to_blocks(slot_gate_values, num_blocks, pick_count)[
        :, :, None
    ] * to_blocks(returned, num_blocks, pick_count).astype(jnp.float32)
    mixed = (
        jnp.einsum(
            "wze,wzi->wei",
            indicator_matrix.astype(jnp.float32),
            gate_weighted_rows,
            precision=lax.Precision.HIGHEST,
        )
        .reshape(tok_rows, model_width)
        .astype(jnp.bfloat16)
    )
    slot_dots = jnp.sum(cot_rows.astype(jnp.float32) * returned.astype(jnp.float32), axis=2)
    dgate = jnp.einsum(
        "bept,ebp->bte",
        position_hits.astype(jnp.float32),
        slot_dots.reshape(expert_count, num_blocks, pick_count),
        precision=lax.Precision.HIGHEST,
    ).reshape(tok_rows, expert_count)
    d_logit = (dgate * gate_values * (1.0 - gate_values)).astype(jnp.bfloat16)
    gathered_grads = jnp.einsum(
        "wze,wzi->wei",
        indicator_matrix.astype(jnp.bfloat16),
        to_blocks(row_grads, num_blocks, pick_count),
        preferred_element_type=jnp.float32,
    ).reshape(tok_rows, model_width)
    grad_tokens = (
        gathered_grads + jnp.dot(d_logit, w_router.T, preferred_element_type=jnp.float32)
    ).astype(jnp.bfloat16)
    router_full = jnp.dot(tokens.T, d_logit, preferred_element_type=jnp.float32)
    router_part = jnp.sum(
        lax.all_to_all(router_full.reshape(expert_count_axis, -1, 128), "expert", 0, 0, tiled=True),
        axis=0,
    )
    grad_gate, grad_up, down_weight_gradient, grad_router = weight_grads(
        expert_rows, hidden, expert_cot, d_pre_gate, d_pre_up, router_part, n
    )
    grad_router = lax.all_to_all(
        jnp.broadcast_to(grad_router[None], (expert_count_axis,) + grad_router.shape),
        "expert",
        0,
        0,
        tiled=True,
    ).reshape(router_full.shape)
    return (mixed, grad_tokens, grad_gate, grad_up, down_weight_gradient, grad_router)


def solution(mesh):
    placed = (
        P(("dp", "expert"), None),
        P(("dp", "expert"), None),
        P(("dp", "expert"), None, None),
        P(),
        P("expert", "dp", None),
        P("expert", "dp", None),
        P("expert", "dp", None),
    )
    return jax.shard_map(
        body,
        mesh=mesh,
        in_specs=placed,
        out_specs=(
            P(("dp", "expert"), None),
            P(("dp", "expert"), None),
            P("expert", "dp", None),
            P("expert", "dp", None),
            P("expert", "dp", None),
            P(),
        ),
        check_vma=False,
    )
```

profile of v0, /device:TPU:5, one launch (start us, length us, event | category | flops | bytes accessed | tf_op | source)
XLA Modules:
  0.0 300.8 jit_solution(17272174830103364338)
XLA Ops:
  1.8 2.9 gather_fusion
  4.7 8.8 %all-to-all-start = ((bf16[16,32,1536]{2,1,0:T(8,128)(2,1)}), bf16[16,32,1536]{2,1,0:T(8,128)(2,1)}, u32[]{:S(2)}, u32[]{:S(2)}) async-start(bf16[16,32,1536]{2,1,0:T(8,128)(2,1)} %bitcast.5), calls=%async_computation | async-start | bytes 3145728 | tf_op jit(solution)/shard_map/all_to_all | solution.py:331
  14.1 4.5 %gather_fusion.2 = f32[512]{0:T(512)S(1)} fusion(f32[16,256]{1,0:T(8,128)S(1)} %bitcast.185, s32[512]{0:T(512)S(1)} %reshape.312), kind=kCustom, calls=%fused_computation.2 | custom fusion | bytes 8192 | tf_op jit(solution)/shard_map/jit(take_along_axis)/gather | solution.py:318
  21.8 88.8 %shard_map.118 = bf16[8,576,1024]{2,1,0:T(8,128)(2,1)} custom-call(bf16[576,1024]{1,0:T(8,128)(2,1)} %pad_maximum_fusion.shard_ref), custom_call_target="tpu_custom_call" | custom-call | tf_op jit(solution)/shard_map/pallas_call | solution.py:261
  114.5 9.3 %all-to-all-start.2 = ((bf16[16,32,1536]{2,1,0:T(8,128)(2,1)}), bf16[16,32,1536]{2,1,0:T(8,128)(2,1)}, u32[]{:S(2)}, u32[]{:S(2)}) async-start(bf16[16,32,1536]{2,1,0:T(8,128)(2,1)} %fusion), calls=%async_computation.2 | async-start | bytes 3145728 | tf_op jit(solution)/shard_map/all_to_all | solution.py:344
  123.8 6.8 %fusion.39 = (bf16[8,192,1024]{2,1,0:T(8,128)(2,1)}, bf16[8,192,1024]{2,1,0:T(8,128)(2,1)}, bf16[8,192,1024]{2,1,0:T(8,128)(2,1)}) fusion(bf16[8,576,1024]{2,1,0:T(8,128)(2,1)} %shard_map.118), kind=kLoop, calls=%fused_computation.117 | loop fusion | bytes 18874368 | tf_op jit(solution)/shard_map/slice | solution.py:329
  130.6 5.9 %reshape.267 = bf16[1024,1536]{1,0:T(8,128)(2,1)} reshape(bf16[8,192,1024]{2,1,0:T(8,128)(2,1)} %get-tuple-element.44) | data formatting | bytes 6291456 | tf_op jit(solution)/shard_map/reshape.12
  136.5 5.6 %fusion.40 = f32[512,1024]{1,0:T(8,128)} fusion(bf16[512,1536]{1,0:T(8,128)(2,1)} %bitcast.6, bf16[1536,1024]{1,0:T(8,128)(2,1)} %bitcast.194), kind=kOutput, calls=%fused_computation.118 | convolution fusion | flops 1610612736 | bytes 6815744 | tf_op jit(solution)/shard_map/erd,edh->erh/dot_general | solution.py:332
  142.1 4.6 %fusion.41 = f32[512,1024]{1,0:T(8,128)} fusion(bf16[512,1536]{1,0:T(8,128)(2,1)} %bitcast.6, bf16[1536,1024]{1,0:T(8,128)(2,1)S(1)} %bitcast.192), kind=kOutput, calls=%fused_computation.119 | convolution fusion | flops 1610612736 | bytes 6815744 | tf_op jit(solution)/shard_map/erd,edh->erh/dot_general | solution.py:335
  146.8 7.2 %multiply_convert_fusion = (bf16[512,1024]{1,0:T(8,128)(2,1)S(1)}, bf16[512,1024]{1,0:T(8,128)(2,1)}, bf16[512,1024]{1,0:T(8,128)(2,1)S(1)}) fusion(f32[512,1024]{1,0:T(8,128)} %fusion.40, f32[512,1024]{1,0:T(8,128)} %fusion.41, bf16[512,1536]{1,0:T(8,128)(2,1)} %bitcast.19, bf16[1024,1536]{1,0:T(8,128)(2,1)} %reshape.267), kind=kOutput, calls=%fused_computation.23 | convolution fusion | flops 1618477056 | bytes 12058624 | tf_op jit(solution)/shard_map/erd,ehd->erh/dot_general | solution.py:346
  154.0 3.0 convolution_convert_fusion.2
  156.9 5.0 %convolution_convert_fusion.1 = bf16[1024,1536]{1,0:T(8,128)(2,1)} fusion(bf16[512,1024]{1,0:T(8,128)(2,1)S(1)} %get-tuple-element.61, bf16[512,1536]{1,0:T(8,128)(2,1)} %bitcast.19), kind=kOutput, calls=%fused_computation.7 | convolution fusion | flops 1612185600 | bytes 5767168 | tf_op jit(solution)/shard_map/erc,erd->cd/dot_general | solution.py:287
  161.9 7.2 %all-to-all-start.1 = ((bf16[16,32,1536]{2,1,0:T(8,128)(2,1)}), bf16[16,32,1536]{2,1,0:T(8,128)(2,1)}, u32[]{:S(2)}, u32[]{:S(2)}) async-start(bf16[16,32,1536]{2,1,0:T(8,128)(2,1)} %bitcast.201), calls=%async_computation.1 | async-start | bytes 3145728 | tf_op jit(solution)/shard_map/all_to_all | solution.py:341
  169.2 4.2 %fusion.42 = f32[512,1536]{1,0:T(8,128)S(1)} fusion(bf16[512,1024]{1,0:T(8,128)(2,1)} %get-tuple-element.60, bf16[1536,1024]{1,0:T(8,128)(2,1)} %bitcast.195), kind=kOutput, calls=%fused_computation.120 | convolution fusion | flops 1610612736 | bytes 7340032 | tf_op jit(solution)/shard_map/erh,edh->erd/dot_general | solution.py:353
  173.5 2.2 collective-permute-start.9
  177.2 3.0 fusion.4
  180.2 5.2 %convolution_convert_fusion = bf16[1536,2048]{1,0:T(8,128)(2,1)S(1)} fusion(bf16[512,1536]{1,0:T(8,128)(2,1)} %bitcast.6, bf16[1,512,1024]{2,1,0:T(8,128)(2,1)S(1)} %bitcast.206, bf16[1,512,1024]{2,1,0:T(8,128)(2,1)S(1)} %bitcast.207), kind=kOutput, calls=%fused_computation.3 | convolution fusion | flops 3228565504 | bytes 9961472 | tf_op jit(solution)/shard_map/erc,erk->ck/dot_general | solution.py:292
  189.6 2.7 collective-permute-start.16
  196.5 7.8 %collective-permute-done.4 = bf16[96,2048]{1,0:T(8,128)(2,1)S(1)} collective-permute-done((bf16[96,2048]{1,0:T(8,128)(2,1)S(1)}, bf16[96,2048]{1,0:T(8,128)(2,1)S(1)}, u32[]{:S(2)}, u32[]{:S(2)}) %collective-permute-start.4) | collective-permute-done | bytes 393248 | tf_op jit(solution)/shard_map/ppermute | solution.py:176
  209.8 4.8 %collective-permute-done.16 = bf16[128,1536]{1,0:T(8,128)(2,1)S(1)} collective-permute-done((bf16[128,1536]{1,0:T(8,128)(2,1)S(1)}, bf16[128,1536]{1,0:T(8,128)(2,1)S(1)}, u32[]{:S(2)}, u32[]{:S(2)}) %collective-permute-start.16) | collective-permute-done | bytes 393248 | tf_op jit(solution)/shard_map/ppermute | solution.py:181
  219.5 12.5 %all-to-all-start.3 = ((bf16[16,32,1536]{2,1,0:T(8,128)(2,1)}), bf16[16,32,1536]{2,1,0:T(8,128)(2,1)}, u32[]{:S(2)}, u32[]{:S(2)}) async-start(bf16[16,32,1536]{2,1,0:T(8,128)(2,1)} %bitcast.200), calls=%async_computation.3 | async-start | bytes 3145728 | tf_op jit(solution)/shard_map/all_to_all | solution.py:356
  233.6 2.3 fusion.25
  235.9 4.1 %collective-permute-done.7 = bf16[192,2048]{1,0:T(8,128)(2,1)} collective-permute-done((bf16[192,2048]{1,0:T(8,128)(2,1)}, bf16[192,2048]{1,0:T(8,128)(2,1)}, u32[]{:S(2)}, u32[]{:S(2)}) %collective-permute-start.7) | collective-permute-done | bytes 786464 | tf_op jit(solution)/shard_map/ppermute | solution.py:181
  240.0 2.9 fusion.11
  246.9 8.1 %all-to-all-done.3 = bf16[16,32,1536]{2,1,0:T(8,128)(2,1)} async-done(((bf16[16,32,1536]{2,1,0:T(8,128)(2,1)}), bf16[16,32,1536]{2,1,0:T(8,128)(2,1)}, u32[]{:S(2)}, u32[]{:S(2)}) %all-to-all-start.3) | async-done | bytes 1572896 | tf_op jit(solution)/shard_map/all_to_all | solution.py:356
  255.0 4.6 %all-to-all-start.4 = ((f32[16,12,128]{2,1,0:T(8,128)}), f32[16,12,128]{2,1,0:T(8,128)S(1)}, u32[]{:S(2)}, u32[]{:S(2)}) async-start(f32[16,12,128]{2,1,0:T(8,128)} %reshape.280), calls=%async_computation.4 | async-start | bytes 262144 | tf_op jit(solution)/shard_map/all_to_all | solution.py:393
  261.4 12.0 %all-to-all-done.4 = f32[16,12,128]{2,1,0:T(8,128)S(1)} async-done(((f32[16,12,128]{2,1,0:T(8,128)}), f32[16,12,128]{2,1,0:T(8,128)S(1)}, u32[]{:S(2)}, u32[]{:S(2)}) %all-to-all-start.4) | async-done | bytes 98336 | tf_op jit(solution)/shard_map/all_to_all | solution.py:393
  274.1 5.7 %all-to-all-start.5 = ((f32[8,12,128]{2,1,0:T(8,128)}), f32[8,12,128]{2,1,0:T(8,128)S(1)}, u32[]{:S(2)}, u32[]{:S(2)}) async-start(f32[8,12,128]{2,1,0:T(8,128)} %broadcast_in_dim.38), calls=%async_computation.5 | async-start | bytes 131072 | tf_op jit(solution)/shard_map/all_to_all | solution.py:297
  281.1 2.2 all-to-all-done.5
  284.0 4.6 %all-to-all-start.6 = ((f32[16,12,128]{2,1,0:T(8,128)}), f32[16,12,128]{2,1,0:T(8,128)S(1)}, u32[]{:S(2)}, u32[]{:S(2)}) async-start(f32[16,12,128]{2,1,0:T(8,128)} %broadcast_in_dim.39), calls=%async_computation.6 | async-start | bytes 262144 | tf_op jit(solution)/shard_map/all_to_all | solution.py:399
  288.6 4.0 %fusion.5 = bf16[4,64,1536]{2,1,0:T(8,128)(2,1)} fusion(f32[4,128]{1,0:T(4,128)S(1)} %copy-done.16, s32[4,128]{1,0:T(4,128)S(1)} %copy-done.15, bf16[16,32,1536]{2,1,0:T(8,128)(2,1)} %all-to-all-done.1), kind=kOutput, calls=%fused_computation.17 | convolution fusion | flops 605978624 | bytes 2363392 | tf_op jit(solution)/shard_map/wze,wzi->wei/dot_general | solution.py:365
  292.6 3.8 %all-to-all-done.6 = f32[16,12,128]{2,1,0:T(8,128)S(1)} async-done(((f32[16,12,128]{2,1,0:T(8,128)}), f32[16,12,128]{2,1,0:T(8,128)S(1)}, u32[]{:S(2)}, u32[]{:S(2)}) %all-to-all-start.6) | async-done | bytes 98336 | tf_op jit(solution)/shard_map/all_to_all | solution.py:399
  (126 shorter events, 43.4 us)
Async XLA Ops:
  4.7 8.8 %copy-start.10 = (s32[4,16,8]{1,2,0:T(8,128)S(1)}, s32[4,16,8]{1,2,0:T(8,128)}, u32[]{:S(2)}) copy-start(s32[4,16,8]{1,2,0:T(8,128)} %param.9) | copy-start | bytes 6148
  4.7 9.0 %copy-start.11 = (bf16[1536,16]{0,1:T(8,128)(2,1)S(1)}, bf16[1536,16]{0,1:T(8,128)(2,1)}, u32[]{:S(2)}) copy-start(bf16[1536,16]{0,1:T(8,128)(2,1)} %param.10) | copy-start | bytes 147460
  4.7 109.8 %all-to-all-start = ((bf16[16,32,1536]{2,1,0:T(8,128)(2,1)}), bf16[16,32,1536]{2,1,0:T(8,128)(2,1)}, u32[]{:S(2)}, u32[]{:S(2)}) async-start(bf16[16,32,1536]{2,1,0:T(8,128)(2,1)} %bitcast.5), calls=%async_computation | async-start | bytes 3145728 | tf_op jit(solution)/shard_map/all_to_all | solution.py:331
  21.8 89.1 %copy-start.1 = (bf16[256,1536]{1,0:T(8,128)(2,1)S(1)}, bf16[256,1536]{1,0:T(8,128)(2,1)}, u32[]{:S(2)}) copy-start(bf16[256,1536]{1,0:T(8,128)(2,1)} %param.8) | copy-start | bytes 2359300
  114.5 32.3 %all-to-all-start.2 = ((bf16[16,32,1536]{2,1,0:T(8,128)(2,1)}), bf16[16,32,1536]{2,1,0:T(8,128)(2,1)}, u32[]{:S(2)}, u32[]{:S(2)}) async-start(bf16[16,32,1536]{2,1,0:T(8,128)(2,1)} %fusion), calls=%async_computation.2 | async-start | bytes 3145728 | tf_op jit(solution)/shard_map/all_to_all | solution.py:344
  161.9 57.6 %all-to-all-start.1 = ((bf16[16,32,1536]{2,1,0:T(8,128)(2,1)}), bf16[16,32,1536]{2,1,0:T(8,128)(2,1)}, u32[]{:S(2)}, u32[]{:S(2)}) async-start(bf16[16,32,1536]{2,1,0:T(8,128)(2,1)} %bitcast.201), calls=%async_computation.1 | async-start | bytes 3145728 | tf_op jit(solution)/shard_map/all_to_all | solution.py:341
  173.5 13.7 %collective-permute-start.9 = (bf16[64,1536]{1,0:T(8,128)(2,1)S(1)}, bf16[64,1536]{1,0:T(8,128)(2,1)S(1)}, u32[]{:S(2)}, u32[]{:S(2)}) collective-permute-start(bf16[64,1536]{1,0:T(8,128)(2,1)S(1)} %get-tuple-element.66), channel_id=1, source_target_pairs={{0,32},{16,48},{32,64},{48,80},{64,96},{80,112},{96,0},{112,16},{1... | collective-permute-start | bytes 589832 | tf_op jit(solution)/shard_map/ppermute | solution.py:176
  175.7 13.3 %collective-permute-start.13 = (bf16[64,1536]{1,0:T(8,128)(2,1)S(1)}, bf16[64,1536]{1,0:T(8,128)(2,1)S(1)}, u32[]{:S(2)}, u32[]{:S(2)}) collective-permute-start(bf16[64,1536]{1,0:T(8,128)(2,1)S(1)} %get-tuple-element.68), channel_id=1, source_target_pairs={{0,32},{16,48},{32,64},{48,80},{64,96},{80,112},{96,0},{112,16},{1... | collective-permute-start | bytes 589832 | tf_op jit(solution)/shard_map/ppermute | solution.py:176
  176.2 12.7 %collective-permute-start.15 = (bf16[64,1536]{1,0:T(8,128)(2,1)S(1)}, bf16[64,1536]{1,0:T(8,128)(2,1)S(1)}, u32[]{:S(2)}, u32[]{:S(2)}) collective-permute-start(bf16[64,1536]{1,0:T(8,128)(2,1)S(1)} %get-tuple-element.70), channel_id=1, source_target_pairs={{0,96},{16,112},{32,0},{48,16},{64,32},{80,48},{96,64},{112,80},{1... | collective-permute-start | bytes 589832 | tf_op jit(solution)/shard_map/ppermute | solution.py:177
  177.2 12.2 %collective-permute-start.11 = (bf16[64,1536]{1,0:T(8,128)(2,1)S(1)}, bf16[64,1536]{1,0:T(8,128)(2,1)S(1)}, u32[]{:S(2)}, u32[]{:S(2)}) collective-permute-start(bf16[64,1536]{1,0:T(8,128)(2,1)S(1)} %get-tuple-element.72), channel_id=1, source_target_pairs={{0,96},{16,112},{32,0},{48,16},{64,32},{80,48},{96,64},{112,80},{1... | collective-permute-start | bytes 589832 | tf_op jit(solution)/shard_map/ppermute | solution.py:177
  185.4 20.8 %copy-start.2 = (bf16[1536,2048]{1,0:T(8,128)(2,1)}, bf16[1536,2048]{1,0:T(8,128)(2,1)S(1)}, u32[]{:S(2)}) copy-start(bf16[1536,2048]{1,0:T(8,128)(2,1)S(1)} %convolution_convert_fusion) | copy-start | bytes 18874372
  185.7 10.3 %collective-permute-start = (bf16[96,2048]{1,0:T(8,128)(2,1)S(1)}, bf16[96,2048]{1,0:T(8,128)(2,1)S(1)}, u32[]{:S(2)}, u32[]{:S(2)}) collective-permute-start(bf16[96,2048]{1,0:T(8,128)(2,1)S(1)} %get-tuple-element.51), channel_id=1, source_target_pairs={{0,32},{16,48},{32,64},{48,80},{64,96},{80,112},{96,0},{112,16},{1... | collective-permute-start | bytes 1179656 | tf_op jit(solution)/shard_map/ppermute | solution.py:176
  187.2 17.2 %collective-permute-start.4 = (bf16[96,2048]{1,0:T(8,128)(2,1)S(1)}, bf16[96,2048]{1,0:T(8,128)(2,1)S(1)}, u32[]{:S(2)}, u32[]{:S(2)}) collective-permute-start(bf16[96,2048]{1,0:T(8,128)(2,1)S(1)} %get-tuple-element.53), channel_id=1, source_target_pairs={{0,32},{16,48},{32,64},{48,80},{64,96},{80,112},{96,0},{112,16},{1... | collective-permute-start | bytes 1179656 | tf_op jit(solution)/shard_map/ppermute | solution.py:176
  189.0 16.6 %collective-permute-start.6 = (bf16[96,2048]{1,0:T(8,128)(2,1)S(1)}, bf16[96,2048]{1,0:T(8,128)(2,1)S(1)}, u32[]{:S(2)}, u32[]{:S(2)}) collective-permute-start(bf16[96,2048]{1,0:T(8,128)(2,1)S(1)} %get-tuple-element.55), channel_id=1, source_target_pairs={{0,96},{16,112},{32,0},{48,16},{64,32},{80,48},{96,64},{112,80},{1... | collective-permute-start | bytes 1179656 | tf_op jit(solution)/shard_map/ppermute | solution.py:177
  189.0 17.2 %collective-permute-start.2 = (bf16[96,2048]{1,0:T(8,128)(2,1)S(1)}, bf16[96,2048]{1,0:T(8,128)(2,1)S(1)}, u32[]{:S(2)}, u32[]{:S(2)}) collective-permute-start(bf16[96,2048]{1,0:T(8,128)(2,1)S(1)} %get-tuple-element.57), channel_id=1, source_target_pairs={{0,96},{16,112},{32,0},{48,16},{64,32},{80,48},{96,64},{112,80},{1... | collective-permute-start | bytes 1179656 | tf_op jit(solution)/shard_map/ppermute | solution.py:177
  189.6 25.0 %collective-permute-start.16 = (bf16[128,1536]{1,0:T(8,128)(2,1)S(1)}, bf16[128,1536]{1,0:T(8,128)(2,1)S(1)}, u32[]{:S(2)}, u32[]{:S(2)}) collective-permute-start(bf16[128,1536]{1,0:T(8,128)(2,1)S(1)} %pad_maximum_fusion.8), channel_id=1, source_target_pairs={{0,96},{16,112},{32,0},{48,16},{64,32},{80,48},{96,64},{112,80},{1... | collective-permute-start | bytes 1179656 | tf_op jit(solution)/shard_map/ppermute | solution.py:181
  196.0 20.8 %collective-permute-start.14 = (bf16[128,1536]{1,0:T(8,128)(2,1)S(1)}, bf16[128,1536]{1,0:T(8,128)(2,1)S(1)}, u32[]{:S(2)}, u32[]{:S(2)}) collective-permute-start(bf16[128,1536]{1,0:T(8,128)(2,1)S(1)} %pad_maximum_fusion.7), channel_id=1, source_target_pairs={{0,32},{16,48},{32,64},{48,80},{64,96},{80,112},{96,0},{112,16},{1... | collective-permute-start | bytes 1179656 | tf_op jit(solution)/shard_map/ppermute | solution.py:180
  204.4 27.6 %collective-permute-start.12 = (bf16[128,1536]{1,0:T(8,128)(2,1)}, bf16[128,1536]{1,0:T(8,128)(2,1)S(1)}, u32[]{:S(2)}, u32[]{:S(2)}) collective-permute-start(bf16[128,1536]{1,0:T(8,128)(2,1)} %pad_maximum_fusion.6), channel_id=1, source_target_pairs={{0,96},{16,112},{32,0},{48,16},{64,32},{80,48},{96,64},{112,80},{1... | collective-permute-start | bytes 1179656 | tf_op jit(solution)/shard_map/ppermute | solution.py:181
  205.6 26.5 %collective-permute-start.10 = (bf16[128,1536]{1,0:T(8,128)(2,1)}, bf16[128,1536]{1,0:T(8,128)(2,1)}, u32[]{:S(2)}, u32[]{:S(2)}) collective-permute-start(bf16[128,1536]{1,0:T(8,128)(2,1)} %pad_maximum_fusion.5), channel_id=1, source_target_pairs={{0,32},{16,48},{32,64},{48,80},{64,96},{80,112},{96,0},{112,16},{1... | collective-permute-start | bytes 1179656 | tf_op jit(solution)/shard_map/ppermute | solution.py:180
  207.7 32.3 %collective-permute-start.7 = (bf16[192,2048]{1,0:T(8,128)(2,1)}, bf16[192,2048]{1,0:T(8,128)(2,1)}, u32[]{:S(2)}, u32[]{:S(2)}) collective-permute-start(bf16[192,2048]{1,0:T(8,128)(2,1)} %pad_maximum_fusion.4), channel_id=1, source_target_pairs={{0,96},{16,112},{32,0},{48,16},{64,32},{80,48},{96,64},{112,80},{1... | collective-permute-start | bytes 2359304 | tf_op jit(solution)/shard_map/ppermute | solution.py:181
  214.6 25.4 %collective-permute-start.5 = (bf16[192,2048]{1,0:T(8,128)(2,1)}, bf16[192,2048]{1,0:T(8,128)(2,1)}, u32[]{:S(2)}, u32[]{:S(2)}) collective-permute-start(bf16[192,2048]{1,0:T(8,128)(2,1)} %pad_maximum_fusion.3), channel_id=1, source_target_pairs={{0,32},{16,48},{32,64},{48,80},{64,96},{80,112},{96,0},{112,16},{1... | collective-permute-start | bytes 2359304 | tf_op jit(solution)/shard_map/ppermute | solution.py:180
  217.6 16.0 %collective-permute-start.17 = (bf16[128,1536]{1,0:T(8,128)(2,1)}, bf16[128,1536]{1,0:T(8,128)(2,1)}, u32[]{:S(2)}, u32[]{:S(2)}) collective-permute-start(bf16[128,1536]{1,0:T(8,128)(2,1)} %fusion.22), channel_id=1, source_target_pairs={{0,16},{16,0},{32,48},{48,32},{64,80},{80,64},{96,112},{112,96},{1... | collective-permute-start | bytes 1179656 | tf_op jit(solution)/shard_map/ppermute | solution.py:196
  219.5 35.5 %all-to-all-start.3 = ((bf16[16,32,1536]{2,1,0:T(8,128)(2,1)}), bf16[16,32,1536]{2,1,0:T(8,128)(2,1)}, u32[]{:S(2)}, u32[]{:S(2)}) async-start(bf16[16,32,1536]{2,1,0:T(8,128)(2,1)} %bitcast.200), calls=%async_computation.3 | async-start | bytes 3145728 | tf_op jit(solution)/shard_map/all_to_all | solution.py:356
  232.0 65.5 %collective-permute-start.3 = (bf16[192,2048]{1,0:T(8,128)(2,1)}, bf16[192,2048]{1,0:T(8,128)(2,1)S(1)}, u32[]{:S(2)}, u32[]{:S(2)}) collective-permute-start(bf16[192,2048]{1,0:T(8,128)(2,1)} %pad_maximum_fusion.2), channel_id=1, source_target_pairs={{0,96},{16,112},{32,0},{48,16},{64,32},{80,48},{96,64},{112,80},{1... | collective-permute-start | bytes 2359304 | tf_op jit(solution)/shard_map/ppermute | solution.py:181
  232.1 65.4 %collective-permute-start.1 = (bf16[192,2048]{1,0:T(8,128)(2,1)}, bf16[192,2048]{1,0:T(8,128)(2,1)}, u32[]{:S(2)}, u32[]{:S(2)}) collective-permute-start(bf16[192,2048]{1,0:T(8,128)(2,1)} %pad_maximum_fusion.1), channel_id=1, source_target_pairs={{0,32},{16,48},{32,64},{48,80},{64,96},{80,112},{96,0},{112,16},{1... | collective-permute-start | bytes 2359304 | tf_op jit(solution)/shard_map/ppermute | solution.py:180
  242.9 54.6 %collective-permute-start.8 = (bf16[192,2048]{1,0:T(8,128)(2,1)}, bf16[192,2048]{1,0:T(8,128)(2,1)}, u32[]{:S(2)}, u32[]{:S(2)}) collective-permute-start(bf16[192,2048]{1,0:T(8,128)(2,1)} %fusion.11), channel_id=1, source_target_pairs={{0,16},{16,0},{32,48},{48,32},{64,80},{80,64},{96,112},{112,96},{1... | collective-permute-start | bytes 2359304 | tf_op jit(solution)/shard_map/ppermute | solution.py:196
  244.8 14.9 %copy-start.15 = (s32[4,128]{1,0:T(4,128)S(1)}, s32[4,128]{1,0:T(4,128)}, u32[]{:S(2)}) copy-start(s32[4,128]{1,0:T(4,128)} %eq.41) | copy-start | bytes 6148
  246.9 32.9 %copy-start.12 = (bf16[1536,16]{0,1:T(8,128)(2,1)S(1)}, bf16[1536,16]{0,1:T(8,128)(2,1)}, u32[]{:S(2)}) copy-start(bf16[1536,16]{0,1:T(8,128)(2,1)} %param.10) | copy-start | bytes 147460
  255.0 18.4 %all-to-all-start.4 = ((f32[16,12,128]{2,1,0:T(8,128)}), f32[16,12,128]{2,1,0:T(8,128)S(1)}, u32[]{:S(2)}, u32[]{:S(2)}) async-start(f32[16,12,128]{2,1,0:T(8,128)} %reshape.280), calls=%async_computation.4 | async-start | bytes 262144 | tf_op jit(solution)/shard_map/all_to_all | solution.py:393
  261.4 27.2 %copy-start.16 = (f32[4,128]{1,0:T(4,128)S(1)}, f32[4,128]{1,0:T(4,128)}, u32[]{:S(2)}) copy-start(f32[4,128]{1,0:T(4,128)} %mul.88) | copy-start | bytes 6148
  274.1 9.2 %all-to-all-start.5 = ((f32[8,12,128]{2,1,0:T(8,128)}), f32[8,12,128]{2,1,0:T(8,128)S(1)}, u32[]{:S(2)}, u32[]{:S(2)}) async-start(f32[8,12,128]{2,1,0:T(8,128)} %broadcast_in_dim.38), calls=%async_computation.5 | async-start | bytes 131072 | tf_op jit(solution)/shard_map/all_to_all | solution.py:297
  284.0 12.4 %all-to-all-start.6 = ((f32[16,12,128]{2,1,0:T(8,128)}), f32[16,12,128]{2,1,0:T(8,128)S(1)}, u32[]{:S(2)}, u32[]{:S(2)}) async-start(f32[16,12,128]{2,1,0:T(8,128)} %broadcast_in_dim.39), calls=%async_computation.6 | async-start | bytes 262144 | tf_op jit(solution)/shard_map/all_to_all | solution.py:399
  (11 other events, 52.9 us)
where the time goes:
time: 304 us; the launch traced here: 301 us
  Pallas kernels  88.8 us (29%)
  starting transfers between devices  69.7 us (23%)
  matrix products  45.8 us (15%)
  waiting for transfers between devices  45.3 us (15%)
  local copies, waits for them, and re-layouts  30.3 us (10%)
  other arithmetic  19.9 us (7%)
    pallas_call x1, Pallas kernels, dp_gather_kernel(): pl.pallas_call(functools.partial(_ring_gather_kernel, n), out_shape=jax.S...  88.8 us
    all_to_all x1, starting transfers between devices, body(): lax.all_to_all(d_rows.reshape(expert_count_axis, -1, model_width), 'exper...  12.5 us
    all_to_all x1, waiting for transfers between devices, body(): lax.all_to_all(router_full.reshape(expert_count_axis, -1, 128), 'expert',...  12 us
    ppermute x4, waiting for transfers between devices, x_ring_scatter(): low = lax.ppermute(blocks[2][:h].astype(jnp.bfloat16), 'dp', _x_shift(n, 1))  9.95 us
    all_to_all x1, starting transfers between devices, body(): lax.all_to_all(scaled_cot, 'expert', 0, 0, tiled=True)  9.3 us
    ppermute x4, waiting for transfers between devices, x_ring_scatter(): lax.ppermute(to_left.astype(jnp.bfloat16), 'dp', _x_shift(n, -1))  8.91 us
    all_to_all x1, starting transfers between devices, body(): lax.all_to_all(picked, 'expert', 0, 0, tiled=True)  8.76 us
    all_to_all x1, waiting for transfers between devices, body(): lax.all_to_all(d_rows.reshape(expert_count_axis, -1, model_width), 'exper...  8.11 us
  transfers between devices with their start and end apart: 25, of which 9 were waited for; matrix products, arithmetic and copies ran while one was open for 24% of the time, Pallas kernels for 30%

commit v1 on v0

--- a/solution.py
+++ b/solution.py
@@ -282,7 +282,7 @@
     )
 
 
-def weight_grads(expert_rows, hidden, expert_cot, d_pre_gate, d_pre_up, router_part, n):
+def weight_grads(expert_rows, hidden, expert_cot, d_pre_gate, d_pre_up, n):
     hidden_activations = hidden.shape[2]
     out_part = jnp.einsum(
         "erc,erd->cd", hidden, expert_cot, preferred_element_type=jnp.float32
@@ -293,16 +293,10 @@
         "erc,erk->ck", expert_rows, both_grads, preferred_element_type=jnp.float32
     ).astype(jnp.bfloat16)
     in_share = dp_scatter_2d(in_part, n)
-    grad_router = jnp.sum(
-        lax.all_to_all(
-            jnp.broadcast_to(router_part[None], (n,) + router_part.shape), "dp", 0, 0, tiled=True
-        ),
-        axis=0,
-    )
     grad_gate = in_share[None, :, :hidden_activations]
     grad_up = in_share[None, :, hidden_activations:]
     down_weight_gradient = out_share[None]
-    return (grad_gate, grad_up, down_weight_gradient, grad_router)
+    return (grad_gate, grad_up, down_weight_gradient)
 
 
 def body(tokens, cotangent, chosen, w_router, w_gate, w_up, w_down):
@@ -389,16 +383,17 @@
         gathered_grads + jnp.dot(d_logit, w_router.T, preferred_element_type=jnp.float32)
     ).astype(jnp.bfloat16)
     router_full = jnp.dot(tokens.T, d_logit, preferred_element_type=jnp.float32)
+    devices = n * expert_count_axis
     router_part = jnp.sum(
-        lax.all_to_all(router_full.reshape(expert_count_axis, -1, 128), "expert", 0, 0, tiled=True),
+        lax.all_to_all(router_full.reshape(devices, -1), ("dp", "expert"), 0, 0, tiled=True),
         axis=0,
     )
-    grad_gate, grad_up, down_weight_gradient, grad_router = weight_grads(
-        expert_rows, hidden, expert_cot, d_pre_gate, d_pre_up, router_part, n
+    grad_gate, grad_up, down_weight_gradient = weight_grads(
+        expert_rows, hidden, expert_cot, d_pre_gate, d_pre_up, n
     )
     grad_router = lax.all_to_all(
-        jnp.broadcast_to(grad_router[None], (expert_count_axis,) + grad_router.shape),
-        "expert",
+        jnp.broadcast_to(router_part[None], (devices,) + router_part.shape),
+        ("dp", "expert"),
         0,
         0,
         tiled=True,

time: 304 us -> 298 us (0.980)
  waiting for transfers between devices: 45.3 us -> 38.7 us
    all_to_all x3 -> x2, waiting for transfers between devices: 18 us -> 11.6 us  [the longest x1 7.54 us: body(): lax.all_to_all(router_full.reshape(devices, -1), ('dp', 'expert'), 0, 0,...]
    all_to_all x3 -> x2, starting transfers between devices: 15 us -> 15.1 us  [the longest x1 7.96 us: body(): lax.all_to_all(router_full.reshape(devices, -1), ('dp', 'expert'), 0, 0,...]
  transfers between devices with their start and end apart: 25 -> 24, of which waited for: 9 -> 9; matrix products, arithmetic and copies ran while one was open for 24% -> 25% of each run, Pallas kernels for 30% -> 30%
where the time goes in v1:
time: 298 us; the launch traced here: 294 us
  Pallas kernels  88.8 us (30%)
  starting transfers between devices  69.7 us (23%)
  matrix products  45.8 us (15%)
  waiting for transfers between devices  38.7 us (13%)
  local copies, waits for them, and re-layouts  29.9 us (10%)
  other arithmetic  20.3 us (7%)
    pallas_call x1, Pallas kernels, dp_gather_kernel(): pl.pallas_call(functools.partial(_ring_gather_kernel, n), out_shape=jax.S...  88.8 us
    all_to_all x1, starting transfers between devices, body(): lax.all_to_all(d_rows.reshape(expert_count_axis, -1, model_width), 'exper...  12.5 us
    ppermute x4, waiting for transfers between devices, x_ring_scatter(): low = lax.ppermute(blocks[2][:h].astype(jnp.bfloat16), 'dp', _x_shift(n, 1))  9.96 us
    all_to_all x1, starting transfers between devices, body(): lax.all_to_all(scaled_cot, 'expert', 0, 0, tiled=True)  9.31 us
    ppermute x4, waiting for transfers between devices, x_ring_scatter(): lax.ppermute(to_left.astype(jnp.bfloat16), 'dp', _x_shift(n, -1))  8.89 us
    all_to_all x1, starting transfers between devices, body(): lax.all_to_all(picked, 'expert', 0, 0, tiled=True)  8.76 us
    all_to_all x1, starting transfers between devices, body(): lax.all_to_all(router_full.reshape(devices, -1), ('dp', 'expert'), 0, 0,...  7.96 us
    all_to_all x1, waiting for transfers between devices, body(): lax.all_to_all(d_rows.reshape(expert_count_axis, -1, model_width), 'exper...  7.94 us
  transfers between devices with their start and end apart: 24, of which 9 were waited for; matrix products, arithmetic and copies ran while one was open for 25% of the time, Pallas kernels for 30%

profile of v1, /device:TPU:5, one launch (start us, length us, event | category | flops | bytes accessed | tf_op | source)
XLA Modules:
  0.0 294.3 jit_solution(4603042305363338745)
XLA Ops:
  1.8 2.9 gather_fusion
  4.7 8.8 %all-to-all-start = ((bf16[16,32,1536]{2,1,0:T(8,128)(2,1)}), bf16[16,32,1536]{2,1,0:T(8,128)(2,1)}, u32[]{:S(2)}, u32[]{:S(2)}) async-start(bf16[16,32,1536]{2,1,0:T(8,128)(2,1)} %bitcast.5), calls=%async_computation | async-start | bytes 3145728 | tf_op jit(solution)/shard_map/all_to_all | solution.py:325
  14.1 4.5 %gather_fusion.2 = f32[512]{0:T(512)S(1)} fusion(f32[16,256]{1,0:T(8,128)S(1)} %bitcast.185, s32[512]{0:T(512)S(1)} %reshape.317), kind=kCustom, calls=%fused_computation.2 | custom fusion | bytes 8192 | tf_op jit(solution)/shard_map/jit(take_along_axis)/gather | solution.py:312
  21.8 88.8 %shard_map.118 = bf16[8,576,1024]{2,1,0:T(8,128)(2,1)} custom-call(bf16[576,1024]{1,0:T(8,128)(2,1)} %pad_maximum_fusion.shard_ref), custom_call_target="tpu_custom_call" | custom-call | tf_op jit(solution)/shard_map/pallas_call | solution.py:261
  110.9 2.1 gather_fusion.1
  114.5 9.3 %all-to-all-start.2 = ((bf16[16,32,1536]{2,1,0:T(8,128)(2,1)}), bf16[16,32,1536]{2,1,0:T(8,128)(2,1)}, u32[]{:S(2)}, u32[]{:S(2)}) async-start(bf16[16,32,1536]{2,1,0:T(8,128)(2,1)} %fusion), calls=%async_computation.2 | async-start | bytes 3145728 | tf_op jit(solution)/shard_map/all_to_all | solution.py:338
  123.8 6.8 %fusion.39 = (bf16[8,192,1024]{2,1,0:T(8,128)(2,1)}, bf16[8,192,1024]{2,1,0:T(8,128)(2,1)}, bf16[8,192,1024]{2,1,0:T(8,128)(2,1)}) fusion(bf16[8,576,1024]{2,1,0:T(8,128)(2,1)} %shard_map.118), kind=kLoop, calls=%fused_computation.117 | loop fusion | bytes 18874368 | tf_op jit(solution)/shard_map/slice | solution.py:323
  130.5 5.9 %reshape.273 = bf16[1024,1536]{1,0:T(8,128)(2,1)} reshape(bf16[8,192,1024]{2,1,0:T(8,128)(2,1)} %get-tuple-element.32) | data formatting | bytes 6291456 | tf_op jit(solution)/shard_map/reshape.12
  136.5 5.6 %fusion.40 = f32[512,1024]{1,0:T(8,128)} fusion(bf16[512,1536]{1,0:T(8,128)(2,1)} %bitcast.6, bf16[1536,1024]{1,0:T(8,128)(2,1)} %bitcast.194), kind=kOutput, calls=%fused_computation.118 | convolution fusion | flops 1610612736 | bytes 6815744 | tf_op jit(solution)/shard_map/erd,edh->erh/dot_general | solution.py:326
  142.1 4.6 %fusion.41 = f32[512,1024]{1,0:T(8,128)} fusion(bf16[512,1536]{1,0:T(8,128)(2,1)} %bitcast.6, bf16[1536,1024]{1,0:T(8,128)(2,1)S(1)} %bitcast.192), kind=kOutput, calls=%fused_computation.119 | convolution fusion | flops 1610612736 | bytes 6815744 | tf_op jit(solution)/shard_map/erd,edh->erh/dot_general | solution.py:329
  146.8 7.2 %multiply_convert_fusion = (bf16[512,1024]{1,0:T(8,128)(2,1)S(1)}, bf16[512,1024]{1,0:T(8,128)(2,1)}, bf16[512,1024]{1,0:T(8,128)(2,1)S(1)}) fusion(f32[512,1024]{1,0:T(8,128)} %fusion.40, f32[512,1024]{1,0:T(8,128)} %fusion.41, bf16[512,1536]{1,0:T(8,128)(2,1)} %bitcast.19, bf16[1024,1536]{1,0:T(8,128)(2,1)} %reshape.273), kind=kOutput, calls=%fused_computation.23 | convolution fusion | flops 1618477056 | bytes 12058624 | tf_op jit(solution)/shard_map/erd,ehd->erh/dot_general | solution.py:340
  154.0 3.0 %convolution_convert_fusion.2 = bf16[512,1536]{1,0:T(8,128)(2,1)} fusion(bf16[512,1024]{1,0:T(8,128)(2,1)S(1)} %get-tuple-element.49, bf16[1024,1536]{1,0:T(8,128)(2,1)S(1)} %copy-done.5), kind=kOutput, calls=%fused_computation.15 | convolution fusion | flops 1611399168 | bytes 5767168 | tf_op jit(solution)/shard_map/erh,ehd->erd/dot_general | solution.py:332
  156.9 5.0 %convolution_convert_fusion.1 = bf16[1024,1536]{1,0:T(8,128)(2,1)} fusion(bf16[512,1024]{1,0:T(8,128)(2,1)S(1)} %get-tuple-element.49, bf16[512,1536]{1,0:T(8,128)(2,1)} %bitcast.19), kind=kOutput, calls=%fused_computation.7 | convolution fusion | flops 1612185600 | bytes 5767168 | tf_op jit(solution)/shard_map/erc,erd->cd/dot_general | solution.py:287
  161.9 7.2 %all-to-all-start.1 = ((bf16[16,32,1536]{2,1,0:T(8,128)(2,1)}), bf16[16,32,1536]{2,1,0:T(8,128)(2,1)}, u32[]{:S(2)}, u32[]{:S(2)}) async-start(bf16[16,32,1536]{2,1,0:T(8,128)(2,1)} %bitcast.201), calls=%async_computation.1 | async-start | bytes 3145728 | tf_op jit(solution)/shard_map/all_to_all | solution.py:335
  169.1 4.2 %fusion.42 = f32[512,1536]{1,0:T(8,128)S(1)} fusion(bf16[512,1024]{1,0:T(8,128)(2,1)} %get-tuple-element.48, bf16[1536,1024]{1,0:T(8,128)(2,1)} %bitcast.195), kind=kOutput, calls=%fused_computation.120 | convolution fusion | flops 1610612736 | bytes 7340032 | tf_op jit(solution)/shard_map/erh,edh->erd/dot_general | solution.py:347
  173.4 2.2 collective-permute-start.9
  177.1 3.0 %fusion.4 = bf16[512,1536]{1,0:T(8,128)(2,1)} fusion(f32[512,1536]{1,0:T(8,128)S(1)} %fusion.42, bf16[512,1024]{1,0:T(8,128)(2,1)S(1)} %get-tuple-element.47, bf16[1536,1024]{1,0:T(8,128)(2,1)S(1)} %bitcast.193), kind=kOutput, calls=%fused_computation.14 | convolution fusion | flops 1612185600 | bytes 8912896 | tf_op jit(solution)/shard_map/erh,edh->erd/dot_general | solution.py:348
  180.1 5.2 %convolution_convert_fusion = bf16[1536,2048]{1,0:T(8,128)(2,1)S(1)} fusion(bf16[512,1536]{1,0:T(8,128)(2,1)} %bitcast.6, bf16[1,512,1024]{2,1,0:T(8,128)(2,1)S(1)} %bitcast.206, bf16[1,512,1024]{2,1,0:T(8,128)(2,1)S(1)} %bitcast.207), kind=kOutput, calls=%fused_computation.3 | convolution fusion | flops 3228565504 | bytes 9961472 | tf_op jit(solution)/shard_map/erc,erk->ck/dot_general | solution.py:292
  189.6 2.7 collective-permute-start.16
  196.5 7.9 %collective-permute-done.4 = bf16[96,2048]{1,0:T(8,128)(2,1)S(1)} collective-permute-done((bf16[96,2048]{1,0:T(8,128)(2,1)S(1)}, bf16[96,2048]{1,0:T(8,128)(2,1)S(1)}, u32[]{:S(2)}, u32[]{:S(2)}) %collective-permute-start.4) | collective-permute-done | bytes 393248 | tf_op jit(solution)/shard_map/ppermute | solution.py:176
  209.7 4.8 %collective-permute-done.16 = bf16[128,1536]{1,0:T(8,128)(2,1)S(1)} collective-permute-done((bf16[128,1536]{1,0:T(8,128)(2,1)S(1)}, bf16[128,1536]{1,0:T(8,128)(2,1)S(1)}, u32[]{:S(2)}, u32[]{:S(2)}) %collective-permute-start.16) | collective-permute-done | bytes 393248 | tf_op jit(solution)/shard_map/ppermute | solution.py:181
  214.5 2.1 collective-permute-start.5
  219.5 12.5 %all-to-all-start.3 = ((bf16[16,32,1536]{2,1,0:T(8,128)(2,1)}), bf16[16,32,1536]{2,1,0:T(8,128)(2,1)}, u32[]{:S(2)}, u32[]{:S(2)}) async-start(bf16[16,32,1536]{2,1,0:T(8,128)(2,1)} %bitcast.200), calls=%async_computation.3 | async-start | bytes 3145728 | tf_op jit(solution)/shard_map/all_to_all | solution.py:350
  233.5 2.3 fusion.25
  235.8 4.1 %collective-permute-done.7 = bf16[192,2048]{1,0:T(8,128)(2,1)} collective-permute-done((bf16[192,2048]{1,0:T(8,128)(2,1)}, bf16[192,2048]{1,0:T(8,128)(2,1)}, u32[]{:S(2)}, u32[]{:S(2)}) %collective-permute-start.7) | collective-permute-done | bytes 786464 | tf_op jit(solution)/shard_map/ppermute | solution.py:181
  239.9 2.9 fusion.11
  247.0 7.9 %all-to-all-done.3 = bf16[16,32,1536]{2,1,0:T(8,128)(2,1)} async-done(((bf16[16,32,1536]{2,1,0:T(8,128)(2,1)}), bf16[16,32,1536]{2,1,0:T(8,128)(2,1)}, u32[]{:S(2)}, u32[]{:S(2)}) %all-to-all-start.3) | async-done | bytes 1572896 | tf_op jit(solution)/shard_map/all_to_all | solution.py:350
  254.9 8.0 %all-to-all-start.4 = ((f32[128,1,192]{2,1,0:T(1,128)}), f32[128,1,192]{2,1,0:T(1,128)S(1)}, u32[]{:S(2)}, u32[]{:S(2)}) async-start(f32[128,1,192]{2,1,0:T(1,128)} %all_to_all.29), calls=%async_computation.4 | async-start | bytes 262144 | tf_op jit(solution)/shard_map/all_to_all | solution.py:388
  266.0 7.5 %all-to-all-done.4 = f32[128,1,192]{2,1,0:T(1,128)S(1)} async-done(((f32[128,1,192]{2,1,0:T(1,128)}), f32[128,1,192]{2,1,0:T(1,128)S(1)}, u32[]{:S(2)}, u32[]{:S(2)}) %all-to-all-start.4) | async-done | bytes 98336 | tf_op jit(solution)/shard_map/all_to_all | solution.py:388
  274.4 7.1 %all-to-all-start.5 = ((f32[128,1,192]{2,1,0:T(1,128)}), f32[128,1,192]{2,1,0:T(1,128)S(1)}, u32[]{:S(2)}, u32[]{:S(2)}) async-start(f32[128,1,192]{2,1,0:T(1,128)} %broadcast_in_dim.32), calls=%async_computation.5 | async-start | bytes 262144 | tf_op jit(solution)/shard_map/all_to_all | solution.py:394
  281.5 4.0 %fusion.5 = bf16[4,64,1536]{2,1,0:T(8,128)(2,1)} fusion(f32[4,128]{1,0:T(4,128)S(1)} %copy-done.16, s32[4,128]{1,0:T(4,128)S(1)} %copy-done.15, bf16[16,32,1536]{2,1,0:T(8,128)(2,1)} %all-to-all-done.1), kind=kOutput, calls=%fused_computation.17 | convolution fusion | flops 605978624 | bytes 2363392 | tf_op jit(solution)/shard_map/wze,wzi->wei/dot_general | solution.py:359
  285.5 4.0 %all-to-all-done.5 = f32[128,1,192]{2,1,0:T(1,128)S(1)} async-done(((f32[128,1,192]{2,1,0:T(1,128)}), f32[128,1,192]{2,1,0:T(1,128)S(1)}, u32[]{:S(2)}, u32[]{:S(2)}) %all-to-all-start.5) | async-done | bytes 98336 | tf_op jit(solution)/shard_map/all_to_all | solution.py:394
  (123 shorter events, 39.3 us)
Async XLA Ops:
  4.7 8.8 %copy-start.10 = (s32[4,16,8]{1,2,0:T(8,128)S(1)}, s32[4,16,8]{1,2,0:T(8,128)}, u32[]{:S(2)}) copy-start(s32[4,16,8]{1,2,0:T(8,128)} %param.9) | copy-start | bytes 6148
  4.7 9.0 %copy-start.11 = (bf16[1536,16]{0,1:T(8,128)(2,1)S(1)}, bf16[1536,16]{0,1:T(8,128)(2,1)}, u32[]{:S(2)}) copy-start(bf16[1536,16]{0,1:T(8,128)(2,1)} %param.10) | copy-start | bytes 147460
  4.7 109.8 %all-to-all-start = ((bf16[16,32,1536]{2,1,0:T(8,128)(2,1)}), bf16[16,32,1536]{2,1,0:T(8,128)(2,1)}, u32[]{:S(2)}, u32[]{:S(2)}) async-start(bf16[16,32,1536]{2,1,0:T(8,128)(2,1)} %bitcast.5), calls=%async_computation | async-start | bytes 3145728 | tf_op jit(solution)/shard_map/all_to_all | solution.py:325
  21.8 89.0 %copy-start.1 = (bf16[256,1536]{1,0:T(8,128)(2,1)S(1)}, bf16[256,1536]{1,0:T(8,128)(2,1)}, u32[]{:S(2)}) copy-start(bf16[256,1536]{1,0:T(8,128)(2,1)} %param.8) | copy-start | bytes 2359300
  114.5 32.3 %all-to-all-start.2 = ((bf16[16,32,1536]{2,1,0:T(8,128)(2,1)}), bf16[16,32,1536]{2,1,0:T(8,128)(2,1)}, u32[]{:S(2)}, u32[]{:S(2)}) async-start(bf16[16,32,1536]{2,1,0:T(8,128)(2,1)} %fusion), calls=%async_computation.2 | async-start | bytes 3145728 | tf_op jit(solution)/shard_map/all_to_all | solution.py:338
  146.8 7.2 %copy-start.5 = (bf16[1024,1536]{1,0:T(8,128)(2,1)S(1)}, bf16[1024,1536]{1,0:T(8,128)(2,1)}, u32[]{:S(2)}) copy-start(bf16[1024,1536]{1,0:T(8,128)(2,1)} %reshape.273) | copy-start | bytes 9437188
  161.9 57.5 %all-to-all-start.1 = ((bf16[16,32,1536]{2,1,0:T(8,128)(2,1)}), bf16[16,32,1536]{2,1,0:T(8,128)(2,1)}, u32[]{:S(2)}, u32[]{:S(2)}) async-start(bf16[16,32,1536]{2,1,0:T(8,128)(2,1)} %bitcast.201), calls=%async_computation.1 | async-start | bytes 3145728 | tf_op jit(solution)/shard_map/all_to_all | solution.py:335
  173.4 13.7 %collective-permute-start.9 = (bf16[64,1536]{1,0:T(8,128)(2,1)S(1)}, bf16[64,1536]{1,0:T(8,128)(2,1)S(1)}, u32[]{:S(2)}, u32[]{:S(2)}) collective-permute-start(bf16[64,1536]{1,0:T(8,128)(2,1)S(1)} %get-tuple-element.54), channel_id=1, source_target_pairs={{0,32},{16,48},{32,64},{48,80},{64,96},{80,112},{96,0},{112,16},{1... | collective-permute-start | bytes 589832 | tf_op jit(solution)/shard_map/ppermute | solution.py:176
  175.6 13.3 %collective-permute-start.13 = (bf16[64,1536]{1,0:T(8,128)(2,1)S(1)}, bf16[64,1536]{1,0:T(8,128)(2,1)S(1)}, u32[]{:S(2)}, u32[]{:S(2)}) collective-permute-start(bf16[64,1536]{1,0:T(8,128)(2,1)S(1)} %get-tuple-element.56), channel_id=1, source_target_pairs={{0,32},{16,48},{32,64},{48,80},{64,96},{80,112},{96,0},{112,16},{1... | collective-permute-start | bytes 589832 | tf_op jit(solution)/shard_map/ppermute | solution.py:176
  176.2 12.7 %collective-permute-start.15 = (bf16[64,1536]{1,0:T(8,128)(2,1)S(1)}, bf16[64,1536]{1,0:T(8,128)(2,1)S(1)}, u32[]{:S(2)}, u32[]{:S(2)}) collective-permute-start(bf16[64,1536]{1,0:T(8,128)(2,1)S(1)} %get-tuple-element.58), channel_id=1, source_target_pairs={{0,96},{16,112},{32,0},{48,16},{64,32},{80,48},{96,64},{112,80},{1... | collective-permute-start | bytes 589832 | tf_op jit(solution)/shard_map/ppermute | solution.py:177
  177.1 12.2 %collective-permute-start.11 = (bf16[64,1536]{1,0:T(8,128)(2,1)S(1)}, bf16[64,1536]{1,0:T(8,128)(2,1)S(1)}, u32[]{:S(2)}, u32[]{:S(2)}) collective-permute-start(bf16[64,1536]{1,0:T(8,128)(2,1)S(1)} %get-tuple-element.60), channel_id=1, source_target_pairs={{0,96},{16,112},{32,0},{48,16},{64,32},{80,48},{96,64},{112,80},{1... | collective-permute-start | bytes 589832 | tf_op jit(solution)/shard_map/ppermute | solution.py:177
  185.4 20.7 %copy-start.2 = (bf16[1536,2048]{1,0:T(8,128)(2,1)}, bf16[1536,2048]{1,0:T(8,128)(2,1)S(1)}, u32[]{:S(2)}) copy-start(bf16[1536,2048]{1,0:T(8,128)(2,1)S(1)} %convolution_convert_fusion) | copy-start | bytes 18874372
  185.7 10.2 %collective-permute-start = (bf16[96,2048]{1,0:T(8,128)(2,1)S(1)}, bf16[96,2048]{1,0:T(8,128)(2,1)S(1)}, u32[]{:S(2)}, u32[]{:S(2)}) collective-permute-start(bf16[96,2048]{1,0:T(8,128)(2,1)S(1)} %get-tuple-element.39), channel_id=1, source_target_pairs={{0,32},{16,48},{32,64},{48,80},{64,96},{80,112},{96,0},{112,16},{1... | collective-permute-start | bytes 1179656 | tf_op jit(solution)/shard_map/ppermute | solution.py:176
  187.2 17.2 %collective-permute-start.4 = (bf16[96,2048]{1,0:T(8,128)(2,1)S(1)}, bf16[96,2048]{1,0:T(8,128)(2,1)S(1)}, u32[]{:S(2)}, u32[]{:S(2)}) collective-permute-start(bf16[96,2048]{1,0:T(8,128)(2,1)S(1)} %get-tuple-element.41), channel_id=1, source_target_pairs={{0,32},{16,48},{32,64},{48,80},{64,96},{80,112},{96,0},{112,16},{1... | collective-permute-start | bytes 1179656 | tf_op jit(solution)/shard_map/ppermute | solution.py:176
  188.9 16.6 %collective-permute-start.6 = (bf16[96,2048]{1,0:T(8,128)(2,1)S(1)}, bf16[96,2048]{1,0:T(8,128)(2,1)S(1)}, u32[]{:S(2)}, u32[]{:S(2)}) collective-permute-start(bf16[96,2048]{1,0:T(8,128)(2,1)S(1)} %get-tuple-element.43), channel_id=1, source_target_pairs={{0,96},{16,112},{32,0},{48,16},{64,32},{80,48},{96,64},{112,80},{1... | collective-permute-start | bytes 1179656 | tf_op jit(solution)/shard_map/ppermute | solution.py:177
  188.9 17.2 %collective-permute-start.2 = (bf16[96,2048]{1,0:T(8,128)(2,1)S(1)}, bf16[96,2048]{1,0:T(8,128)(2,1)S(1)}, u32[]{:S(2)}, u32[]{:S(2)}) collective-permute-start(bf16[96,2048]{1,0:T(8,128)(2,1)S(1)} %get-tuple-element.45), channel_id=1, source_target_pairs={{0,96},{16,112},{32,0},{48,16},{64,32},{80,48},{96,64},{112,80},{1... | collective-permute-start | bytes 1179656 | tf_op jit(solution)/shard_map/ppermute | solution.py:177
  189.6 24.9 %collective-permute-start.16 = (bf16[128,1536]{1,0:T(8,128)(2,1)S(1)}, bf16[128,1536]{1,0:T(8,128)(2,1)S(1)}, u32[]{:S(2)}, u32[]{:S(2)}) collective-permute-start(bf16[128,1536]{1,0:T(8,128)(2,1)S(1)} %pad_maximum_fusion.8), channel_id=1, source_target_pairs={{0,96},{16,112},{32,0},{48,16},{64,32},{80,48},{96,64},{112,80},{1... | collective-permute-start | bytes 1179656 | tf_op jit(solution)/shard_map/ppermute | solution.py:181
  195.9 20.8 %collective-permute-start.14 = (bf16[128,1536]{1,0:T(8,128)(2,1)S(1)}, bf16[128,1536]{1,0:T(8,128)(2,1)S(1)}, u32[]{:S(2)}, u32[]{:S(2)}) collective-permute-start(bf16[128,1536]{1,0:T(8,128)(2,1)S(1)} %pad_maximum_fusion.7), channel_id=1, source_target_pairs={{0,32},{16,48},{32,64},{48,80},{64,96},{80,112},{96,0},{112,16},{1... | collective-permute-start | bytes 1179656 | tf_op jit(solution)/shard_map/ppermute | solution.py:180
  204.3 27.6 %collective-permute-start.12 = (bf16[128,1536]{1,0:T(8,128)(2,1)}, bf16[128,1536]{1,0:T(8,128)(2,1)S(1)}, u32[]{:S(2)}, u32[]{:S(2)}) collective-permute-start(bf16[128,1536]{1,0:T(8,128)(2,1)} %pad_maximum_fusion.6), channel_id=1, source_target_pairs={{0,96},{16,112},{32,0},{48,16},{64,32},{80,48},{96,64},{112,80},{1... | collective-permute-start | bytes 1179656 | tf_op jit(solution)/shard_map/ppermute | solution.py:181
  205.5 26.5 %collective-permute-start.10 = (bf16[128,1536]{1,0:T(8,128)(2,1)}, bf16[128,1536]{1,0:T(8,128)(2,1)}, u32[]{:S(2)}, u32[]{:S(2)}) collective-permute-start(bf16[128,1536]{1,0:T(8,128)(2,1)} %pad_maximum_fusion.5), channel_id=1, source_target_pairs={{0,32},{16,48},{32,64},{48,80},{64,96},{80,112},{96,0},{112,16},{1... | collective-permute-start | bytes 1179656 | tf_op jit(solution)/shard_map/ppermute | solution.py:180
  207.6 32.3 %collective-permute-start.7 = (bf16[192,2048]{1,0:T(8,128)(2,1)}, bf16[192,2048]{1,0:T(8,128)(2,1)}, u32[]{:S(2)}, u32[]{:S(2)}) collective-permute-start(bf16[192,2048]{1,0:T(8,128)(2,1)} %pad_maximum_fusion.4), channel_id=1, source_target_pairs={{0,96},{16,112},{32,0},{48,16},{64,32},{80,48},{96,64},{112,80},{1... | collective-permute-start | bytes 2359304 | tf_op jit(solution)/shard_map/ppermute | solution.py:181
  214.5 25.4 %collective-permute-start.5 = (bf16[192,2048]{1,0:T(8,128)(2,1)}, bf16[192,2048]{1,0:T(8,128)(2,1)}, u32[]{:S(2)}, u32[]{:S(2)}) collective-permute-start(bf16[192,2048]{1,0:T(8,128)(2,1)} %pad_maximum_fusion.3), channel_id=1, source_target_pairs={{0,32},{16,48},{32,64},{48,80},{64,96},{80,112},{96,0},{112,16},{1... | collective-permute-start | bytes 2359304 | tf_op jit(solution)/shard_map/ppermute | solution.py:180
  217.6 15.9 %collective-permute-start.17 = (bf16[128,1536]{1,0:T(8,128)(2,1)}, bf16[128,1536]{1,0:T(8,128)(2,1)}, u32[]{:S(2)}, u32[]{:S(2)}) collective-permute-start(bf16[128,1536]{1,0:T(8,128)(2,1)} %fusion.22), channel_id=1, source_target_pairs={{0,16},{16,0},{32,48},{48,32},{64,80},{80,64},{96,112},{112,96},{1... | collective-permute-start | bytes 1179656 | tf_op jit(solution)/shard_map/ppermute | solution.py:196
  219.5 35.5 %all-to-all-start.3 = ((bf16[16,32,1536]{2,1,0:T(8,128)(2,1)}), bf16[16,32,1536]{2,1,0:T(8,128)(2,1)}, u32[]{:S(2)}, u32[]{:S(2)}) async-start(bf16[16,32,1536]{2,1,0:T(8,128)(2,1)} %bitcast.200), calls=%async_computation.3 | async-start | bytes 3145728 | tf_op jit(solution)/shard_map/all_to_all | solution.py:350
  232.0 59.0 %collective-permute-start.3 = (bf16[192,2048]{1,0:T(8,128)(2,1)}, bf16[192,2048]{1,0:T(8,128)(2,1)S(1)}, u32[]{:S(2)}, u32[]{:S(2)}) collective-permute-start(bf16[192,2048]{1,0:T(8,128)(2,1)} %pad_maximum_fusion.2), channel_id=1, source_target_pairs={{0,96},{16,112},{32,0},{48,16},{64,32},{80,48},{96,64},{112,80},{1... | collective-permute-start | bytes 2359304 | tf_op jit(solution)/shard_map/ppermute | solution.py:181
  232.1 58.9 %collective-permute-start.1 = (bf16[192,2048]{1,0:T(8,128)(2,1)}, bf16[192,2048]{1,0:T(8,128)(2,1)}, u32[]{:S(2)}, u32[]{:S(2)}) collective-permute-start(bf16[192,2048]{1,0:T(8,128)(2,1)} %pad_maximum_fusion.1), channel_id=1, source_target_pairs={{0,32},{16,48},{32,64},{48,80},{64,96},{80,112},{96,0},{112,16},{1... | collective-permute-start | bytes 2359304 | tf_op jit(solution)/shard_map/ppermute | solution.py:180
  242.8 48.2 %collective-permute-start.8 = (bf16[192,2048]{1,0:T(8,128)(2,1)}, bf16[192,2048]{1,0:T(8,128)(2,1)}, u32[]{:S(2)}, u32[]{:S(2)}) collective-permute-start(bf16[192,2048]{1,0:T(8,128)(2,1)} %fusion.11), channel_id=1, source_target_pairs={{0,16},{16,0},{32,48},{48,32},{64,80},{80,64},{96,112},{112,96},{1... | collective-permute-start | bytes 2359304 | tf_op jit(solution)/shard_map/ppermute | solution.py:196
  244.7 18.2 %copy-start.15 = (s32[4,128]{1,0:T(4,128)S(1)}, s32[4,128]{1,0:T(4,128)}, u32[]{:S(2)}) copy-start(s32[4,128]{1,0:T(4,128)} %eq.41) | copy-start | bytes 6148
  245.9 18.8 %copy-start.12 = (bf16[1536,16]{0,1:T(8,128)(2,1)S(1)}, bf16[1536,16]{0,1:T(8,128)(2,1)}, u32[]{:S(2)}) copy-start(bf16[1536,16]{0,1:T(8,128)(2,1)} %param.10) | copy-start | bytes 147460
  254.9 18.6 %all-to-all-start.4 = ((f32[128,1,192]{2,1,0:T(1,128)}), f32[128,1,192]{2,1,0:T(1,128)S(1)}, u32[]{:S(2)}, u32[]{:S(2)}) async-start(f32[128,1,192]{2,1,0:T(1,128)} %all_to_all.29), calls=%async_computation.4 | async-start | bytes 262144 | tf_op jit(solution)/shard_map/all_to_all | solution.py:388
  264.7 16.9 %copy-start.16 = (f32[4,128]{1,0:T(4,128)S(1)}, f32[4,128]{1,0:T(4,128)}, u32[]{:S(2)}) copy-start(f32[4,128]{1,0:T(4,128)} %mul.88) | copy-start | bytes 6148
  274.4 15.1 %all-to-all-start.5 = ((f32[128,1,192]{2,1,0:T(1,128)}), f32[128,1,192]{2,1,0:T(1,128)S(1)}, u32[]{:S(2)}, u32[]{:S(2)}) async-start(f32[128,1,192]{2,1,0:T(1,128)} %broadcast_in_dim.32), calls=%async_computation.5 | async-start | bytes 262144 | tf_op jit(solution)/shard_map/all_to_all | solution.py:394
  (10 other events, 45.8 us)

commit v2 on v1

--- a/solution.py
+++ b/solution.py
@@ -347,9 +347,6 @@
         jnp.einsum("erh,edh->erd", d_pre_gate, back_gate, preferred_element_type=jnp.float32)
         + jnp.einsum("erh,edh->erd", d_pre_up, back_up, preferred_element_type=jnp.float32)
     ).astype(jnp.bfloat16)
-    row_grads = lax.all_to_all(
-        d_rows.reshape(expert_count_axis, -1, model_width), "expert", 0, 0, tiled=True
-    )
     position_hits = chosen[:, :, :, None] == jnp.arange(block_rows, dtype=jnp.int32)
     indicator_matrix = position_hits.reshape(num_blocks, expert_count * pick_count, block_rows)
     gate_weighted_rows = to_blocks(slot_gate_values, num_blocks, pick_count)[
@@ -373,6 +370,16 @@
         precision=lax.Precision.HIGHEST,
     ).reshape(tok_rows, expert_count)
     d_logit = (dgate * gate_values * (1.0 - gate_values)).astype(jnp.bfloat16)
+    router_full = jnp.dot(tokens.T, d_logit, preferred_element_type=jnp.float32)
+    devices = n * expert_count_axis
+    router_part = jnp.sum(
+        lax.all_to_all(router_full.reshape(devices, -1), ("dp", "expert"), 0, 0, tiled=True),
+        axis=0,
+    )
+    router_part, d_rows = lax.optimization_barrier((router_part, d_rows))
+    row_grads = lax.all_to_all(
+        d_rows.reshape(expert_count_axis, -1, model_width), "expert", 0, 0, tiled=True
+    )
     gathered_grads = jnp.einsum(
         "wze,wzi->wei",
         indicator_matrix.astype(jnp.bfloat16),
@@ -382,12 +389,6 @@
     grad_tokens = (
         gathered_grads + jnp.dot(d_logit, w_router.T, preferred_element_type=jnp.float32)
     ).astype(jnp.bfloat16)
-    router_full = jnp.dot(tokens.T, d_logit, preferred_element_type=jnp.float32)
-    devices = n * expert_count_axis
-    router_part = jnp.sum(
-        lax.all_to_all(router_full.reshape(devices, -1), ("dp", "expert"), 0, 0, tiled=True),
-        axis=0,
-    )
     grad_gate, grad_up, down_weight_gradient = weight_grads(
         expert_rows, hidden, expert_cot, d_pre_gate, d_pre_up, n
     )

time: 298 us -> 312 us (1.047)
  waiting for transfers between devices: 38.7 us -> 50 us
    all_to_all x1, waiting for transfers between devices: 7.94 us -> 18 us  [body(): lax.all_to_all(d_rows.reshape(expert_count_axis, -1, model_width), 'exper...]
    ppermute x4, waiting for transfers between devices: 8.89 us -> 0.01 us  [x_ring_scatter(): lax.ppermute(to_left.astype(jnp.bfloat16), 'dp', _x_shift(n, -1))]
    all_to_all x1, starting transfers between devices: 7.96 us -> 16.4 us  [body(): lax.all_to_all(router_full.reshape(devices, -1), ('dp', 'expert'), 0, 0,...]
    all_to_all x1, starting transfers between devices: 12.5 us -> 5.42 us  [body(): lax.all_to_all(d_rows.reshape(expert_count_axis, -1, model_width), 'exper...]
    ppermute x2, waiting for transfers between devices: 0.01 us -> 6.52 us  [dp_scatter_2d(): sent = lax.ppermute(partner_sum.astype(jnp.bfloat16), 'dp', _y_pair(n))]
    all_to_all x1, waiting for transfers between devices: 7.54 us -> 12.3 us  [body(): lax.all_to_all(router_full.reshape(devices, -1), ('dp', 'expert'), 0, 0,...]
  transfers between devices with their start and end apart: 24 -> 24, of which waited for: 9 -> 8; matrix products, arithmetic and copies ran while one was open for 25% -> 25% of each run, Pallas kernels for 30% -> 29%
where the time goes in v2:
time: 312 us; the launch traced here: 309 us
  Pallas kernels  88.8 us (28%)
  starting transfers between devices  71.6 us (23%)
  waiting for transfers between devices  50 us (16%)
  matrix products  45 us (14%)
  local copies, waits for them, and re-layouts  30.6 us (10%)
  other arithmetic  22.3 us (7%)
    pallas_call x1, Pallas kernels, dp_gather_kernel(): pl.pallas_call(functools.partial(_ring_gather_kernel, n), out_shape=jax.S...  88.8 us
    all_to_all x1, waiting for transfers between devices, body(): lax.all_to_all(d_rows.reshape(expert_count_axis, -1, model_width), 'exper...  18 us
    all_to_all x1, starting transfers between devices, body(): lax.all_to_all(router_full.reshape(devices, -1), ('dp', 'expert'), 0, 0,...  16.4 us
    all_to_all x1, waiting for transfers between devices, body(): lax.all_to_all(router_full.reshape(devices, -1), ('dp', 'expert'), 0, 0,...  12.3 us
    all_to_all x1, starting transfers between devices, body(): lax.all_to_all(scaled_cot, 'expert', 0, 0, tiled=True)  9.3 us
    ppermute x4, waiting for transfers between devices, x_ring_scatter(): low = lax.ppermute(blocks[2][:h].astype(jnp.bfloat16), 'dp', _x_shift(n, 1))  9.24 us
    all_to_all x1, starting transfers between devices, body(): lax.all_to_all(picked, 'expert', 0, 0, tiled=True)  8.76 us
    dot_general x1, matrix products, body(): jnp.einsum('erd,ehd->erh', expert_cot, back_down, preferred_element_type=...  7.2 us
  transfers between devices with their start and end apart: 24, of which 8 were waited for; matrix products, arithmetic and copies ran while one was open for 25% of the time, Pallas kernels for 29%

profile of v2, /device:TPU:5, one launch (start us, length us, event | category | flops | bytes accessed | tf_op | source)
XLA Modules:
  0.0 309.3 jit_solution(443150159094917000)
XLA Ops:
  1.8 3.0 gather_fusion
  4.7 8.8 %all-to-all-start = ((bf16[16,32,1536]{2,1,0:T(8,128)(2,1)}), bf16[16,32,1536]{2,1,0:T(8,128)(2,1)}, u32[]{:S(2)}, u32[]{:S(2)}) async-start(bf16[16,32,1536]{2,1,0:T(8,128)(2,1)} %bitcast.5), calls=%async_computation | async-start | bytes 3145728 | tf_op jit(solution)/shard_map/all_to_all | solution.py:325
  14.1 4.5 %gather_fusion.2 = f32[512]{0:T(512)S(1)} fusion(f32[16,256]{1,0:T(8,128)S(1)} %bitcast.187, s32[512]{0:T(512)S(1)} %reshape.316), kind=kCustom, calls=%fused_computation.2 | custom fusion | bytes 8192 | tf_op jit(solution)/shard_map/jit(take_along_axis)/gather | solution.py:312
  21.8 88.8 %shard_map.118 = bf16[8,576,1024]{2,1,0:T(8,128)(2,1)} custom-call(bf16[576,1024]{1,0:T(8,128)(2,1)} %pad_maximum_fusion.shard_ref), custom_call_target="tpu_custom_call" | custom-call | tf_op jit(solution)/shard_map/pallas_call | solution.py:261
  110.9 2.1 gather_fusion.1
  114.5 9.3 %all-to-all-start.3 = ((bf16[16,32,1536]{2,1,0:T(8,128)(2,1)}), bf16[16,32,1536]{2,1,0:T(8,128)(2,1)}, u32[]{:S(2)}, u32[]{:S(2)}) async-start(bf16[16,32,1536]{2,1,0:T(8,128)(2,1)} %fusion.1), calls=%async_computation.3 | async-start | bytes 3145728 | tf_op jit(solution)/shard_map/all_to_all | solution.py:338
  123.8 6.7 %fusion.40 = (bf16[8,192,1024]{2,1,0:T(8,128)(2,1)}, bf16[8,192,1024]{2,1,0:T(8,128)(2,1)}, bf16[8,192,1024]{2,1,0:T(8,128)(2,1)}) fusion(bf16[8,576,1024]{2,1,0:T(8,128)(2,1)} %shard_map.118), kind=kLoop, calls=%fused_computation.118 | loop fusion | bytes 18874368 | tf_op jit(solution)/shard_map/slice | solution.py:323
  130.5 5.9 %reshape.272 = bf16[1024,1536]{1,0:T(8,128)(2,1)} reshape(bf16[8,192,1024]{2,1,0:T(8,128)(2,1)} %get-tuple-element.36) | data formatting | bytes 6291456 | tf_op jit(solution)/shard_map/reshape.12
  136.4 5.6 %fusion.41 = f32[512,1024]{1,0:T(8,128)} fusion(bf16[512,1536]{1,0:T(8,128)(2,1)} %bitcast.6, bf16[1536,1024]{1,0:T(8,128)(2,1)} %bitcast.196), kind=kOutput, calls=%fused_computation.119 | convolution fusion | flops 1610612736 | bytes 6815744 | tf_op jit(solution)/shard_map/erd,edh->erh/dot_general | solution.py:326
  142.1 4.6 %fusion.42 = f32[512,1024]{1,0:T(8,128)} fusion(bf16[512,1536]{1,0:T(8,128)(2,1)} %bitcast.6, bf16[1536,1024]{1,0:T(8,128)(2,1)S(1)} %bitcast.194), kind=kOutput, calls=%fused_computation.120 | convolution fusion | flops 1610612736 | bytes 6815744 | tf_op jit(solution)/shard_map/erd,edh->erh/dot_general | solution.py:329
  146.8 7.2 %multiply_convert_fusion = (bf16[512,1024]{1,0:T(8,128)(2,1)S(1)}, bf16[512,1024]{1,0:T(8,128)(2,1)}, bf16[512,1024]{1,0:T(8,128)(2,1)S(1)}) fusion(f32[512,1024]{1,0:T(8,128)} %fusion.41, f32[512,1024]{1,0:T(8,128)} %fusion.42, bf16[512,1536]{1,0:T(8,128)(2,1)} %bitcast.25, bf16[1024,1536]{1,0:T(8,128)(2,1)} %reshape.272), kind=kOutput, calls=%fused_computation.24 | convolution fusion | flops 1618477056 | bytes 12058624 | tf_op jit(solution)/shard_map/erd,ehd->erh/dot_general | solution.py:340
  154.0 3.0 convolution_convert_fusion.2
  157.0 5.0 %convolution_convert_fusion.1 = bf16[1024,1536]{1,0:T(8,128)(2,1)} fusion(bf16[512,1024]{1,0:T(8,128)(2,1)S(1)} %get-tuple-element.53, bf16[512,1536]{1,0:T(8,128)(2,1)} %bitcast.25), kind=kOutput, calls=%fused_computation.7 | convolution fusion | flops 1612185600 | bytes 5767168 | tf_op jit(solution)/shard_map/erc,erd->cd/dot_general | solution.py:287
  161.9 7.1 %all-to-all-start.1 = ((bf16[16,32,1536]{2,1,0:T(8,128)(2,1)}), bf16[16,32,1536]{2,1,0:T(8,128)(2,1)}, u32[]{:S(2)}, u32[]{:S(2)}) async-start(bf16[16,32,1536]{2,1,0:T(8,128)(2,1)} %bitcast.203), calls=%async_computation.1 | async-start | bytes 3145728 | tf_op jit(solution)/shard_map/all_to_all | solution.py:335
  169.0 4.2 %fusion.43 = f32[512,1536]{1,0:T(8,128)S(1)} fusion(bf16[512,1024]{1,0:T(8,128)(2,1)} %get-tuple-element.52, bf16[1536,1024]{1,0:T(8,128)(2,1)} %bitcast.197), kind=kOutput, calls=%fused_computation.121 | convolution fusion | flops 1610612736 | bytes 7340032 | tf_op jit(solution)/shard_map/erh,edh->erd/dot_general | solution.py:347
  173.4 2.2 collective-permute-start.9
  177.1 3.0 fusion.5
  180.0 5.2 %convolution_convert_fusion = bf16[1536,2048]{1,0:T(8,128)(2,1)S(1)} fusion(bf16[512,1536]{1,0:T(8,128)(2,1)} %bitcast.6, bf16[1,512,1024]{2,1,0:T(8,128)(2,1)S(1)} %bitcast.208, bf16[1,512,1024]{2,1,0:T(8,128)(2,1)S(1)} %bitcast.209), kind=kOutput, calls=%fused_computation.3 | convolution fusion | flops 3228565504 | bytes 9961472 | tf_op jit(solution)/shard_map/erc,erk->ck/dot_general | solution.py:292
  190.2 2.6 collective-permute-start.16
  196.4 7.8 %collective-permute-done.4 = bf16[96,2048]{1,0:T(8,128)(2,1)S(1)} collective-permute-done((bf16[96,2048]{1,0:T(8,128)(2,1)S(1)}, bf16[96,2048]{1,0:T(8,128)(2,1)S(1)}, u32[]{:S(2)}, u32[]{:S(2)}) %collective-permute-start.4) | collective-permute-done | bytes 393248 | tf_op jit(solution)/shard_map/ppermute | solution.py:176
  211.7 2.5 fusion
  217.9 16.4 %all-to-all-start.2 = ((f32[128,1,192]{2,1,0:T(1,128)}), f32[128,1,192]{2,1,0:T(1,128)S(1)}, u32[]{:S(2)}, u32[]{:S(2)}) async-start(f32[128,1,192]{2,1,0:T(1,128)} %all_to_all.29), calls=%async_computation.2 | async-start | bytes 262144 | tf_op jit(solution)/shard_map/all_to_all | solution.py:376
  238.0 12.3 %all-to-all-done.2 = f32[128,1,192]{2,1,0:T(1,128)S(1)} async-done(((f32[128,1,192]{2,1,0:T(1,128)}), f32[128,1,192]{2,1,0:T(1,128)S(1)}, u32[]{:S(2)}, u32[]{:S(2)}) %all-to-all-start.2) | async-done | bytes 98336 | tf_op jit(solution)/shard_map/all_to_all | solution.py:376
  251.2 6.7 %all-to-all-start.5 = ((f32[128,1,192]{2,1,0:T(1,128)}), f32[128,1,192]{2,1,0:T(1,128)S(1)}, u32[]{:S(2)}, u32[]{:S(2)}) async-start(f32[128,1,192]{2,1,0:T(1,128)} %broadcast_in_dim.32), calls=%async_computation.5 | async-start | bytes 262144 | tf_op jit(solution)/shard_map/all_to_all | solution.py:395
  260.1 2.9 fusion.12
  263.2 3.1 %all-to-all-done.5 = f32[128,1,192]{2,1,0:T(1,128)S(1)} async-done(((f32[128,1,192]{2,1,0:T(1,128)}), f32[128,1,192]{2,1,0:T(1,128)S(1)}, u32[]{:S(2)}, u32[]{:S(2)}) %all-to-all-start.5) | async-done | bytes 98336 | tf_op jit(solution)/shard_map/all_to_all | solution.py:395
  266.4 5.4 %all-to-all-start.4 = ((bf16[16,32,1536]{2,1,0:T(8,128)(2,1)}), bf16[16,32,1536]{2,1,0:T(8,128)(2,1)S(1)}, u32[]{:S(2)}, u32[]{:S(2)}) async-start(bf16[16,32,1536]{2,1,0:T(8,128)(2,1)} %bitcast.202), calls=%async_computation.4 | async-start | bytes 3145728 | tf_op jit(solution)/shard_map/all_to_all | solution.py:380
  271.8 2.3 fusion.26
  274.1 4.0 %fusion.6 = bf16[4,64,1536]{2,1,0:T(8,128)(2,1)} fusion(f32[4,128]{1,0:T(4,128)S(1)} %copy-done.17, s32[4,128]{1,0:T(4,128)S(1)} %copy-done.16, bf16[16,32,1536]{2,1,0:T(8,128)(2,1)} %all-to-all-done.1), kind=kOutput, calls=%fused_computation.18 | convolution fusion | flops 605978624 | bytes 2363392 | tf_op jit(solution)/shard_map/wze,wzi->wei/dot_general | solution.py:356
  279.6 6.5 %collective-permute-done.8 = bf16[192,2048]{1,0:T(8,128)(2,1)} collective-permute-done((bf16[192,2048]{1,0:T(8,128)(2,1)}, bf16[192,2048]{1,0:T(8,128)(2,1)}, u32[]{:S(2)}, u32[]{:S(2)}) %collective-permute-start.8) | collective-permute-done | bytes 786464 | tf_op jit(solution)/shard_map/ppermute | solution.py:196
  286.1 2.4 fusion.14
  289.7 18.0 %all-to-all-done.4 = bf16[16,32,1536]{2,1,0:T(8,128)(2,1)S(1)} async-done(((bf16[16,32,1536]{2,1,0:T(8,128)(2,1)}), bf16[16,32,1536]{2,1,0:T(8,128)(2,1)S(1)}, u32[]{:S(2)}, u32[]{:S(2)}) %all-to-all-start.4) | async-done | bytes 1572896 | tf_op jit(solution)/shard_map/all_to_all | solution.py:380
  (125 shorter events, 39.2 us)
Async XLA Ops:
  4.7 8.8 %copy-start.10 = (s32[4,16,8]{1,2,0:T(8,128)S(1)}, s32[4,16,8]{1,2,0:T(8,128)}, u32[]{:S(2)}) copy-start(s32[4,16,8]{1,2,0:T(8,128)} %param.9) | copy-start | bytes 6148
  4.7 9.0 %copy-start.11 = (bf16[1536,16]{0,1:T(8,128)(2,1)S(1)}, bf16[1536,16]{0,1:T(8,128)(2,1)}, u32[]{:S(2)}) copy-start(bf16[1536,16]{0,1:T(8,128)(2,1)} %param.10) | copy-start | bytes 147460
  4.7 109.8 %all-to-all-start = ((bf16[16,32,1536]{2,1,0:T(8,128)(2,1)}), bf16[16,32,1536]{2,1,0:T(8,128)(2,1)}, u32[]{:S(2)}, u32[]{:S(2)}) async-start(bf16[16,32,1536]{2,1,0:T(8,128)(2,1)} %bitcast.5), calls=%async_computation | async-start | bytes 3145728 | tf_op jit(solution)/shard_map/all_to_all | solution.py:325
  21.8 89.1 %copy-start.1 = (bf16[256,1536]{1,0:T(8,128)(2,1)S(1)}, bf16[256,1536]{1,0:T(8,128)(2,1)}, u32[]{:S(2)}) copy-start(bf16[256,1536]{1,0:T(8,128)(2,1)} %param.8) | copy-start | bytes 2359300
  114.5 32.3 %all-to-all-start.3 = ((bf16[16,32,1536]{2,1,0:T(8,128)(2,1)}), bf16[16,32,1536]{2,1,0:T(8,128)(2,1)}, u32[]{:S(2)}, u32[]{:S(2)}) async-start(bf16[16,32,1536]{2,1,0:T(8,128)(2,1)} %fusion.1), calls=%async_computation.3 | async-start | bytes 3145728 | tf_op jit(solution)/shard_map/all_to_all | solution.py:338
  161.9 49.8 %all-to-all-start.1 = ((bf16[16,32,1536]{2,1,0:T(8,128)(2,1)}), bf16[16,32,1536]{2,1,0:T(8,128)(2,1)}, u32[]{:S(2)}, u32[]{:S(2)}) async-start(bf16[16,32,1536]{2,1,0:T(8,128)(2,1)} %bitcast.203), calls=%async_computation.1 | async-start | bytes 3145728 | tf_op jit(solution)/shard_map/all_to_all | solution.py:335
  173.4 13.7 %collective-permute-start.9 = (bf16[64,1536]{1,0:T(8,128)(2,1)S(1)}, bf16[64,1536]{1,0:T(8,128)(2,1)S(1)}, u32[]{:S(2)}, u32[]{:S(2)}) collective-permute-start(bf16[64,1536]{1,0:T(8,128)(2,1)S(1)} %get-tuple-element.58), channel_id=1, source_target_pairs={{0,32},{16,48},{32,64},{48,80},{64,96},{80,112},{96,0},{112,16},{1... | collective-permute-start | bytes 589832 | tf_op jit(solution)/shard_map/ppermute | solution.py:176
  175.6 13.3 %collective-permute-start.13 = (bf16[64,1536]{1,0:T(8,128)(2,1)S(1)}, bf16[64,1536]{1,0:T(8,128)(2,1)S(1)}, u32[]{:S(2)}, u32[]{:S(2)}) collective-permute-start(bf16[64,1536]{1,0:T(8,128)(2,1)S(1)} %get-tuple-element.60), channel_id=1, source_target_pairs={{0,32},{16,48},{32,64},{48,80},{64,96},{80,112},{96,0},{112,16},{1... | collective-permute-start | bytes 589832 | tf_op jit(solution)/shard_map/ppermute | solution.py:176
  176.1 12.7 %collective-permute-start.15 = (bf16[64,1536]{1,0:T(8,128)(2,1)S(1)}, bf16[64,1536]{1,0:T(8,128)(2,1)S(1)}, u32[]{:S(2)}, u32[]{:S(2)}) collective-permute-start(bf16[64,1536]{1,0:T(8,128)(2,1)S(1)} %get-tuple-element.62), channel_id=1, source_target_pairs={{0,96},{16,112},{32,0},{48,16},{64,32},{80,48},{96,64},{112,80},{1... | collective-permute-start | bytes 589832 | tf_op jit(solution)/shard_map/ppermute | solution.py:177
  177.0 12.2 %collective-permute-start.11 = (bf16[64,1536]{1,0:T(8,128)(2,1)S(1)}, bf16[64,1536]{1,0:T(8,128)(2,1)S(1)}, u32[]{:S(2)}, u32[]{:S(2)}) collective-permute-start(bf16[64,1536]{1,0:T(8,128)(2,1)S(1)} %get-tuple-element.64), channel_id=1, source_target_pairs={{0,96},{16,112},{32,0},{48,16},{64,32},{80,48},{96,64},{112,80},{1... | collective-permute-start | bytes 589832 | tf_op jit(solution)/shard_map/ppermute | solution.py:177
  185.3 20.7 %copy-start.2 = (bf16[1536,2048]{1,0:T(8,128)(2,1)}, bf16[1536,2048]{1,0:T(8,128)(2,1)S(1)}, u32[]{:S(2)}) copy-start(bf16[1536,2048]{1,0:T(8,128)(2,1)S(1)} %convolution_convert_fusion) | copy-start | bytes 18874372
  185.5 10.3 %collective-permute-start = (bf16[96,2048]{1,0:T(8,128)(2,1)S(1)}, bf16[96,2048]{1,0:T(8,128)(2,1)S(1)}, u32[]{:S(2)}, u32[]{:S(2)}) collective-permute-start(bf16[96,2048]{1,0:T(8,128)(2,1)S(1)} %get-tuple-element.43), channel_id=1, source_target_pairs={{0,32},{16,48},{32,64},{48,80},{64,96},{80,112},{96,0},{112,16},{1... | collective-permute-start | bytes 1179656 | tf_op jit(solution)/shard_map/ppermute | solution.py:176
  187.1 17.2 %collective-permute-start.4 = (bf16[96,2048]{1,0:T(8,128)(2,1)S(1)}, bf16[96,2048]{1,0:T(8,128)(2,1)S(1)}, u32[]{:S(2)}, u32[]{:S(2)}) collective-permute-start(bf16[96,2048]{1,0:T(8,128)(2,1)S(1)} %get-tuple-element.45), channel_id=1, source_target_pairs={{0,32},{16,48},{32,64},{48,80},{64,96},{80,112},{96,0},{112,16},{1... | collective-permute-start | bytes 1179656 | tf_op jit(solution)/shard_map/ppermute | solution.py:176
  188.8 16.6 %collective-permute-start.6 = (bf16[96,2048]{1,0:T(8,128)(2,1)S(1)}, bf16[96,2048]{1,0:T(8,128)(2,1)S(1)}, u32[]{:S(2)}, u32[]{:S(2)}) collective-permute-start(bf16[96,2048]{1,0:T(8,128)(2,1)S(1)} %get-tuple-element.47), channel_id=1, source_target_pairs={{0,96},{16,112},{32,0},{48,16},{64,32},{80,48},{96,64},{112,80},{1... | collective-permute-start | bytes 1179656 | tf_op jit(solution)/shard_map/ppermute | solution.py:177
  188.8 17.2 %collective-permute-start.2 = (bf16[96,2048]{1,0:T(8,128)(2,1)S(1)}, bf16[96,2048]{1,0:T(8,128)(2,1)S(1)}, u32[]{:S(2)}, u32[]{:S(2)}) collective-permute-start(bf16[96,2048]{1,0:T(8,128)(2,1)S(1)} %get-tuple-element.49), channel_id=1, source_target_pairs={{0,96},{16,112},{32,0},{48,16},{64,32},{80,48},{96,64},{112,80},{1... | collective-permute-start | bytes 1179656 | tf_op jit(solution)/shard_map/ppermute | solution.py:177
  190.2 44.1 %collective-permute-start.16 = (bf16[128,1536]{1,0:T(8,128)(2,1)}, bf16[128,1536]{1,0:T(8,128)(2,1)}, u32[]{:S(2)}, u32[]{:S(2)}) collective-permute-start(bf16[128,1536]{1,0:T(8,128)(2,1)} %pad_maximum_fusion.8), channel_id=1, source_target_pairs={{0,96},{16,112},{32,0},{48,16},{64,32},{80,48},{96,64},{112,80},{1... | collective-permute-start | bytes 1179656 | tf_op jit(solution)/shard_map/ppermute | solution.py:181
  195.8 39.5 %collective-permute-start.14 = (bf16[128,1536]{1,0:T(8,128)(2,1)S(1)}, bf16[128,1536]{1,0:T(8,128)(2,1)}, u32[]{:S(2)}, u32[]{:S(2)}) collective-permute-start(bf16[128,1536]{1,0:T(8,128)(2,1)S(1)} %pad_maximum_fusion.7), channel_id=1, source_target_pairs={{0,32},{16,48},{32,64},{48,80},{64,96},{80,112},{96,0},{112,16},{1... | collective-permute-start | bytes 1179656 | tf_op jit(solution)/shard_map/ppermute | solution.py:180
  204.2 58.7 %collective-permute-start.12 = (bf16[128,1536]{1,0:T(8,128)(2,1)}, bf16[128,1536]{1,0:T(8,128)(2,1)}, u32[]{:S(2)}, u32[]{:S(2)}) collective-permute-start(bf16[128,1536]{1,0:T(8,128)(2,1)} %pad_maximum_fusion.6), channel_id=1, source_target_pairs={{0,96},{16,112},{32,0},{48,16},{64,32},{80,48},{96,64},{112,80},{1... | collective-permute-start | bytes 1179656 | tf_op jit(solution)/shard_map/ppermute | solution.py:181
  207.5 50.4 %collective-permute-start.7 = (bf16[192,2048]{1,0:T(8,128)(2,1)}, bf16[192,2048]{1,0:T(8,128)(2,1)}, u32[]{:S(2)}, u32[]{:S(2)}) collective-permute-start(bf16[192,2048]{1,0:T(8,128)(2,1)} %pad_maximum_fusion.4), channel_id=1, source_target_pairs={{0,96},{16,112},{32,0},{48,16},{64,32},{80,48},{96,64},{112,80},{1... | collective-permute-start | bytes 2359304 | tf_op jit(solution)/shard_map/ppermute | solution.py:181
  208.8 50.1 %collective-permute-start.5 = (bf16[192,2048]{1,0:T(8,128)(2,1)S(1)}, bf16[192,2048]{1,0:T(8,128)(2,1)}, u32[]{:S(2)}, u32[]{:S(2)}) collective-permute-start(bf16[192,2048]{1,0:T(8,128)(2,1)S(1)} %pad_maximum_fusion.3), channel_id=1, source_target_pairs={{0,32},{16,48},{32,64},{48,80},{64,96},{80,112},{96,0},{112,16},{1... | collective-permute-start | bytes 2359304 | tf_op jit(solution)/shard_map/ppermute | solution.py:180
  216.3 21.7 %copy-start.14 = (bf16[256,16]{0,1:T(8,128)(2,1)}, bf16[256,16]{0,1:T(8,128)(2,1)S(1)}, u32[]{:S(2)}) copy-start(bf16[256,16]{0,1:T(8,128)(2,1)S(1)} %multiply_convert_fusion.3) | copy-start | bytes 24580
  217.9 32.4 %all-to-all-start.2 = ((f32[128,1,192]{2,1,0:T(1,128)}), f32[128,1,192]{2,1,0:T(1,128)S(1)}, u32[]{:S(2)}, u32[]{:S(2)}) async-start(f32[128,1,192]{2,1,0:T(1,128)} %all_to_all.29), calls=%async_computation.2 | async-start | bytes 262144 | tf_op jit(solution)/shard_map/all_to_all | solution.py:376
  234.3 37.5 %collective-permute-start.10 = (bf16[128,1536]{1,0:T(8,128)(2,1)}, bf16[128,1536]{1,0:T(8,128)(2,1)}, u32[]{:S(2)}, u32[]{:S(2)}) collective-permute-start(bf16[128,1536]{1,0:T(8,128)(2,1)} %pad_maximum_fusion.5), channel_id=1, source_target_pairs={{0,32},{16,48},{32,64},{48,80},{64,96},{80,112},{96,0},{112,16},{1... | collective-permute-start | bytes 1179656 | tf_op jit(solution)/shard_map/ppermute | solution.py:180
  235.3 44.2 %collective-permute-start.3 = (bf16[192,2048]{1,0:T(8,128)(2,1)}, bf16[192,2048]{1,0:T(8,128)(2,1)}, u32[]{:S(2)}, u32[]{:S(2)}) collective-permute-start(bf16[192,2048]{1,0:T(8,128)(2,1)} %pad_maximum_fusion.2), channel_id=1, source_target_pairs={{0,96},{16,112},{32,0},{48,16},{64,32},{80,48},{96,64},{112,80},{1... | collective-permute-start | bytes 2359304 | tf_op jit(solution)/shard_map/ppermute | solution.py:181
  251.2 15.2 %all-to-all-start.5 = ((f32[128,1,192]{2,1,0:T(1,128)}), f32[128,1,192]{2,1,0:T(1,128)S(1)}, u32[]{:S(2)}, u32[]{:S(2)}) async-start(f32[128,1,192]{2,1,0:T(1,128)} %broadcast_in_dim.32), calls=%async_computation.5 | async-start | bytes 262144 | tf_op jit(solution)/shard_map/all_to_all | solution.py:395
  257.9 21.6 %collective-permute-start.1 = (bf16[192,2048]{1,0:T(8,128)(2,1)}, bf16[192,2048]{1,0:T(8,128)(2,1)}, u32[]{:S(2)}, u32[]{:S(2)}) collective-permute-start(bf16[192,2048]{1,0:T(8,128)(2,1)} %pad_maximum_fusion.1), channel_id=1, source_target_pairs={{0,32},{16,48},{32,64},{48,80},{64,96},{80,112},{96,0},{112,16},{1... | collective-permute-start | bytes 2359304 | tf_op jit(solution)/shard_map/ppermute | solution.py:180
  258.9 12.9 %collective-permute-start.17 = (bf16[128,1536]{1,0:T(8,128)(2,1)}, bf16[128,1536]{1,0:T(8,128)(2,1)S(1)}, u32[]{:S(2)}, u32[]{:S(2)}) collective-permute-start(bf16[128,1536]{1,0:T(8,128)(2,1)} %fusion.23), channel_id=1, source_target_pairs={{0,16},{16,0},{32,48},{48,32},{64,80},{80,64},{96,112},{112,96},{1... | collective-permute-start | bytes 1179656 | tf_op jit(solution)/shard_map/ppermute | solution.py:196
  263.0 23.1 %collective-permute-start.8 = (bf16[192,2048]{1,0:T(8,128)(2,1)}, bf16[192,2048]{1,0:T(8,128)(2,1)}, u32[]{:S(2)}, u32[]{:S(2)}) collective-permute-start(bf16[192,2048]{1,0:T(8,128)(2,1)} %fusion.12), channel_id=1, source_target_pairs={{0,16},{16,0},{32,48},{48,32},{64,80},{80,64},{96,112},{112,96},{1... | collective-permute-start | bytes 2359304 | tf_op jit(solution)/shard_map/ppermute | solution.py:196
  266.4 7.8 %copy-start.17 = (f32[4,128]{1,0:T(4,128)S(1)}, f32[4,128]{1,0:T(4,128)}, u32[]{:S(2)}) copy-start(f32[4,128]{1,0:T(4,128)} %mul.88) | copy-start | bytes 6148
  266.4 41.3 %all-to-all-start.4 = ((bf16[16,32,1536]{2,1,0:T(8,128)(2,1)}), bf16[16,32,1536]{2,1,0:T(8,128)(2,1)S(1)}, u32[]{:S(2)}, u32[]{:S(2)}) async-start(bf16[16,32,1536]{2,1,0:T(8,128)(2,1)} %bitcast.202), calls=%async_computation.4 | async-start | bytes 3145728 | tf_op jit(solution)/shard_map/all_to_all | solution.py:380
  289.7 18.4 %copy-start.12 = (bf16[1536,16]{0,1:T(8,128)(2,1)S(1)}, bf16[1536,16]{0,1:T(8,128)(2,1)}, u32[]{:S(2)}) copy-start(bf16[1536,16]{0,1:T(8,128)(2,1)} %param.10) | copy-start | bytes 147460
  289.7 18.4 %copy-start.15 = (bf16[256,16]{0,1:T(8,128)(2,1)S(1)}, bf16[256,16]{0,1:T(8,128)(2,1)}, u32[]{:S(2)}) copy-start(bf16[256,16]{0,1:T(8,128)(2,1)} %copy-done.14) | copy-start | bytes 24580
  (11 other events, 58.6 us)

commit v3 on v1

--- a/solution.py
+++ b/solution.py
@@ -198,7 +198,10 @@
     return own_sum + sent.astype(jnp.float32)
 
 
-def _ring_gather_kernel(n, shard_ref, out_ref, send_sem, recv_sem, local_sem):
+def _ring_gather_kernel(n, *refs):
+    count = (len(refs) - 3) // 2
+    shards, outs = refs[:count], refs[count : 2 * count]
+    send_sem, recv_sem, local_sem = refs[2 * count :]
     me = lax.axis_index("dp")
     ex = lax.axis_index("expert")
     right, left, partner = lax.rem(me + 2, n), lax.rem(me + n - 2, n), me + 1 - 2 * lax.rem(me, 2)
@@ -206,70 +209,84 @@
     for peer in (right, left, partner):
         pl.semaphore_signal(barrier, inc=1, device_id=(peer, ex), device_id_type=MESH)
     pl.semaphore_wait(barrier, 3)
-    half = shard_ref.shape[0] // 2
-
-    def send(role, src, slot, rows, peer):
+
+    def send(a, role, src, slot, rows, peer):
         copy = pltpu.make_async_remote_copy(
             src_ref=src,
-            dst_ref=out_ref.at[slot, rows],
-            send_sem=send_sem.at[role],
-            recv_sem=recv_sem.at[role],
+            dst_ref=outs[a].at[slot, rows],
+            send_sem=send_sem.at[a, role],
+            recv_sem=recv_sem.at[a, role],
             device_id=(peer, ex),
             device_id_type=MESH,
         )
         copy.start()
         return copy
 
-    whole, low, high = pl.ds(0, 2 * half), pl.ds(0, half), pl.ds(half, half)
-    local = pltpu.make_async_copy(shard_ref, out_ref.at[me], local_sem.at[0])
-    local.start()
-    first = [
-        send(0, shard_ref, me, whole, right),
-        send(1, shard_ref, me, whole, left),
-        send(2, shard_ref, me, whole, partner),
-    ]
+    spans = []
+    for a in range(count):
+        half = shards[a].shape[0] // 2
+        spans.append((pl.ds(0, 2 * half), pl.ds(0, half), pl.ds(half, half)))
+    locals_, first, second, third = [], [], [], []
+    for a in range(count):
+        local = pltpu.make_async_copy(shards[a], outs[a].at[me], local_sem.at[a])
+        local.start()
+        locals_.append(local)
+        whole = spans[a][0]
+        first += [
+            send(a, 0, shards[a], me, whole, right),
+            send(a, 1, shards[a], me, whole, left),
+            send(a, 2, shards[a], me, whole, partner),
+        ]
     for copy in first:
         copy.wait_recv()
     mate = partner
-    second = [
-        send(3, out_ref.at[left, low], left, low, right),
-        send(4, out_ref.at[right, high], right, high, left),
-        send(5, out_ref.at[mate], mate, whole, right),
-        send(6, out_ref.at[mate], mate, whole, left),
-    ]
-    second[2].wait_recv()
-    second[3].wait_recv()
+    for a in range(count):
+        whole, low, high = spans[a]
+        second += [
+            send(a, 3, outs[a].at[left, low], left, low, right),
+            send(a, 4, outs[a].at[right, high], right, high, left),
+            send(a, 5, outs[a].at[mate], mate, whole, right),
+            send(a, 6, outs[a].at[mate], mate, whole, left),
+        ]
+    for a in range(count):
+        second[4 * a + 2].wait_recv()
+        second[4 * a + 3].wait_recv()
     mate_left, mate_right = lax.rem(mate + n - 2, n), lax.rem(mate + 2, n)
-    third = [
-        send(7, out_ref.at[mate_left, low], mate_left, low, right),
-        send(8, out_ref.at[mate_right, high], mate_right, high, left),
-    ]
+    for a in range(count):
+        whole, low, high = spans[a]
+        third += [
+            send(a, 7, outs[a].at[mate_left, low], mate_left, low, right),
+            send(a, 8, outs[a].at[mate_right, high], mate_right, high, left),
+        ]
     for copy in first:
         copy.wait_send()
-    for copy in second[:2]:
-        copy.wait_recv()
+    for a in range(count):
+        second[4 * a].wait_recv()
+        second[4 * a + 1].wait_recv()
     for copy in second:
         copy.wait_send()
     for copy in third:
         copy.wait_recv()
         copy.wait_send()
-    local.wait()
-
-
-def dp_gather_kernel(shard, n):
+    for local in locals_:
+        local.wait()
+
+
+def dp_gather_kernel(shards, n):
     assert n == 8
+    count = len(shards)
     return pl.pallas_call(
         functools.partial(_ring_gather_kernel, n),
-        out_shape=jax.ShapeDtypeStruct((n,) + shard.shape, shard.dtype),
-        in_specs=[pl.BlockSpec(memory_space=pl.ANY)],
-        out_specs=pl.BlockSpec(memory_space=pl.ANY),
+        out_shape=[jax.ShapeDtypeStruct((n,) + s.shape, s.dtype) for s in shards],
+        in_specs=[pl.BlockSpec(memory_space=pl.ANY)] * count,
+        out_specs=[pl.BlockSpec(memory_space=pl.ANY)] * count,
         scratch_shapes=[
-            pltpu.SemaphoreType.DMA((9,)),
-            pltpu.SemaphoreType.DMA((9,)),
-            pltpu.SemaphoreType.DMA((1,)),
+            pltpu.SemaphoreType.DMA((count, 9)),
+            pltpu.SemaphoreType.DMA((count, 9)),
+            pltpu.SemaphoreType.DMA((count,)),
         ],
         compiler_params=pltpu.CompilerParams(collective_id=2, has_side_effects=True),
-    )(shard)
+    )(*shards)
 
 
 def to_blocks(slot_array, num_blocks, pick_count):
@@ -313,14 +330,10 @@
     cot_rows = cotangent[slot_rows]
     scaled_cot = (slot_gate_values[:, :, None] * cot_rows.astype(jnp.float32)).astype(jnp.bfloat16)
     n = lax.axis_size("dp")
-    shard_rows = w_gate.shape[1]
-    packed = jnp.concatenate(
-        [w_gate[0], w_up[0], w_down[0].reshape(-1, w_gate.shape[2])], axis=0
-    )
-    full = dp_gather_kernel(packed, n)
-    full_gate = full[:, :shard_rows].reshape(1, -1, w_gate.shape[2])
-    full_up = full[:, shard_rows : 2 * shard_rows].reshape(1, -1, w_up.shape[2])
-    full_down = full[:, 2 * shard_rows :].reshape(1, -1, w_down.shape[2])
+    full_gate, full_up, full_down = (
+        g.reshape((1, -1) + g.shape[2:])
+        for g in dp_gather_kernel([w_gate[0], w_up[0], w_down[0]], n)
+    )
     expert_count_axis = lax.axis_size("expert")
     expert_rows = lax.all_to_all(picked, "expert", 0, 0, tiled=True).reshape(1, -1, model_width)
     pre_gate = jnp.einsum(

time: 298 us -> 303 us (1.017)
  waiting for transfers between devices: 38.7 us -> 53.4 us
  local copies, waits for them, and re-layouts: 29.9 us -> 17 us
  Pallas kernels: 88.8 us -> 95.3 us
    all_to_all x1, waiting for transfers between devices: 0.01 us -> 14 us  [body(): lax.all_to_all(picked, 'expert', 0, 0, tiled=True)]
    slice x1 -> x0, local copies, waits for them, and re-layouts: 6.75 us -> none  [body(): full_down = full[:, 2 * shard_rows:].reshape(1, -1, w_down.shape[2])]
    pallas_call x1, Pallas kernels: 88.8 us -> 95.3 us  [dp_gather_kernel(): pl.pallas_call(functools.partial(_ring_gather_kernel, n), out_shape=[jax....]
    another operation x2 -> x0, local copies, waits for them, and re-layouts: 6.15 us -> none
    all_to_all x1, starting transfers between devices: 9.31 us -> 5.06 us  [body(): lax.all_to_all(scaled_cot, 'expert', 0, 0, tiled=True)]
  transfers between devices with their start and end apart: 24 -> 24, of which waited for: 9 -> 9; matrix products, arithmetic and copies ran while one was open for 25% -> 19% of each run, Pallas kernels for 30% -> 32%
where the time goes in v3:
time: 303 us; the launch traced here: 299 us
  Pallas kernels  95.3 us (31%)
  starting transfers between devices  68 us (22%)
  waiting for transfers between devices  53.4 us (18%)
  matrix products  45.8 us (15%)
  other arithmetic  18.5 us (6%)
  local copies, waits for them, and re-layouts  17 us (6%)
    pallas_call x1, Pallas kernels, dp_gather_kernel(): pl.pallas_call(functools.partial(_ring_gather_kernel, n), out_shape=[jax....  95.3 us
    all_to_all x1, waiting for transfers between devices, body(): lax.all_to_all(picked, 'expert', 0, 0, tiled=True)  14 us
    all_to_all x1, starting transfers between devices, body(): lax.all_to_all(d_rows.reshape(expert_count_axis, -1, model_width), 'exper...  12.5 us
    ppermute x4, waiting for transfers between devices, x_ring_scatter(): low = lax.ppermute(blocks[2][:h].astype(jnp.bfloat16), 'dp', _x_shift(n, 1))  10.7 us
    all_to_all x1, starting transfers between devices, body(): lax.all_to_all(expert_out.reshape(expert_count_axis, -1, model_width), 'e...  9.78 us
    ppermute x4, waiting for transfers between devices, x_ring_scatter(): lax.ppermute(to_left.astype(jnp.bfloat16), 'dp', _x_shift(n, -1))  8.92 us
    all_to_all x1, starting transfers between devices, body(): lax.all_to_all(picked, 'expert', 0, 0, tiled=True)  8.76 us
    all_to_all x1, starting transfers between devices, body(): lax.all_to_all(router_full.reshape(devices, -1), ('dp', 'expert'), 0, 0,...  7.95 us
  transfers between devices with their start and end apart: 24, of which 9 were waited for; matrix products, arithmetic and copies ran while one was open for 19% of the time, Pallas kernels for 32%

profile of v3, /device:TPU:5, one launch (start us, length us, event | category | flops | bytes accessed | tf_op | source)
XLA Modules:
  0.0 299.1 jit_solution(1180068627838236693)
XLA Ops:
  1.8 2.9 gather_fusion
  4.7 8.8 %all-to-all-start = ((bf16[16,32,1536]{2,1,0:T(8,128)(2,1)}), bf16[16,32,1536]{2,1,0:T(8,128)(2,1)}, u32[]{:S(2)}, u32[]{:S(2)}) async-start(bf16[16,32,1536]{2,1,0:T(8,128)(2,1)} %bitcast.5), calls=%async_computation | async-start | bytes 3145728 | tf_op jit(solution)/shard_map/all_to_all | solution.py:338
  14.0 4.5 %gather_fusion.2 = f32[512]{0:T(512)S(1)} fusion(f32[16,256]{1,0:T(8,128)S(1)} %bitcast.187, s32[512]{0:T(512)S(1)} %reshape.317), kind=kCustom, calls=%fused_computation.2 | custom fusion | bytes 8192 | tf_op jit(solution)/shard_map/jit(take_along_axis)/gather | solution.py:329
  18.8 2.1 gather_fusion.1
  22.5 14.0 %all-to-all-done = bf16[16,32,1536]{2,1,0:T(8,128)(2,1)} async-done(((bf16[16,32,1536]{2,1,0:T(8,128)(2,1)}), bf16[16,32,1536]{2,1,0:T(8,128)(2,1)}, u32[]{:S(2)}, u32[]{:S(2)}) %all-to-all-start) | async-done | bytes 1572896 | tf_op jit(solution)/shard_map/all_to_all | solution.py:338
  36.4 5.1 %all-to-all-start.2 = ((bf16[16,32,1536]{2,1,0:T(8,128)(2,1)}), bf16[16,32,1536]{2,1,0:T(8,128)(2,1)}, u32[]{:S(2)}, u32[]{:S(2)}) async-start(bf16[16,32,1536]{2,1,0:T(8,128)(2,1)} %fusion), calls=%async_computation.2 | async-start | bytes 3145728 | tf_op jit(solution)/shard_map/all_to_all | solution.py:351
  43.3 95.3 %shard_map.118 = (bf16[8,192,1024]{2,1,0:T(8,128)(2,1)}, bf16[8,192,1024]{2,1,0:T(8,128)(2,1)}, bf16[8,128,1536]{2,1,0:T(8,128)(2,1)}) custom-call(bf16[192,1024]{1,0:T(8,128)(2,1)} %bitcast.200, bf16[192,1024]{1,0:T(8,128)(2,1)} %bitcast.201, bf16[128,1536]{1,0:T(8,128)(2,1)} %bitcast.202), custom_call_target="tpu_custom_call" | custom-call | tf_op jit(solution)/shard_map/pallas_call | solution.py:278
  138.7 5.6 %fusion.39 = f32[512,1024]{1,0:T(8,128)} fusion(bf16[512,1536]{1,0:T(8,128)(2,1)} %bitcast.6, bf16[1536,1024]{1,0:T(8,128)(2,1)} %bitcast.207), kind=kOutput, calls=%fused_computation.116 | convolution fusion | flops 1610612736 | bytes 6815744 | tf_op jit(solution)/shard_map/erd,edh->erh/dot_general | solution.py:339
  144.3 4.6 %fusion.40 = f32[512,1024]{1,0:T(8,128)} fusion(bf16[512,1536]{1,0:T(8,128)(2,1)} %bitcast.6, bf16[1536,1024]{1,0:T(8,128)(2,1)S(1)} %bitcast.205), kind=kOutput, calls=%fused_computation.117 | convolution fusion | flops 1610612736 | bytes 6815744 | tf_op jit(solution)/shard_map/erd,edh->erh/dot_general | solution.py:342
  148.9 7.2 %multiply_convert_fusion = (bf16[512,1024]{1,0:T(8,128)(2,1)S(1)}, bf16[512,1024]{1,0:T(8,128)(2,1)}, bf16[512,1024]{1,0:T(8,128)(2,1)S(1)}) fusion(f32[512,1024]{1,0:T(8,128)} %fusion.39, f32[512,1024]{1,0:T(8,128)} %fusion.40, bf16[512,1536]{1,0:T(8,128)(2,1)} %bitcast.21, bf16[1024,1536]{1,0:T(8,128)(2,1)} %bitcast.209), kind=kOutput, calls=%fused_computation.23 | convolution fusion | flops 1618477056 | bytes 12058624 | tf_op jit(solution)/shard_map/erd,ehd->erh/dot_general | solution.py:353
  156.1 3.0 convolution_convert_fusion.2
  159.1 5.0 %convolution_convert_fusion.1 = bf16[1024,1536]{1,0:T(8,128)(2,1)} fusion(bf16[512,1024]{1,0:T(8,128)(2,1)S(1)} %get-tuple-element.52, bf16[512,1536]{1,0:T(8,128)(2,1)} %bitcast.21), kind=kOutput, calls=%fused_computation.7 | convolution fusion | flops 1612185600 | bytes 5767168 | tf_op jit(solution)/shard_map/erc,erd->cd/dot_general | solution.py:304
  164.0 9.8 %all-to-all-start.1 = ((bf16[16,32,1536]{2,1,0:T(8,128)(2,1)}), bf16[16,32,1536]{2,1,0:T(8,128)(2,1)}, u32[]{:S(2)}, u32[]{:S(2)}) async-start(bf16[16,32,1536]{2,1,0:T(8,128)(2,1)} %bitcast.199), calls=%async_computation.1 | async-start | bytes 3145728 | tf_op jit(solution)/shard_map/all_to_all | solution.py:348
  173.8 4.2 %fusion.41 = f32[512,1536]{1,0:T(8,128)S(1)} fusion(bf16[512,1024]{1,0:T(8,128)(2,1)} %get-tuple-element.51, bf16[1536,1024]{1,0:T(8,128)(2,1)} %bitcast.208), kind=kOutput, calls=%fused_computation.118 | convolution fusion | flops 1610612736 | bytes 7340032 | tf_op jit(solution)/shard_map/erh,edh->erd/dot_general | solution.py:360
  178.2 2.2 collective-permute-start.9
  181.9 3.0 %fusion.4 = bf16[512,1536]{1,0:T(8,128)(2,1)} fusion(f32[512,1536]{1,0:T(8,128)S(1)} %fusion.41, bf16[512,1024]{1,0:T(8,128)(2,1)S(1)} %get-tuple-element.50, bf16[1536,1024]{1,0:T(8,128)(2,1)S(1)} %bitcast.206), kind=kOutput, calls=%fused_computation.14 | convolution fusion | flops 1612185600 | bytes 8912896 | tf_op jit(solution)/shard_map/erh,edh->erd/dot_general | solution.py:361
  184.9 5.2 %convolution_convert_fusion = bf16[1536,2048]{1,0:T(8,128)(2,1)S(1)} fusion(bf16[512,1536]{1,0:T(8,128)(2,1)} %bitcast.6, bf16[1,512,1024]{2,1,0:T(8,128)(2,1)S(1)} %bitcast.211, bf16[1,512,1024]{2,1,0:T(8,128)(2,1)S(1)} %bitcast.212), kind=kOutput, calls=%fused_computation.3 | convolution fusion | flops 3228565504 | bytes 9961472 | tf_op jit(solution)/shard_map/erc,erk->ck/dot_general | solution.py:309
  194.3 2.7 collective-permute-start.16
  197.8 2.8 collective-permute-done
  201.2 7.9 %collective-permute-done.4 = bf16[96,2048]{1,0:T(8,128)(2,1)S(1)} collective-permute-done((bf16[96,2048]{1,0:T(8,128)(2,1)S(1)}, bf16[96,2048]{1,0:T(8,128)(2,1)S(1)}, u32[]{:S(2)}, u32[]{:S(2)}) %collective-permute-start.4) | collective-permute-done | bytes 393248 | tf_op jit(solution)/shard_map/ppermute | solution.py:176
  214.5 4.8 %collective-permute-done.16 = bf16[128,1536]{1,0:T(8,128)(2,1)S(1)} collective-permute-done((bf16[128,1536]{1,0:T(8,128)(2,1)S(1)}, bf16[128,1536]{1,0:T(8,128)(2,1)S(1)}, u32[]{:S(2)}, u32[]{:S(2)}) %collective-permute-start.16) | collective-permute-done | bytes 393248 | tf_op jit(solution)/shard_map/ppermute | solution.py:181
  219.3 2.1 collective-permute-start.5
  224.2 12.5 %all-to-all-start.3 = ((bf16[16,32,1536]{2,1,0:T(8,128)(2,1)}), bf16[16,32,1536]{2,1,0:T(8,128)(2,1)}, u32[]{:S(2)}, u32[]{:S(2)}) async-start(bf16[16,32,1536]{2,1,0:T(8,128)(2,1)} %bitcast.198), calls=%async_computation.3 | async-start | bytes 3145728 | tf_op jit(solution)/shard_map/all_to_all | solution.py:363
  238.3 2.3 fusion.25
  240.6 4.1 %collective-permute-done.7 = bf16[192,2048]{1,0:T(8,128)(2,1)} collective-permute-done((bf16[192,2048]{1,0:T(8,128)(2,1)}, bf16[192,2048]{1,0:T(8,128)(2,1)}, u32[]{:S(2)}, u32[]{:S(2)}) %collective-permute-start.7) | collective-permute-done | bytes 786464 | tf_op jit(solution)/shard_map/ppermute | solution.py:181
  244.7 2.9 fusion.11
  251.8 7.9 %all-to-all-done.3 = bf16[16,32,1536]{2,1,0:T(8,128)(2,1)} async-done(((bf16[16,32,1536]{2,1,0:T(8,128)(2,1)}), bf16[16,32,1536]{2,1,0:T(8,128)(2,1)}, u32[]{:S(2)}, u32[]{:S(2)}) %all-to-all-start.3) | async-done | bytes 1572896 | tf_op jit(solution)/shard_map/all_to_all | solution.py:363
  259.7 8.0 %all-to-all-start.4 = ((f32[128,1,192]{2,1,0:T(1,128)}), f32[128,1,192]{2,1,0:T(1,128)S(1)}, u32[]{:S(2)}, u32[]{:S(2)}) async-start(f32[128,1,192]{2,1,0:T(1,128)} %all_to_all.29), calls=%async_computation.4 | async-start | bytes 262144 | tf_op jit(solution)/shard_map/all_to_all | solution.py:401
  270.7 7.5 %all-to-all-done.4 = f32[128,1,192]{2,1,0:T(1,128)S(1)} async-done(((f32[128,1,192]{2,1,0:T(1,128)}), f32[128,1,192]{2,1,0:T(1,128)S(1)}, u32[]{:S(2)}, u32[]{:S(2)}) %all-to-all-start.4) | async-done | bytes 98336 | tf_op jit(solution)/shard_map/all_to_all | solution.py:401
  279.2 7.1 %all-to-all-start.5 = ((f32[128,1,192]{2,1,0:T(1,128)}), f32[128,1,192]{2,1,0:T(1,128)S(1)}, u32[]{:S(2)}, u32[]{:S(2)}) async-start(f32[128,1,192]{2,1,0:T(1,128)} %broadcast_in_dim.32), calls=%async_computation.5 | async-start | bytes 262144 | tf_op jit(solution)/shard_map/all_to_all | solution.py:407
  286.3 4.0 %fusion.5 = bf16[4,64,1536]{2,1,0:T(8,128)(2,1)} fusion(f32[4,128]{1,0:T(4,128)S(1)} %copy-done.10, s32[4,128]{1,0:T(4,128)S(1)} %copy-done.9, bf16[16,32,1536]{2,1,0:T(8,128)(2,1)} %all-to-all-done.1), kind=kOutput, calls=%fused_computation.17 | convolution fusion | flops 605978624 | bytes 2363392 | tf_op jit(solution)/shard_map/wze,wzi->wei/dot_general | solution.py:372
  290.3 4.0 %all-to-all-done.5 = f32[128,1,192]{2,1,0:T(1,128)S(1)} async-done(((f32[128,1,192]{2,1,0:T(1,128)}), f32[128,1,192]{2,1,0:T(1,128)S(1)}, u32[]{:S(2)}, u32[]{:S(2)}) %all-to-all-start.5) | async-done | bytes 98336 | tf_op jit(solution)/shard_map/all_to_all | solution.py:407
  (113 shorter events, 35.0 us)
Async XLA Ops:
  4.7 8.9 %copy-start.5 = (bf16[1536,16]{0,1:T(8,128)(2,1)S(1)}, bf16[1536,16]{0,1:T(8,128)(2,1)}, u32[]{:S(2)}) copy-start(bf16[1536,16]{0,1:T(8,128)(2,1)} %param.10) | copy-start | bytes 147460
  4.7 31.7 %all-to-all-start = ((bf16[16,32,1536]{2,1,0:T(8,128)(2,1)}), bf16[16,32,1536]{2,1,0:T(8,128)(2,1)}, u32[]{:S(2)}, u32[]{:S(2)}) async-start(bf16[16,32,1536]{2,1,0:T(8,128)(2,1)} %bitcast.5), calls=%async_computation | async-start | bytes 3145728 | tf_op jit(solution)/shard_map/all_to_all | solution.py:338
  36.4 112.4 %all-to-all-start.2 = ((bf16[16,32,1536]{2,1,0:T(8,128)(2,1)}), bf16[16,32,1536]{2,1,0:T(8,128)(2,1)}, u32[]{:S(2)}, u32[]{:S(2)}) async-start(bf16[16,32,1536]{2,1,0:T(8,128)(2,1)} %fusion), calls=%async_computation.2 | async-start | bytes 3145728 | tf_op jit(solution)/shard_map/all_to_all | solution.py:351
  41.7 102.6 %copy-start.7 = (s32[4,16,8]{2,1,0:T(8,128)}, s32[4,16,8]{2,1,0:T(8,128)S(1)}, u32[]{:S(2)}) copy-start(s32[4,16,8]{2,1,0:T(8,128)S(1)} %copy.55) | copy-start | bytes 6148
  138.7 5.6 %copy-start.11 = (bf16[8,192,1024]{2,1,0:T(8,128)(2,1)S(1)}, bf16[8,192,1024]{2,1,0:T(8,128)(2,1)}, u32[]{:S(2)}) copy-start(bf16[8,192,1024]{2,1,0:T(8,128)(2,1)} %get-tuple-element.10) | copy-start | bytes 9437188
  148.9 7.2 %copy-start.13 = (bf16[8,128,1536]{2,1,0:T(8,128)(2,1)S(1)}, bf16[8,128,1536]{2,1,0:T(8,128)(2,1)}, u32[]{:S(2)}) copy-start(bf16[8,128,1536]{2,1,0:T(8,128)(2,1)} %get-tuple-element.11) | copy-start | bytes 9437188
  164.0 60.2 %all-to-all-start.1 = ((bf16[16,32,1536]{2,1,0:T(8,128)(2,1)}), bf16[16,32,1536]{2,1,0:T(8,128)(2,1)}, u32[]{:S(2)}, u32[]{:S(2)}) async-start(bf16[16,32,1536]{2,1,0:T(8,128)(2,1)} %bitcast.199), calls=%async_computation.1 | async-start | bytes 3145728 | tf_op jit(solution)/shard_map/all_to_all | solution.py:348
  178.2 13.7 %collective-permute-start.9 = (bf16[64,1536]{1,0:T(8,128)(2,1)S(1)}, bf16[64,1536]{1,0:T(8,128)(2,1)S(1)}, u32[]{:S(2)}, u32[]{:S(2)}) collective-permute-start(bf16[64,1536]{1,0:T(8,128)(2,1)S(1)} %get-tuple-element.57), channel_id=1, source_target_pairs={{0,32},{16,48},{32,64},{48,80},{64,96},{80,112},{96,0},{112,16},{1... | collective-permute-start | bytes 589832 | tf_op jit(solution)/shard_map/ppermute | solution.py:176
  180.4 13.3 %collective-permute-start.13 = (bf16[64,1536]{1,0:T(8,128)(2,1)S(1)}, bf16[64,1536]{1,0:T(8,128)(2,1)S(1)}, u32[]{:S(2)}, u32[]{:S(2)}) collective-permute-start(bf16[64,1536]{1,0:T(8,128)(2,1)S(1)} %get-tuple-element.59), channel_id=1, source_target_pairs={{0,32},{16,48},{32,64},{48,80},{64,96},{80,112},{96,0},{112,16},{1... | collective-permute-start | bytes 589832 | tf_op jit(solution)/shard_map/ppermute | solution.py:176
  180.9 12.8 %collective-permute-start.15 = (bf16[64,1536]{1,0:T(8,128)(2,1)S(1)}, bf16[64,1536]{1,0:T(8,128)(2,1)S(1)}, u32[]{:S(2)}, u32[]{:S(2)}) collective-permute-start(bf16[64,1536]{1,0:T(8,128)(2,1)S(1)} %get-tuple-element.61), channel_id=1, source_target_pairs={{0,96},{16,112},{32,0},{48,16},{64,32},{80,48},{96,64},{112,80},{1... | collective-permute-start | bytes 589832 | tf_op jit(solution)/shard_map/ppermute | solution.py:177
  181.8 12.3 %collective-permute-start.11 = (bf16[64,1536]{1,0:T(8,128)(2,1)S(1)}, bf16[64,1536]{1,0:T(8,128)(2,1)S(1)}, u32[]{:S(2)}, u32[]{:S(2)}) collective-permute-start(bf16[64,1536]{1,0:T(8,128)(2,1)S(1)} %get-tuple-element.63), channel_id=1, source_target_pairs={{0,96},{16,112},{32,0},{48,16},{64,32},{80,48},{96,64},{112,80},{1... | collective-permute-start | bytes 589832 | tf_op jit(solution)/shard_map/ppermute | solution.py:177
  190.2 20.7 %copy-start.2 = (bf16[1536,2048]{1,0:T(8,128)(2,1)}, bf16[1536,2048]{1,0:T(8,128)(2,1)S(1)}, u32[]{:S(2)}) copy-start(bf16[1536,2048]{1,0:T(8,128)(2,1)S(1)} %convolution_convert_fusion) | copy-start | bytes 18874372
  190.4 10.3 %collective-permute-start = (bf16[96,2048]{1,0:T(8,128)(2,1)S(1)}, bf16[96,2048]{1,0:T(8,128)(2,1)S(1)}, u32[]{:S(2)}, u32[]{:S(2)}) collective-permute-start(bf16[96,2048]{1,0:T(8,128)(2,1)S(1)} %get-tuple-element.42), channel_id=1, source_target_pairs={{0,32},{16,48},{32,64},{48,80},{64,96},{80,112},{96,0},{112,16},{1... | collective-permute-start | bytes 1179656 | tf_op jit(solution)/shard_map/ppermute | solution.py:176
  191.9 17.2 %collective-permute-start.4 = (bf16[96,2048]{1,0:T(8,128)(2,1)S(1)}, bf16[96,2048]{1,0:T(8,128)(2,1)S(1)}, u32[]{:S(2)}, u32[]{:S(2)}) collective-permute-start(bf16[96,2048]{1,0:T(8,128)(2,1)S(1)} %get-tuple-element.44), channel_id=1, source_target_pairs={{0,32},{16,48},{32,64},{48,80},{64,96},{80,112},{96,0},{112,16},{1... | collective-permute-start | bytes 1179656 | tf_op jit(solution)/shard_map/ppermute | solution.py:176
  193.7 16.6 %collective-permute-start.6 = (bf16[96,2048]{1,0:T(8,128)(2,1)S(1)}, bf16[96,2048]{1,0:T(8,128)(2,1)S(1)}, u32[]{:S(2)}, u32[]{:S(2)}) collective-permute-start(bf16[96,2048]{1,0:T(8,128)(2,1)S(1)} %get-tuple-element.46), channel_id=1, source_target_pairs={{0,96},{16,112},{32,0},{48,16},{64,32},{80,48},{96,64},{112,80},{1... | collective-permute-start | bytes 1179656 | tf_op jit(solution)/shard_map/ppermute | solution.py:177
  193.7 17.2 %collective-permute-start.2 = (bf16[96,2048]{1,0:T(8,128)(2,1)S(1)}, bf16[96,2048]{1,0:T(8,128)(2,1)S(1)}, u32[]{:S(2)}, u32[]{:S(2)}) collective-permute-start(bf16[96,2048]{1,0:T(8,128)(2,1)S(1)} %get-tuple-element.48), channel_id=1, source_target_pairs={{0,96},{16,112},{32,0},{48,16},{64,32},{80,48},{96,64},{112,80},{1... | collective-permute-start | bytes 1179656 | tf_op jit(solution)/shard_map/ppermute | solution.py:177
  194.3 25.0 %collective-permute-start.16 = (bf16[128,1536]{1,0:T(8,128)(2,1)S(1)}, bf16[128,1536]{1,0:T(8,128)(2,1)S(1)}, u32[]{:S(2)}, u32[]{:S(2)}) collective-permute-start(bf16[128,1536]{1,0:T(8,128)(2,1)S(1)} %pad_maximum_fusion.7), channel_id=1, source_target_pairs={{0,96},{16,112},{32,0},{48,16},{64,32},{80,48},{96,64},{112,80},{1... | collective-permute-start | bytes 1179656 | tf_op jit(solution)/shard_map/ppermute | solution.py:181
  200.7 20.8 %collective-permute-start.14 = (bf16[128,1536]{1,0:T(8,128)(2,1)S(1)}, bf16[128,1536]{1,0:T(8,128)(2,1)S(1)}, u32[]{:S(2)}, u32[]{:S(2)}) collective-permute-start(bf16[128,1536]{1,0:T(8,128)(2,1)S(1)} %pad_maximum_fusion.6), channel_id=1, source_target_pairs={{0,32},{16,48},{32,64},{48,80},{64,96},{80,112},{96,0},{112,16},{1... | collective-permute-start | bytes 1179656 | tf_op jit(solution)/shard_map/ppermute | solution.py:180
  209.1 27.6 %collective-permute-start.12 = (bf16[128,1536]{1,0:T(8,128)(2,1)S(1)}, bf16[128,1536]{1,0:T(8,128)(2,1)S(1)}, u32[]{:S(2)}, u32[]{:S(2)}) collective-permute-start(bf16[128,1536]{1,0:T(8,128)(2,1)S(1)} %pad_maximum_fusion.5), channel_id=1, source_target_pairs={{0,96},{16,112},{32,0},{48,16},{64,32},{80,48},{96,64},{112,80},{1... | collective-permute-start | bytes 1179656 | tf_op jit(solution)/shard_map/ppermute | solution.py:181
  210.3 26.5 %collective-permute-start.10 = (bf16[128,1536]{1,0:T(8,128)(2,1)}, bf16[128,1536]{1,0:T(8,128)(2,1)}, u32[]{:S(2)}, u32[]{:S(2)}) collective-permute-start(bf16[128,1536]{1,0:T(8,128)(2,1)} %pad_maximum_fusion.4), channel_id=1, source_target_pairs={{0,32},{16,48},{32,64},{48,80},{64,96},{80,112},{96,0},{112,16},{1... | collective-permute-start | bytes 1179656 | tf_op jit(solution)/shard_map/ppermute | solution.py:180
  212.4 32.3 %collective-permute-start.7 = (bf16[192,2048]{1,0:T(8,128)(2,1)}, bf16[192,2048]{1,0:T(8,128)(2,1)}, u32[]{:S(2)}, u32[]{:S(2)}) collective-permute-start(bf16[192,2048]{1,0:T(8,128)(2,1)} %pad_maximum_fusion.3), channel_id=1, source_target_pairs={{0,96},{16,112},{32,0},{48,16},{64,32},{80,48},{96,64},{112,80},{1... | collective-permute-start | bytes 2359304 | tf_op jit(solution)/shard_map/ppermute | solution.py:181
  219.3 25.4 %collective-permute-start.5 = (bf16[192,2048]{1,0:T(8,128)(2,1)}, bf16[192,2048]{1,0:T(8,128)(2,1)}, u32[]{:S(2)}, u32[]{:S(2)}) collective-permute-start(bf16[192,2048]{1,0:T(8,128)(2,1)} %pad_maximum_fusion.2), channel_id=1, source_target_pairs={{0,32},{16,48},{32,64},{48,80},{64,96},{80,112},{96,0},{112,16},{1... | collective-permute-start | bytes 2359304 | tf_op jit(solution)/shard_map/ppermute | solution.py:180
  222.3 16.0 %collective-permute-start.17 = (bf16[128,1536]{1,0:T(8,128)(2,1)}, bf16[128,1536]{1,0:T(8,128)(2,1)}, u32[]{:S(2)}, u32[]{:S(2)}) collective-permute-start(bf16[128,1536]{1,0:T(8,128)(2,1)} %fusion.22), channel_id=1, source_target_pairs={{0,16},{16,0},{32,48},{48,32},{64,80},{80,64},{96,112},{112,96},{1... | collective-permute-start | bytes 1179656 | tf_op jit(solution)/shard_map/ppermute | solution.py:196
  224.2 35.4 %all-to-all-start.3 = ((bf16[16,32,1536]{2,1,0:T(8,128)(2,1)}), bf16[16,32,1536]{2,1,0:T(8,128)(2,1)}, u32[]{:S(2)}, u32[]{:S(2)}) async-start(bf16[16,32,1536]{2,1,0:T(8,128)(2,1)} %bitcast.198), calls=%async_computation.3 | async-start | bytes 3145728 | tf_op jit(solution)/shard_map/all_to_all | solution.py:363
  236.7 59.0 %collective-permute-start.3 = (bf16[192,2048]{1,0:T(8,128)(2,1)}, bf16[192,2048]{1,0:T(8,128)(2,1)S(1)}, u32[]{:S(2)}, u32[]{:S(2)}) collective-permute-start(bf16[192,2048]{1,0:T(8,128)(2,1)} %pad_maximum_fusion.1), channel_id=1, source_target_pairs={{0,96},{16,112},{32,0},{48,16},{64,32},{80,48},{96,64},{112,80},{1... | collective-permute-start | bytes 2359304 | tf_op jit(solution)/shard_map/ppermute | solution.py:181
  236.8 58.9 %collective-permute-start.1 = (bf16[192,2048]{1,0:T(8,128)(2,1)}, bf16[192,2048]{1,0:T(8,128)(2,1)}, u32[]{:S(2)}, u32[]{:S(2)}) collective-permute-start(bf16[192,2048]{1,0:T(8,128)(2,1)} %pad_maximum_fusion), channel_id=1, source_target_pairs={{0,32},{16,48},{32,64},{48,80},{64,96},{80,112},{96,0},{112,16},{1... | collective-permute-start | bytes 2359304 | tf_op jit(solution)/shard_map/ppermute | solution.py:180
  247.6 48.1 %collective-permute-start.8 = (bf16[192,2048]{1,0:T(8,128)(2,1)}, bf16[192,2048]{1,0:T(8,128)(2,1)}, u32[]{:S(2)}, u32[]{:S(2)}) collective-permute-start(bf16[192,2048]{1,0:T(8,128)(2,1)} %fusion.11), channel_id=1, source_target_pairs={{0,16},{16,0},{32,48},{48,32},{64,80},{80,64},{96,112},{112,96},{1... | collective-permute-start | bytes 2359304 | tf_op jit(solution)/shard_map/ppermute | solution.py:196
  249.5 18.2 %copy-start.9 = (s32[4,128]{1,0:T(4,128)S(1)}, s32[4,128]{1,0:T(4,128)}, u32[]{:S(2)}) copy-start(s32[4,128]{1,0:T(4,128)} %eq.41) | copy-start | bytes 6148
  250.7 18.8 %copy-start.6 = (bf16[1536,16]{0,1:T(8,128)(2,1)S(1)}, bf16[1536,16]{0,1:T(8,128)(2,1)}, u32[]{:S(2)}) copy-start(bf16[1536,16]{0,1:T(8,128)(2,1)} %param.10) | copy-start | bytes 147460
  259.7 18.6 %all-to-all-start.4 = ((f32[128,1,192]{2,1,0:T(1,128)}), f32[128,1,192]{2,1,0:T(1,128)S(1)}, u32[]{:S(2)}, u32[]{:S(2)}) async-start(f32[128,1,192]{2,1,0:T(1,128)} %all_to_all.29), calls=%async_computation.4 | async-start | bytes 262144 | tf_op jit(solution)/shard_map/all_to_all | solution.py:401
  269.4 16.9 %copy-start.10 = (f32[4,128]{1,0:T(4,128)S(1)}, f32[4,128]{1,0:T(4,128)}, u32[]{:S(2)}) copy-start(f32[4,128]{1,0:T(4,128)} %mul.88) | copy-start | bytes 6148
  279.2 15.1 %all-to-all-start.5 = ((f32[128,1,192]{2,1,0:T(1,128)}), f32[128,1,192]{2,1,0:T(1,128)S(1)}, u32[]{:S(2)}, u32[]{:S(2)}) async-start(f32[128,1,192]{2,1,0:T(1,128)} %broadcast_in_dim.32), calls=%async_computation.5 | async-start | bytes 262144 | tf_op jit(solution)/shard_map/all_to_all | solution.py:407
  (7 other events, 23.9 us)

commit v4 on v3

--- a/solution.py
+++ b/solution.py
@@ -335,7 +335,11 @@
         for g in dp_gather_kernel([w_gate[0], w_up[0], w_down[0]], n)
     )
     expert_count_axis = lax.axis_size("expert")
-    expert_rows = lax.all_to_all(picked, "expert", 0, 0, tiled=True).reshape(1, -1, model_width)
+    dispatched = lax.all_to_all(
+        jnp.concatenate([picked, scaled_cot], axis=1), "expert", 0, 0, tiled=True
+    )
+    slot_width = picked.shape[1]
+    expert_rows = dispatched[:, :slot_width].reshape(1, -1, model_width)
     pre_gate = jnp.einsum(
         "erd,edh->erh", expert_rows, full_gate, preferred_element_type=jnp.float32
     )
@@ -348,7 +352,7 @@
     returned = lax.all_to_all(
         expert_out.reshape(expert_count_axis, -1, model_width), "expert", 0, 0, tiled=True
     )
-    expert_cot = lax.all_to_all(scaled_cot, "expert", 0, 0, tiled=True).reshape(1, -1, model_width)
+    expert_cot = dispatched[:, slot_width:].reshape(1, -1, model_width)
     back_gate, back_up, back_down = (full_gate, full_up, full_down)
     d_hidden = jnp.einsum("erd,ehd->erh", expert_cot, back_down, preferred_element_type=jnp.float32)
     gate_sigmoid = jax.nn.sigmoid(pre_gate)

time: 303 us -> 293 us (0.967)
  Pallas kernels: 95.3 us -> 114 us
  waiting for transfers between devices: 53.4 us -> 40 us
  matrix products: 45.8 us -> 33.5 us
  starting transfers between devices: 68 us -> 60.5 us
  local copies, waits for them, and re-layouts: 17 us -> 21.1 us
    pallas_call x1, Pallas kernels: 95.3 us -> 114 us  [dp_gather_kernel(): pl.pallas_call(functools.partial(_ring_gather_kernel, n), out_shape=[jax....]
    all_to_all x2 -> x1, waiting for transfers between devices: 14 us -> 0.01 us  [body(): lax.all_to_all(jnp.concatenate([picked, scaled_cot], axis=1), 'expert', 0...]
    all_to_all x2 -> x1, starting transfers between devices: 13.8 us -> 8.63 us  [body(): lax.all_to_all(jnp.concatenate([picked, scaled_cot], axis=1), 'expert', 0...]
    dot_general x1, matrix products: 5.6 us -> 1.79 us  [body(): jnp.einsum('erd,edh->erh', expert_rows, full_gate, preferred_element_type...]
    dot_general x1, matrix products: 7.21 us -> 3.52 us  [body(): jnp.einsum('erd,ehd->erh', expert_cot, back_down, preferred_element_type=...]
  transfers between devices with their start and end apart: 24 -> 23, of which waited for: 9 -> 8; matrix products, arithmetic and copies ran while one was open for 19% -> 13% of each run, Pallas kernels for 32% -> 39%
where the time goes in v4:
time: 293 us; the launch traced here: 289 us
  Pallas kernels  114 us (39%)
  starting transfers between devices  60.5 us (21%)
  waiting for transfers between devices  40 us (14%)
  matrix products  33.5 us (11%)
  local copies, waits for them, and re-layouts  21.1 us (7%)
  other arithmetic  19.3 us (7%)
    pallas_call x1, Pallas kernels, dp_gather_kernel(): pl.pallas_call(functools.partial(_ring_gather_kernel, n), out_shape=[jax....  114 us
    all_to_all x1, starting transfers between devices, body(): lax.all_to_all(d_rows.reshape(expert_count_axis, -1, model_width), 'exper...  13.2 us
    ppermute x4, waiting for transfers between devices, x_ring_scatter(): low = lax.ppermute(blocks[2][:h].astype(jnp.bfloat16), 'dp', _x_shift(n, 1))  10.7 us
    all_to_all x1, waiting for transfers between devices, body(): lax.all_to_all(d_rows.reshape(expert_count_axis, -1, model_width), 'exper...  8.67 us
    all_to_all x1, starting transfers between devices, body(): lax.all_to_all(jnp.concatenate([picked, scaled_cot], axis=1), 'expert', 0...  8.63 us
    ppermute x4, waiting for transfers between devices, x_ring_scatter(): lax.ppermute(to_left.astype(jnp.bfloat16), 'dp', _x_shift(n, -1))  8.16 us
    all_to_all x1, waiting for transfers between devices, body(): lax.all_to_all(router_full.reshape(devices, -1), ('dp', 'expert'), 0, 0,...  8.13 us
    all_to_all x1, starting transfers between devices, body(): lax.all_to_all(expert_out.reshape(expert_count_axis, -1, model_width), 'e...  7.99 us
  transfers between devices with their start and end apart: 23, of which 8 were waited for; matrix products, arithmetic and copies ran while one was open for 13% of the time, Pallas kernels for 39%

profile of v4, /device:TPU:5, one launch (start us, length us, event | category | flops | bytes accessed | tf_op | source)
XLA Modules:
  0.0 289.3 jit_solution(7994671331690608311)
XLA Ops:
  2.9 4.5 %gather_fusion.2 = f32[512]{0:T(512)S(1)} fusion(f32[16,256]{1,0:T(8,128)S(1)} %bitcast.187, s32[512]{0:T(512)S(1)} %reshape.317), kind=kCustom, calls=%fused_computation.2 | custom fusion | bytes 8192 | tf_op jit(solution)/shard_map/jit(take_along_axis)/gather | solution.py:329
  7.9 2.9 %gather_fusion = bf16[512,1536]{1,0:T(8,128)(2,1)} fusion(bf16[256,1536]{1,0:T(8,128)(2,1)S(1)} %copy-done, s32[1024]{0:T(1024)S(1)} %pad_clamp_fusion), kind=kCustom, calls=%fused_computation | custom fusion | bytes 3147776 | tf_op jit(solution)/shard_map/gather | solution.py:328
  10.9 2.1 gather_fusion.1
  14.4 1.9 pad_maximum_fusion
  16.4 8.6 %all-to-all-start = ((bf16[16,64,1536]{2,1,0:T(8,128)(2,1)}), bf16[16,64,1536]{2,1,0:T(8,128)(2,1)}, u32[]{:S(2)}, u32[]{:S(2)}) async-start(bf16[16,64,1536]{2,1,0:T(8,128)(2,1)} %pad_maximum_fusion), calls=%async_computation | async-start | bytes 6291456 | tf_op jit(solution)/shard_map/all_to_all | solution.py:338
  26.8 113.9 %shard_map.118 = (bf16[8,192,1024]{2,1,0:T(8,128)(2,1)}, bf16[8,192,1024]{2,1,0:T(8,128)(2,1)}, bf16[8,128,1536]{2,1,0:T(8,128)(2,1)}) custom-call(bf16[192,1024]{1,0:T(8,128)(2,1)} %bitcast.206, bf16[192,1024]{1,0:T(8,128)(2,1)} %bitcast.207, bf16[128,1536]{1,0:T(8,128)(2,1)} %bitcast.208), custom_call_target="tpu_custom_call" | custom-call | tf_op jit(solution)/shard_map/pallas_call | solution.py:278
  140.7 2.2 fusion.39
  147.3 3.5 %multiply_convert_fusion = (bf16[512,1024]{1,0:T(8,128)(2,1)S(1)}, bf16[512,1024]{1,0:T(8,128)(2,1)}, bf16[512,1024]{1,0:T(8,128)(2,1)S(1)}) fusion(f32[512,1024]{1,0:T(8,128)S(1)} %fusion.40, f32[512,1024]{1,0:T(8,128)S(1)} %fusion.41, bf16[512,1536]{1,0:T(8,128)(2,1)S(1)} %bitcast.204, bf16[1024,1536]{1,0:T(8,128)(2,1)S(1)} %bitcast.215), kind=kOutput, calls=%fused_computation.24 | convolution fusion | flops 1618477056 | bytes 12058624 | tf_op jit(solution)/shard_map/erd,ehd->erh/dot_general | solution.py:357
  150.8 3.0 %convolution_convert_fusion.2 = bf16[512,1536]{1,0:T(8,128)(2,1)} fusion(bf16[512,1024]{1,0:T(8,128)(2,1)S(1)} %get-tuple-element.52, bf16[1024,1536]{1,0:T(8,128)(2,1)S(1)} %bitcast.216), kind=kOutput, calls=%fused_computation.16 | convolution fusion | flops 1611399168 | bytes 5767168 | tf_op jit(solution)/shard_map/erh,ehd->erd/dot_general | solution.py:349
  153.8 3.6 %convolution_convert_fusion.1 = bf16[1024,1536]{1,0:T(8,128)(2,1)} fusion(bf16[512,1024]{1,0:T(8,128)(2,1)S(1)} %get-tuple-element.52, bf16[512,1536]{1,0:T(8,128)(2,1)S(1)} %bitcast.205), kind=kOutput, calls=%fused_computation.7 | convolution fusion | flops 1612185600 | bytes 5767168 | tf_op jit(solution)/shard_map/erc,erd->cd/dot_general | solution.py:304
  157.3 8.0 %all-to-all-start.1 = ((bf16[16,32,1536]{2,1,0:T(8,128)(2,1)}), bf16[16,32,1536]{2,1,0:T(8,128)(2,1)}, u32[]{:S(2)}, u32[]{:S(2)}) async-start(bf16[16,32,1536]{2,1,0:T(8,128)(2,1)} %bitcast.200), calls=%async_computation.1 | async-start | bytes 3145728 | tf_op jit(solution)/shard_map/all_to_all | solution.py:352
  165.3 4.2 %fusion.42 = f32[512,1536]{1,0:T(8,128)S(1)} fusion(bf16[512,1024]{1,0:T(8,128)(2,1)} %get-tuple-element.51, bf16[1536,1024]{1,0:T(8,128)(2,1)} %bitcast.213), kind=kOutput, calls=%fused_computation.120 | convolution fusion | flops 1610612736 | bytes 7340032 | tf_op jit(solution)/shard_map/erh,edh->erd/dot_general | solution.py:364
  169.7 2.2 collective-permute-start.9
  173.4 3.1 %fusion.4 = bf16[512,1536]{1,0:T(8,128)(2,1)} fusion(f32[512,1536]{1,0:T(8,128)S(1)} %fusion.42, bf16[512,1024]{1,0:T(8,128)(2,1)S(1)} %get-tuple-element.50, bf16[1536,1024]{1,0:T(8,128)(2,1)S(1)} %bitcast.212), kind=kOutput, calls=%fused_computation.15 | convolution fusion | flops 1612185600 | bytes 8912896 | tf_op jit(solution)/shard_map/erh,edh->erd/dot_general | solution.py:365
  176.5 3.8 %convolution_convert_fusion = bf16[1536,2048]{1,0:T(8,128)(2,1)S(1)} fusion(bf16[512,1536]{1,0:T(8,128)(2,1)S(1)} %bitcast.203, bf16[1,512,1024]{2,1,0:T(8,128)(2,1)S(1)} %bitcast.217, bf16[1,512,1024]{2,1,0:T(8,128)(2,1)S(1)} %bitcast.218), kind=kOutput, calls=%fused_computation.3 | convolution fusion | flops 3228565504 | bytes 9961472 | tf_op jit(solution)/shard_map/erc,erk->ck/dot_general | solution.py:309
  184.5 2.7 collective-permute-start.16
  188.0 2.8 collective-permute-done
  191.4 7.9 %collective-permute-done.4 = bf16[96,2048]{1,0:T(8,128)(2,1)S(1)} collective-permute-done((bf16[96,2048]{1,0:T(8,128)(2,1)S(1)}, bf16[96,2048]{1,0:T(8,128)(2,1)S(1)}, u32[]{:S(2)}, u32[]{:S(2)}) %collective-permute-start.4) | collective-permute-done | bytes 393248 | tf_op jit(solution)/shard_map/ppermute | solution.py:176
  204.7 4.8 %collective-permute-done.16 = bf16[128,1536]{1,0:T(8,128)(2,1)S(1)} collective-permute-done((bf16[128,1536]{1,0:T(8,128)(2,1)S(1)}, bf16[128,1536]{1,0:T(8,128)(2,1)S(1)}, u32[]{:S(2)}, u32[]{:S(2)}) %collective-permute-start.16) | collective-permute-done | bytes 393248 | tf_op jit(solution)/shard_map/ppermute | solution.py:181
  209.5 2.1 collective-permute-start.5
  214.4 13.2 %all-to-all-start.2 = ((bf16[16,32,1536]{2,1,0:T(8,128)(2,1)}), bf16[16,32,1536]{2,1,0:T(8,128)(2,1)}, u32[]{:S(2)}, u32[]{:S(2)}) async-start(bf16[16,32,1536]{2,1,0:T(8,128)(2,1)} %bitcast.199), calls=%async_computation.2 | async-start | bytes 3145728 | tf_op jit(solution)/shard_map/all_to_all | solution.py:367
  229.2 2.3 fusion.25
  231.5 3.4 %collective-permute-done.7 = bf16[192,2048]{1,0:T(8,128)(2,1)} collective-permute-done((bf16[192,2048]{1,0:T(8,128)(2,1)}, bf16[192,2048]{1,0:T(8,128)(2,1)}, u32[]{:S(2)}, u32[]{:S(2)}) %collective-permute-start.7) | collective-permute-done | bytes 786464 | tf_op jit(solution)/shard_map/ppermute | solution.py:181
  234.9 2.9 fusion.11
  237.8 1.9 fusion.1
  241.9 8.7 %all-to-all-done.2 = bf16[16,32,1536]{2,1,0:T(8,128)(2,1)} async-done(((bf16[16,32,1536]{2,1,0:T(8,128)(2,1)}), bf16[16,32,1536]{2,1,0:T(8,128)(2,1)}, u32[]{:S(2)}, u32[]{:S(2)}) %all-to-all-start.2) | async-done | bytes 1572896 | tf_op jit(solution)/shard_map/all_to_all | solution.py:367
  250.6 7.4 %all-to-all-start.3 = ((f32[128,1,192]{2,1,0:T(1,128)}), f32[128,1,192]{2,1,0:T(1,128)S(1)}, u32[]{:S(2)}, u32[]{:S(2)}) async-start(f32[128,1,192]{2,1,0:T(1,128)} %all_to_all.25), calls=%async_computation.3 | async-start | bytes 262144 | tf_op jit(solution)/shard_map/all_to_all | solution.py:405
  261.1 8.1 %all-to-all-done.3 = f32[128,1,192]{2,1,0:T(1,128)S(1)} async-done(((f32[128,1,192]{2,1,0:T(1,128)}), f32[128,1,192]{2,1,0:T(1,128)S(1)}, u32[]{:S(2)}, u32[]{:S(2)}) %all-to-all-start.3) | async-done | bytes 98336 | tf_op jit(solution)/shard_map/all_to_all | solution.py:405
  270.1 6.4 %all-to-all-start.4 = ((f32[128,1,192]{2,1,0:T(1,128)}), f32[128,1,192]{2,1,0:T(1,128)S(1)}, u32[]{:S(2)}, u32[]{:S(2)}) async-start(f32[128,1,192]{2,1,0:T(1,128)} %broadcast_in_dim.32), calls=%async_computation.4 | async-start | bytes 262144 | tf_op jit(solution)/shard_map/all_to_all | solution.py:411
  276.5 4.0 %fusion.5 = bf16[4,64,1536]{2,1,0:T(8,128)(2,1)} fusion(f32[4,128]{1,0:T(4,128)S(1)} %copy-done.12, s32[4,128]{1,0:T(4,128)S(1)} %copy-done.11, bf16[16,32,1536]{2,1,0:T(8,128)(2,1)} %all-to-all-done.1), kind=kOutput, calls=%fused_computation.18 | convolution fusion | flops 605978624 | bytes 2363392 | tf_op jit(solution)/shard_map/wze,wzi->wei/dot_general | solution.py:376
  280.5 4.0 %all-to-all-done.4 = f32[128,1,192]{2,1,0:T(1,128)S(1)} async-done(((f32[128,1,192]{2,1,0:T(1,128)}), f32[128,1,192]{2,1,0:T(1,128)S(1)}, u32[]{:S(2)}, u32[]{:S(2)}) %all-to-all-start.4) | async-done | bytes 98336 | tf_op jit(solution)/shard_map/all_to_all | solution.py:411
  285.9 2.1 fusion.13
  (119 shorter events, 36.0 us)
Async XLA Ops:
  2.9 4.7 %copy-start.7 = (s32[4,16,8]{1,2,0:T(8,128)S(1)}, s32[4,16,8]{1,2,0:T(8,128)}, u32[]{:S(2)}) copy-start(s32[4,16,8]{1,2,0:T(8,128)} %param.9) | copy-start | bytes 6148
  16.4 124.3 %all-to-all-start = ((bf16[16,64,1536]{2,1,0:T(8,128)(2,1)}), bf16[16,64,1536]{2,1,0:T(8,128)(2,1)}, u32[]{:S(2)}, u32[]{:S(2)}) async-start(bf16[16,64,1536]{2,1,0:T(8,128)(2,1)} %pad_maximum_fusion), calls=%async_computation | async-start | bytes 6291456 | tf_op jit(solution)/shard_map/all_to_all | solution.py:338
  25.2 117.8 %copy-start.9 = (s32[4,16,8]{2,1,0:T(8,128)}, s32[4,16,8]{2,1,0:T(8,128)S(1)}, u32[]{:S(2)}) copy-start(s32[4,16,8]{2,1,0:T(8,128)S(1)} %copy.55) | copy-start | bytes 6148
  157.3 57.1 %all-to-all-start.1 = ((bf16[16,32,1536]{2,1,0:T(8,128)(2,1)}), bf16[16,32,1536]{2,1,0:T(8,128)(2,1)}, u32[]{:S(2)}, u32[]{:S(2)}) async-start(bf16[16,32,1536]{2,1,0:T(8,128)(2,1)} %bitcast.200), calls=%async_computation.1 | async-start | bytes 3145728 | tf_op jit(solution)/shard_map/all_to_all | solution.py:352
  165.3 4.2 %copy-start.4 = (bf16[1024,1536]{1,0:T(8,128)(2,1)S(1)}, bf16[1024,1536]{1,0:T(8,128)(2,1)}, u32[]{:S(2)}) copy-start(bf16[1024,1536]{1,0:T(8,128)(2,1)} %convolution_convert_fusion.1) | copy-start | bytes 9437188
  169.5 3.8 %copy-start.14 = (bf16[8,192,1024]{2,1,0:T(8,128)(2,1)S(1)}, bf16[8,192,1024]{2,1,0:T(8,128)(2,1)}, u32[]{:S(2)}) copy-start(bf16[8,192,1024]{2,1,0:T(8,128)(2,1)} %get-tuple-element.10) | copy-start | bytes 9437188
  169.7 12.4 %collective-permute-start.9 = (bf16[64,1536]{1,0:T(8,128)(2,1)S(1)}, bf16[64,1536]{1,0:T(8,128)(2,1)S(1)}, u32[]{:S(2)}, u32[]{:S(2)}) collective-permute-start(bf16[64,1536]{1,0:T(8,128)(2,1)S(1)} %get-tuple-element.57), channel_id=1, source_target_pairs={{0,32},{16,48},{32,64},{48,80},{64,96},{80,112},{96,0},{112,16},{1... | collective-permute-start | bytes 589832 | tf_op jit(solution)/shard_map/ppermute | solution.py:176
  171.9 12.0 %collective-permute-start.13 = (bf16[64,1536]{1,0:T(8,128)(2,1)S(1)}, bf16[64,1536]{1,0:T(8,128)(2,1)S(1)}, u32[]{:S(2)}, u32[]{:S(2)}) collective-permute-start(bf16[64,1536]{1,0:T(8,128)(2,1)S(1)} %get-tuple-element.59), channel_id=1, source_target_pairs={{0,32},{16,48},{32,64},{48,80},{64,96},{80,112},{96,0},{112,16},{1... | collective-permute-start | bytes 589832 | tf_op jit(solution)/shard_map/ppermute | solution.py:176
  172.4 11.4 %collective-permute-start.15 = (bf16[64,1536]{1,0:T(8,128)(2,1)S(1)}, bf16[64,1536]{1,0:T(8,128)(2,1)S(1)}, u32[]{:S(2)}, u32[]{:S(2)}) collective-permute-start(bf16[64,1536]{1,0:T(8,128)(2,1)S(1)} %get-tuple-element.61), channel_id=1, source_target_pairs={{0,96},{16,112},{32,0},{48,16},{64,32},{80,48},{96,64},{112,80},{1... | collective-permute-start | bytes 589832 | tf_op jit(solution)/shard_map/ppermute | solution.py:177
  173.3 10.9 %collective-permute-start.11 = (bf16[64,1536]{1,0:T(8,128)(2,1)S(1)}, bf16[64,1536]{1,0:T(8,128)(2,1)S(1)}, u32[]{:S(2)}, u32[]{:S(2)}) collective-permute-start(bf16[64,1536]{1,0:T(8,128)(2,1)S(1)} %get-tuple-element.63), channel_id=1, source_target_pairs={{0,96},{16,112},{32,0},{48,16},{64,32},{80,48},{96,64},{112,80},{1... | collective-permute-start | bytes 589832 | tf_op jit(solution)/shard_map/ppermute | solution.py:177
  173.4 3.1 %copy-start.17 = (bf16[512,1024]{1,0:T(8,128)(2,1)S(1)}, bf16[512,1024]{1,0:T(8,128)(2,1)}, u32[]{:S(2)}) copy-start(bf16[512,1024]{1,0:T(8,128)(2,1)} %get-tuple-element.51) | copy-start | bytes 3145732
  180.3 20.8 %copy-start.3 = (bf16[1536,2048]{1,0:T(8,128)(2,1)}, bf16[1536,2048]{1,0:T(8,128)(2,1)S(1)}, u32[]{:S(2)}) copy-start(bf16[1536,2048]{1,0:T(8,128)(2,1)S(1)} %convolution_convert_fusion) | copy-start | bytes 18874372
  180.6 10.3 %collective-permute-start = (bf16[96,2048]{1,0:T(8,128)(2,1)S(1)}, bf16[96,2048]{1,0:T(8,128)(2,1)S(1)}, u32[]{:S(2)}, u32[]{:S(2)}) collective-permute-start(bf16[96,2048]{1,0:T(8,128)(2,1)S(1)} %get-tuple-element.42), channel_id=1, source_target_pairs={{0,32},{16,48},{32,64},{48,80},{64,96},{80,112},{96,0},{112,16},{1... | collective-permute-start | bytes 1179656 | tf_op jit(solution)/shard_map/ppermute | solution.py:176
  182.1 17.2 %collective-permute-start.4 = (bf16[96,2048]{1,0:T(8,128)(2,1)S(1)}, bf16[96,2048]{1,0:T(8,128)(2,1)S(1)}, u32[]{:S(2)}, u32[]{:S(2)}) collective-permute-start(bf16[96,2048]{1,0:T(8,128)(2,1)S(1)} %get-tuple-element.44), channel_id=1, source_target_pairs={{0,32},{16,48},{32,64},{48,80},{64,96},{80,112},{96,0},{112,16},{1... | collective-permute-start | bytes 1179656 | tf_op jit(solution)/shard_map/ppermute | solution.py:176
  183.9 16.6 %collective-permute-start.6 = (bf16[96,2048]{1,0:T(8,128)(2,1)S(1)}, bf16[96,2048]{1,0:T(8,128)(2,1)S(1)}, u32[]{:S(2)}, u32[]{:S(2)}) collective-permute-start(bf16[96,2048]{1,0:T(8,128)(2,1)S(1)} %get-tuple-element.46), channel_id=1, source_target_pairs={{0,96},{16,112},{32,0},{48,16},{64,32},{80,48},{96,64},{112,80},{1... | collective-permute-start | bytes 1179656 | tf_op jit(solution)/shard_map/ppermute | solution.py:177
  183.9 17.2 %collective-permute-start.2 = (bf16[96,2048]{1,0:T(8,128)(2,1)S(1)}, bf16[96,2048]{1,0:T(8,128)(2,1)S(1)}, u32[]{:S(2)}, u32[]{:S(2)}) collective-permute-start(bf16[96,2048]{1,0:T(8,128)(2,1)S(1)} %get-tuple-element.48), channel_id=1, source_target_pairs={{0,96},{16,112},{32,0},{48,16},{64,32},{80,48},{96,64},{112,80},{1... | collective-permute-start | bytes 1179656 | tf_op jit(solution)/shard_map/ppermute | solution.py:177
  184.5 25.0 %collective-permute-start.16 = (bf16[128,1536]{1,0:T(8,128)(2,1)S(1)}, bf16[128,1536]{1,0:T(8,128)(2,1)S(1)}, u32[]{:S(2)}, u32[]{:S(2)}) collective-permute-start(bf16[128,1536]{1,0:T(8,128)(2,1)S(1)} %pad_maximum_fusion.8), channel_id=1, source_target_pairs={{0,96},{16,112},{32,0},{48,16},{64,32},{80,48},{96,64},{112,80},{1... | collective-permute-start | bytes 1179656 | tf_op jit(solution)/shard_map/ppermute | solution.py:181
  190.8 20.8 %collective-permute-start.14 = (bf16[128,1536]{1,0:T(8,128)(2,1)S(1)}, bf16[128,1536]{1,0:T(8,128)(2,1)S(1)}, u32[]{:S(2)}, u32[]{:S(2)}) collective-permute-start(bf16[128,1536]{1,0:T(8,128)(2,1)S(1)} %pad_maximum_fusion.7), channel_id=1, source_target_pairs={{0,32},{16,48},{32,64},{48,80},{64,96},{80,112},{96,0},{112,16},{1... | collective-permute-start | bytes 1179656 | tf_op jit(solution)/shard_map/ppermute | solution.py:180
  199.3 28.4 %collective-permute-start.12 = (bf16[128,1536]{1,0:T(8,128)(2,1)S(1)}, bf16[128,1536]{1,0:T(8,128)(2,1)S(1)}, u32[]{:S(2)}, u32[]{:S(2)}) collective-permute-start(bf16[128,1536]{1,0:T(8,128)(2,1)S(1)} %pad_maximum_fusion.6), channel_id=1, source_target_pairs={{0,96},{16,112},{32,0},{48,16},{64,32},{80,48},{96,64},{112,80},{1... | collective-permute-start | bytes 1179656 | tf_op jit(solution)/shard_map/ppermute | solution.py:181
  200.4 27.3 %collective-permute-start.10 = (bf16[128,1536]{1,0:T(8,128)(2,1)}, bf16[128,1536]{1,0:T(8,128)(2,1)}, u32[]{:S(2)}, u32[]{:S(2)}) collective-permute-start(bf16[128,1536]{1,0:T(8,128)(2,1)} %pad_maximum_fusion.5), channel_id=1, source_target_pairs={{0,32},{16,48},{32,64},{48,80},{64,96},{80,112},{96,0},{112,16},{1... | collective-permute-start | bytes 1179656 | tf_op jit(solution)/shard_map/ppermute | solution.py:180
  202.6 32.3 %collective-permute-start.7 = (bf16[192,2048]{1,0:T(8,128)(2,1)}, bf16[192,2048]{1,0:T(8,128)(2,1)}, u32[]{:S(2)}, u32[]{:S(2)}) collective-permute-start(bf16[192,2048]{1,0:T(8,128)(2,1)} %pad_maximum_fusion.4), channel_id=1, source_target_pairs={{0,96},{16,112},{32,0},{48,16},{64,32},{80,48},{96,64},{112,80},{1... | collective-permute-start | bytes 2359304 | tf_op jit(solution)/shard_map/ppermute | solution.py:181
  209.5 25.4 %collective-permute-start.5 = (bf16[192,2048]{1,0:T(8,128)(2,1)}, bf16[192,2048]{1,0:T(8,128)(2,1)}, u32[]{:S(2)}, u32[]{:S(2)}) collective-permute-start(bf16[192,2048]{1,0:T(8,128)(2,1)} %pad_maximum_fusion.3), channel_id=1, source_target_pairs={{0,32},{16,48},{32,64},{48,80},{64,96},{80,112},{96,0},{112,16},{1... | collective-permute-start | bytes 2359304 | tf_op jit(solution)/shard_map/ppermute | solution.py:180
  212.5 16.7 %collective-permute-start.17 = (bf16[128,1536]{1,0:T(8,128)(2,1)}, bf16[128,1536]{1,0:T(8,128)(2,1)}, u32[]{:S(2)}, u32[]{:S(2)}) collective-permute-start(bf16[128,1536]{1,0:T(8,128)(2,1)} %fusion.22), channel_id=1, source_target_pairs={{0,16},{16,0},{32,48},{48,32},{64,80},{80,64},{96,112},{112,96},{1... | collective-permute-start | bytes 1179656 | tf_op jit(solution)/shard_map/ppermute | solution.py:196
  214.4 36.2 %all-to-all-start.2 = ((bf16[16,32,1536]{2,1,0:T(8,128)(2,1)}), bf16[16,32,1536]{2,1,0:T(8,128)(2,1)}, u32[]{:S(2)}, u32[]{:S(2)}) async-start(bf16[16,32,1536]{2,1,0:T(8,128)(2,1)} %bitcast.199), calls=%async_computation.2 | async-start | bytes 3145728 | tf_op jit(solution)/shard_map/all_to_all | solution.py:367
  227.7 58.3 %collective-permute-start.3 = (bf16[192,2048]{1,0:T(8,128)(2,1)}, bf16[192,2048]{1,0:T(8,128)(2,1)S(1)}, u32[]{:S(2)}, u32[]{:S(2)}) collective-permute-start(bf16[192,2048]{1,0:T(8,128)(2,1)} %pad_maximum_fusion.2), channel_id=1, source_target_pairs={{0,96},{16,112},{32,0},{48,16},{64,32},{80,48},{96,64},{112,80},{1... | collective-permute-start | bytes 2359304 | tf_op jit(solution)/shard_map/ppermute | solution.py:181
  227.8 58.2 %collective-permute-start.1 = (bf16[192,2048]{1,0:T(8,128)(2,1)}, bf16[192,2048]{1,0:T(8,128)(2,1)}, u32[]{:S(2)}, u32[]{:S(2)}) collective-permute-start(bf16[192,2048]{1,0:T(8,128)(2,1)} %pad_maximum_fusion.1), channel_id=1, source_target_pairs={{0,32},{16,48},{32,64},{48,80},{64,96},{80,112},{96,0},{112,16},{1... | collective-permute-start | bytes 2359304 | tf_op jit(solution)/shard_map/ppermute | solution.py:180
  237.8 48.2 %collective-permute-start.8 = (bf16[192,2048]{1,0:T(8,128)(2,1)}, bf16[192,2048]{1,0:T(8,128)(2,1)}, u32[]{:S(2)}, u32[]{:S(2)}) collective-permute-start(bf16[192,2048]{1,0:T(8,128)(2,1)} %fusion.11), channel_id=1, source_target_pairs={{0,16},{16,0},{32,48},{48,32},{64,80},{80,64},{96,112},{112,96},{1... | collective-permute-start | bytes 2359304 | tf_op jit(solution)/shard_map/ppermute | solution.py:196
  239.7 18.3 %copy-start.11 = (s32[4,128]{1,0:T(4,128)S(1)}, s32[4,128]{1,0:T(4,128)}, u32[]{:S(2)}) copy-start(s32[4,128]{1,0:T(4,128)} %eq.41) | copy-start | bytes 6148
  240.8 19.0 %copy-start.8 = (bf16[1536,16]{0,1:T(8,128)(2,1)S(1)}, bf16[1536,16]{0,1:T(8,128)(2,1)}, u32[]{:S(2)}) copy-start(bf16[1536,16]{0,1:T(8,128)(2,1)} %param.10) | copy-start | bytes 147460
  250.6 18.6 %all-to-all-start.3 = ((f32[128,1,192]{2,1,0:T(1,128)}), f32[128,1,192]{2,1,0:T(1,128)S(1)}, u32[]{:S(2)}, u32[]{:S(2)}) async-start(f32[128,1,192]{2,1,0:T(1,128)} %all_to_all.25), calls=%async_computation.3 | async-start | bytes 262144 | tf_op jit(solution)/shard_map/all_to_all | solution.py:405
  259.8 16.7 %copy-start.12 = (f32[4,128]{1,0:T(4,128)S(1)}, f32[4,128]{1,0:T(4,128)}, u32[]{:S(2)}) copy-start(f32[4,128]{1,0:T(4,128)} %mul.88) | copy-start | bytes 6148
  270.1 14.4 %all-to-all-start.4 = ((f32[128,1,192]{2,1,0:T(1,128)}), f32[128,1,192]{2,1,0:T(1,128)S(1)}, u32[]{:S(2)}, u32[]{:S(2)}) async-start(f32[128,1,192]{2,1,0:T(1,128)} %broadcast_in_dim.32), calls=%async_computation.4 | async-start | bytes 262144 | tf_op jit(solution)/shard_map/all_to_all | solution.py:411
  (9 other events, 19.6 us)

commit v5 on v4

--- a/solution.py
+++ b/solution.py
@@ -364,9 +364,6 @@
         jnp.einsum("erh,edh->erd", d_pre_gate, back_gate, preferred_element_type=jnp.float32)
         + jnp.einsum("erh,edh->erd", d_pre_up, back_up, preferred_element_type=jnp.float32)
     ).astype(jnp.bfloat16)
-    row_grads = lax.all_to_all(
-        d_rows.reshape(expert_count_axis, -1, model_width), "expert", 0, 0, tiled=True
-    )
     position_hits = chosen[:, :, :, None] == jnp.arange(block_rows, dtype=jnp.int32)
     indicator_matrix = position_hits.reshape(num_blocks, expert_count * pick_count, block_rows)
     gate_weighted_rows = to_blocks(slot_gate_values, num_blocks, pick_count)[
@@ -390,6 +387,16 @@
         precision=lax.Precision.HIGHEST,
     ).reshape(tok_rows, expert_count)
     d_logit = (dgate * gate_values * (1.0 - gate_values)).astype(jnp.bfloat16)
+    router_full = jnp.dot(tokens.T, d_logit, preferred_element_type=jnp.float32)
+    router_full, d_rows = lax.optimization_barrier((router_full, d_rows))
+    devices = n * expert_count_axis
+    router_part = jnp.sum(
+        lax.all_to_all(router_full.reshape(devices, -1), ("dp", "expert"), 0, 0, tiled=True),
+        axis=0,
+    )
+    row_grads = lax.all_to_all(
+        d_rows.reshape(expert_count_axis, -1, model_width), "expert", 0, 0, tiled=True
+    )
     gathered_grads = jnp.einsum(
         "wze,wzi->wei",
         indicator_matrix.astype(jnp.bfloat16),
@@ -399,12 +406,6 @@
     grad_tokens = (
         gathered_grads + jnp.dot(d_logit, w_router.T, preferred_element_type=jnp.float32)
     ).astype(jnp.bfloat16)
-    router_full = jnp.dot(tokens.T, d_logit, preferred_element_type=jnp.float32)
-    devices = n * expert_count_axis
-    router_part = jnp.sum(
-        lax.all_to_all(router_full.reshape(devices, -1), ("dp", "expert"), 0, 0, tiled=True),
-        axis=0,
-    )
     grad_gate, grad_up, down_weight_gradient = weight_grads(
         expert_rows, hidden, expert_cot, d_pre_gate, d_pre_up, n
     )

time: 293 us -> 309 us (1.055)
  waiting for transfers between devices: 40 us -> 50.8 us
    all_to_all x1, waiting for transfers between devices: 8.67 us -> 18.3 us  [body(): lax.all_to_all(d_rows.reshape(expert_count_axis, -1, model_width), 'exper...]
    all_to_all x1, starting transfers between devices: 7.38 us -> 16.4 us  [body(): lax.all_to_all(router_full.reshape(devices, -1), ('dp', 'expert'), 0, 0,...]
    ppermute x4, waiting for transfers between devices: 8.16 us -> 0.01 us  [x_ring_scatter(): lax.ppermute(to_left.astype(jnp.bfloat16), 'dp', _x_shift(n, -1))]
    all_to_all x1, starting transfers between devices: 13.2 us -> 5.41 us  [body(): lax.all_to_all(d_rows.reshape(expert_count_axis, -1, model_width), 'exper...]
    ppermute x2, waiting for transfers between devices: 0.01 us -> 5.76 us  [dp_scatter_2d(): sent = lax.ppermute(partner_sum.astype(jnp.bfloat16), 'dp', _y_pair(n))]
    all_to_all x1, waiting for transfers between devices: 8.13 us -> 13.6 us  [body(): lax.all_to_all(router_full.reshape(devices, -1), ('dp', 'expert'), 0, 0,...]
  transfers between devices with their start and end apart: 23 -> 23, of which waited for: 8 -> 7; matrix products, arithmetic and copies ran while one was open for 13% -> 13% of each run, Pallas kernels for 39% -> 37%
where the time goes in v5:
time: 309 us; the launch traced here: 306 us
  Pallas kernels  114 us (37%)
  starting transfers between devices  62.9 us (20%)
  waiting for transfers between devices  50.8 us (16%)
  matrix products  33.4 us (11%)
  local copies, waits for them, and re-layouts  22 us (7%)
  other arithmetic  21.8 us (7%)
    pallas_call x1, Pallas kernels, dp_gather_kernel(): pl.pallas_call(functools.partial(_ring_gather_kernel, n), out_shape=[jax....  114 us
    all_to_all x1, waiting for transfers between devices, body(): lax.all_to_all(d_rows.reshape(expert_count_axis, -1, model_width), 'exper...  18.3 us
    all_to_all x1, starting transfers between devices, body(): lax.all_to_all(router_full.reshape(devices, -1), ('dp', 'expert'), 0, 0,...  16.4 us
    all_to_all x1, waiting for transfers between devices, body(): lax.all_to_all(router_full.reshape(devices, -1), ('dp', 'expert'), 0, 0,...  13.6 us
    ppermute x4, waiting for transfers between devices, x_ring_scatter(): low = lax.ppermute(blocks[2][:h].astype(jnp.bfloat16), 'dp', _x_shift(n, 1))  9.31 us
    all_to_all x1, starting transfers between devices, body(): lax.all_to_all(jnp.concatenate([picked, scaled_cot], axis=1), 'expert', 0...  8.63 us
    all_to_all x1, starting transfers between devices, body(): lax.all_to_all(expert_out.reshape(expert_count_axis, -1, model_width), 'e...  8 us
    all_to_all x1, starting transfers between devices, body(): lax.all_to_all(jnp.broadcast_to(router_part[None], (devices,) + router_pa...  6.69 us
  transfers between devices with their start and end apart: 23, of which 7 were waited for; matrix products, arithmetic and copies ran while one was open for 13% of the time, Pallas kernels for 37%

profile of v5, /device:TPU:5, one launch (start us, length us, event | category | flops | bytes accessed | tf_op | source)
XLA Modules:
  0.0 305.8 jit_solution(7375250964502283720)
XLA Ops:
  2.9 4.5 %gather_fusion.2 = f32[512]{0:T(512)S(1)} fusion(f32[16,256]{1,0:T(8,128)S(1)} %bitcast.189, s32[512]{0:T(512)S(1)} %reshape.316), kind=kCustom, calls=%fused_computation.2 | custom fusion | bytes 8192 | tf_op jit(solution)/shard_map/jit(take_along_axis)/gather | solution.py:329
  7.9 2.9 gather_fusion
  10.9 2.1 gather_fusion.1
  14.4 1.9 pad_maximum_fusion
  16.3 8.6 %all-to-all-start = ((bf16[16,64,1536]{2,1,0:T(8,128)(2,1)}), bf16[16,64,1536]{2,1,0:T(8,128)(2,1)}, u32[]{:S(2)}, u32[]{:S(2)}) async-start(bf16[16,64,1536]{2,1,0:T(8,128)(2,1)} %pad_maximum_fusion), calls=%async_computation | async-start | bytes 6291456 | tf_op jit(solution)/shard_map/all_to_all | solution.py:338
  26.8 113.8 %shard_map.118 = (bf16[8,192,1024]{2,1,0:T(8,128)(2,1)}, bf16[8,192,1024]{2,1,0:T(8,128)(2,1)}, bf16[8,128,1536]{2,1,0:T(8,128)(2,1)}) custom-call(bf16[192,1024]{1,0:T(8,128)(2,1)} %bitcast.207, bf16[192,1024]{1,0:T(8,128)(2,1)} %bitcast.208, bf16[128,1536]{1,0:T(8,128)(2,1)} %bitcast.209), custom_call_target="tpu_custom_call" | custom-call | tf_op jit(solution)/shard_map/pallas_call | solution.py:278
  140.7 2.2 fusion.40
  143.5 1.8 fusion.41
  145.4 1.8 fusion.42
  147.3 3.5 %multiply_convert_fusion = (bf16[512,1024]{1,0:T(8,128)(2,1)S(1)}, bf16[512,1024]{1,0:T(8,128)(2,1)}, bf16[512,1024]{1,0:T(8,128)(2,1)S(1)}) fusion(f32[512,1024]{1,0:T(8,128)S(1)} %fusion.41, f32[512,1024]{1,0:T(8,128)S(1)} %fusion.42, bf16[512,1536]{1,0:T(8,128)(2,1)S(1)} %bitcast.205, bf16[1024,1536]{1,0:T(8,128)(2,1)S(1)} %bitcast.216), kind=kOutput, calls=%fused_computation.25 | convolution fusion | flops 1618477056 | bytes 12058624 | tf_op jit(solution)/shard_map/erd,ehd->erh/dot_general | solution.py:357
  150.8 3.0 convolution_convert_fusion.2
  153.8 3.5 %convolution_convert_fusion.1 = bf16[1024,1536]{1,0:T(8,128)(2,1)} fusion(bf16[512,1024]{1,0:T(8,128)(2,1)S(1)} %get-tuple-element.56, bf16[512,1536]{1,0:T(8,128)(2,1)S(1)} %bitcast.206), kind=kOutput, calls=%fused_computation.7 | convolution fusion | flops 1612185600 | bytes 5767168 | tf_op jit(solution)/shard_map/erc,erd->cd/dot_general | solution.py:304
  157.3 8.0 %all-to-all-start.1 = ((bf16[16,32,1536]{2,1,0:T(8,128)(2,1)}), bf16[16,32,1536]{2,1,0:T(8,128)(2,1)}, u32[]{:S(2)}, u32[]{:S(2)}) async-start(bf16[16,32,1536]{2,1,0:T(8,128)(2,1)} %bitcast.201), calls=%async_computation.1 | async-start | bytes 3145728 | tf_op jit(solution)/shard_map/all_to_all | solution.py:352
  165.3 4.2 %fusion.43 = f32[512,1536]{1,0:T(8,128)S(1)} fusion(bf16[512,1024]{1,0:T(8,128)(2,1)} %get-tuple-element.55, bf16[1536,1024]{1,0:T(8,128)(2,1)} %bitcast.214), kind=kOutput, calls=%fused_computation.121 | convolution fusion | flops 1610612736 | bytes 7340032 | tf_op jit(solution)/shard_map/erh,edh->erd/dot_general | solution.py:364
  169.7 2.2 collective-permute-start.9
  173.4 3.1 %fusion.5 = bf16[1,512,1536]{2,1,0:T(8,128)(2,1)} fusion(f32[512,1536]{1,0:T(8,128)S(1)} %fusion.43, bf16[512,1024]{1,0:T(8,128)(2,1)S(1)} %get-tuple-element.54, bf16[1536,1024]{1,0:T(8,128)(2,1)S(1)} %bitcast.213), kind=kOutput, calls=%fused_computation.18 | convolution fusion | flops 1612185600 | bytes 8912896 | tf_op jit(solution)/shard_map/erh,edh->erd/dot_general | solution.py:365
  176.4 3.8 %convolution_convert_fusion = bf16[1536,2048]{1,0:T(8,128)(2,1)S(1)} fusion(bf16[512,1536]{1,0:T(8,128)(2,1)S(1)} %bitcast.204, bf16[1,512,1024]{2,1,0:T(8,128)(2,1)S(1)} %bitcast.218, bf16[1,512,1024]{2,1,0:T(8,128)(2,1)S(1)} %bitcast.219), kind=kOutput, calls=%fused_computation.3 | convolution fusion | flops 3228565504 | bytes 9961472 | tf_op jit(solution)/shard_map/erc,erk->ck/dot_general | solution.py:309
  185.2 2.6 collective-permute-start.16
  191.4 7.9 %collective-permute-done.4 = bf16[96,2048]{1,0:T(8,128)(2,1)S(1)} collective-permute-done((bf16[96,2048]{1,0:T(8,128)(2,1)S(1)}, bf16[96,2048]{1,0:T(8,128)(2,1)S(1)}, u32[]{:S(2)}, u32[]{:S(2)}) %collective-permute-start.4) | collective-permute-done | bytes 393248 | tf_op jit(solution)/shard_map/ppermute | solution.py:176
  207.5 1.9 fusion.1
  211.7 16.4 %all-to-all-start.3 = ((f32[128,1,192]{2,1,0:T(1,128)}), f32[128,1,192]{2,1,0:T(1,128)S(1)}, u32[]{:S(2)}, u32[]{:S(2)}) async-start(f32[128,1,192]{2,1,0:T(1,128)} %all_to_all.25), calls=%async_computation.3 | async-start | bytes 262144 | tf_op jit(solution)/shard_map/all_to_all | solution.py:394
  229.6 2.1 fusion.23
  231.8 13.6 %all-to-all-done.3 = f32[128,1,192]{2,1,0:T(1,128)S(1)} async-done(((f32[128,1,192]{2,1,0:T(1,128)}), f32[128,1,192]{2,1,0:T(1,128)S(1)}, u32[]{:S(2)}, u32[]{:S(2)}) %all-to-all-start.3) | async-done | bytes 98336 | tf_op jit(solution)/shard_map/all_to_all | solution.py:394
  246.2 6.7 %all-to-all-start.4 = ((f32[128,1,192]{2,1,0:T(1,128)}), f32[128,1,192]{2,1,0:T(1,128)S(1)}, u32[]{:S(2)}, u32[]{:S(2)}) async-start(f32[128,1,192]{2,1,0:T(1,128)} %broadcast_in_dim.32), calls=%async_computation.4 | async-start | bytes 262144 | tf_op jit(solution)/shard_map/all_to_all | solution.py:412
  255.1 2.9 fusion.12
  258.3 3.2 %all-to-all-done.4 = f32[128,1,192]{2,1,0:T(1,128)S(1)} async-done(((f32[128,1,192]{2,1,0:T(1,128)}), f32[128,1,192]{2,1,0:T(1,128)S(1)}, u32[]{:S(2)}, u32[]{:S(2)}) %all-to-all-start.4) | async-done | bytes 98336 | tf_op jit(solution)/shard_map/all_to_all | solution.py:412
  261.4 5.4 %all-to-all-start.2 = ((bf16[16,32,1536]{2,1,0:T(8,128)(2,1)}), bf16[16,32,1536]{2,1,0:T(8,128)(2,1)}, u32[]{:S(2)}, u32[]{:S(2)}) async-start(bf16[16,32,1536]{2,1,0:T(8,128)(2,1)} %bitcast.29), calls=%async_computation.2 | async-start | bytes 3145728 | tf_op jit(solution)/shard_map/all_to_all | solution.py:397
  266.8 2.2 fusion.26
  269.0 4.0 %fusion.6 = bf16[4,64,1536]{2,1,0:T(8,128)(2,1)} fusion(f32[4,128]{1,0:T(4,128)S(1)} %copy-done.11, s32[4,128]{1,0:T(4,128)S(1)} %copy-done.10, bf16[16,32,1536]{2,1,0:T(8,128)(2,1)} %all-to-all-done.1), kind=kOutput, calls=%fused_computation.19 | convolution fusion | flops 605978624 | bytes 2363392 | tf_op jit(solution)/shard_map/wze,wzi->wei/dot_general | solution.py:373
  275.3 5.8 %collective-permute-done.8 = bf16[192,2048]{1,0:T(8,128)(2,1)} collective-permute-done((bf16[192,2048]{1,0:T(8,128)(2,1)}, bf16[192,2048]{1,0:T(8,128)(2,1)}, u32[]{:S(2)}, u32[]{:S(2)}) %collective-permute-start.8) | collective-permute-done | bytes 786464 | tf_op jit(solution)/shard_map/ppermute | solution.py:196
  281.1 2.1 fusion.14
  284.4 18.3 %all-to-all-done.2 = bf16[16,32,1536]{2,1,0:T(8,128)(2,1)} async-done(((bf16[16,32,1536]{2,1,0:T(8,128)(2,1)}), bf16[16,32,1536]{2,1,0:T(8,128)(2,1)}, u32[]{:S(2)}, u32[]{:S(2)}) %all-to-all-start.2) | async-done | bytes 1572896 | tf_op jit(solution)/shard_map/all_to_all | solution.py:397
  (117 shorter events, 38.7 us)
Async XLA Ops:
  2.9 4.7 %copy-start.8 = (s32[4,16,8]{1,2,0:T(8,128)S(1)}, s32[4,16,8]{1,2,0:T(8,128)}, u32[]{:S(2)}) copy-start(s32[4,16,8]{1,2,0:T(8,128)} %param.9) | copy-start | bytes 6148
  16.3 124.3 %all-to-all-start = ((bf16[16,64,1536]{2,1,0:T(8,128)(2,1)}), bf16[16,64,1536]{2,1,0:T(8,128)(2,1)}, u32[]{:S(2)}, u32[]{:S(2)}) async-start(bf16[16,64,1536]{2,1,0:T(8,128)(2,1)} %pad_maximum_fusion), calls=%async_computation | async-start | bytes 6291456 | tf_op jit(solution)/shard_map/all_to_all | solution.py:338
  157.3 50.2 %all-to-all-start.1 = ((bf16[16,32,1536]{2,1,0:T(8,128)(2,1)}), bf16[16,32,1536]{2,1,0:T(8,128)(2,1)}, u32[]{:S(2)}, u32[]{:S(2)}) async-start(bf16[16,32,1536]{2,1,0:T(8,128)(2,1)} %bitcast.201), calls=%async_computation.1 | async-start | bytes 3145728 | tf_op jit(solution)/shard_map/all_to_all | solution.py:352
  165.3 4.2 %copy-start.4 = (bf16[1024,1536]{1,0:T(8,128)(2,1)S(1)}, bf16[1024,1536]{1,0:T(8,128)(2,1)}, u32[]{:S(2)}) copy-start(bf16[1024,1536]{1,0:T(8,128)(2,1)} %convolution_convert_fusion.1) | copy-start | bytes 9437188
  169.5 3.8 %copy-start.13 = (bf16[8,192,1024]{2,1,0:T(8,128)(2,1)S(1)}, bf16[8,192,1024]{2,1,0:T(8,128)(2,1)}, u32[]{:S(2)}) copy-start(bf16[8,192,1024]{2,1,0:T(8,128)(2,1)} %get-tuple-element.12) | copy-start | bytes 9437188
  169.7 12.4 %collective-permute-start.9 = (bf16[64,1536]{1,0:T(8,128)(2,1)S(1)}, bf16[64,1536]{1,0:T(8,128)(2,1)S(1)}, u32[]{:S(2)}, u32[]{:S(2)}) collective-permute-start(bf16[64,1536]{1,0:T(8,128)(2,1)S(1)} %get-tuple-element.61), channel_id=1, source_target_pairs={{0,32},{16,48},{32,64},{48,80},{64,96},{80,112},{96,0},{112,16},{1... | collective-permute-start | bytes 589832 | tf_op jit(solution)/shard_map/ppermute | solution.py:176
  171.9 12.0 %collective-permute-start.13 = (bf16[64,1536]{1,0:T(8,128)(2,1)S(1)}, bf16[64,1536]{1,0:T(8,128)(2,1)S(1)}, u32[]{:S(2)}, u32[]{:S(2)}) collective-permute-start(bf16[64,1536]{1,0:T(8,128)(2,1)S(1)} %get-tuple-element.63), channel_id=1, source_target_pairs={{0,32},{16,48},{32,64},{48,80},{64,96},{80,112},{96,0},{112,16},{1... | collective-permute-start | bytes 589832 | tf_op jit(solution)/shard_map/ppermute | solution.py:176
  172.4 11.4 %collective-permute-start.15 = (bf16[64,1536]{1,0:T(8,128)(2,1)S(1)}, bf16[64,1536]{1,0:T(8,128)(2,1)S(1)}, u32[]{:S(2)}, u32[]{:S(2)}) collective-permute-start(bf16[64,1536]{1,0:T(8,128)(2,1)S(1)} %get-tuple-element.65), channel_id=1, source_target_pairs={{0,96},{16,112},{32,0},{48,16},{64,32},{80,48},{96,64},{112,80},{1... | collective-permute-start | bytes 589832 | tf_op jit(solution)/shard_map/ppermute | solution.py:177
  173.3 10.9 %collective-permute-start.11 = (bf16[64,1536]{1,0:T(8,128)(2,1)S(1)}, bf16[64,1536]{1,0:T(8,128)(2,1)S(1)}, u32[]{:S(2)}, u32[]{:S(2)}) collective-permute-start(bf16[64,1536]{1,0:T(8,128)(2,1)S(1)} %get-tuple-element.67), channel_id=1, source_target_pairs={{0,96},{16,112},{32,0},{48,16},{64,32},{80,48},{96,64},{112,80},{1... | collective-permute-start | bytes 589832 | tf_op jit(solution)/shard_map/ppermute | solution.py:177
  173.4 3.1 %copy-start.6 = (bf16[16,32,1536]{2,1,0:T(8,128)(2,1)S(1)}, bf16[16,32,1536]{2,1,0:T(8,128)(2,1)}, u32[]{:S(2)}) copy-start(bf16[16,32,1536]{2,1,0:T(8,128)(2,1)} %copy-done.5) | copy-start | bytes 4718596
  173.4 3.1 %copy-start.16 = (bf16[512,1024]{1,0:T(8,128)(2,1)S(1)}, bf16[512,1024]{1,0:T(8,128)(2,1)}, u32[]{:S(2)}) copy-start(bf16[512,1024]{1,0:T(8,128)(2,1)} %get-tuple-element.55) | copy-start | bytes 3145732
  180.3 20.8 %copy-start.3 = (bf16[1536,2048]{1,0:T(8,128)(2,1)}, bf16[1536,2048]{1,0:T(8,128)(2,1)S(1)}, u32[]{:S(2)}) copy-start(bf16[1536,2048]{1,0:T(8,128)(2,1)S(1)} %convolution_convert_fusion) | copy-start | bytes 18874372
  180.6 10.3 %collective-permute-start = (bf16[96,2048]{1,0:T(8,128)(2,1)S(1)}, bf16[96,2048]{1,0:T(8,128)(2,1)S(1)}, u32[]{:S(2)}, u32[]{:S(2)}) collective-permute-start(bf16[96,2048]{1,0:T(8,128)(2,1)S(1)} %get-tuple-element.46), channel_id=1, source_target_pairs={{0,32},{16,48},{32,64},{48,80},{64,96},{80,112},{96,0},{112,16},{1... | collective-permute-start | bytes 1179656 | tf_op jit(solution)/shard_map/ppermute | solution.py:176
  182.1 17.2 %collective-permute-start.4 = (bf16[96,2048]{1,0:T(8,128)(2,1)S(1)}, bf16[96,2048]{1,0:T(8,128)(2,1)S(1)}, u32[]{:S(2)}, u32[]{:S(2)}) collective-permute-start(bf16[96,2048]{1,0:T(8,128)(2,1)S(1)} %get-tuple-element.48), channel_id=1, source_target_pairs={{0,32},{16,48},{32,64},{48,80},{64,96},{80,112},{96,0},{112,16},{1... | collective-permute-start | bytes 1179656 | tf_op jit(solution)/shard_map/ppermute | solution.py:176
  183.8 16.6 %collective-permute-start.6 = (bf16[96,2048]{1,0:T(8,128)(2,1)S(1)}, bf16[96,2048]{1,0:T(8,128)(2,1)S(1)}, u32[]{:S(2)}, u32[]{:S(2)}) collective-permute-start(bf16[96,2048]{1,0:T(8,128)(2,1)S(1)} %get-tuple-element.50), channel_id=1, source_target_pairs={{0,96},{16,112},{32,0},{48,16},{64,32},{80,48},{96,64},{112,80},{1... | collective-permute-start | bytes 1179656 | tf_op jit(solution)/shard_map/ppermute | solution.py:177
  183.9 17.2 %collective-permute-start.2 = (bf16[96,2048]{1,0:T(8,128)(2,1)S(1)}, bf16[96,2048]{1,0:T(8,128)(2,1)S(1)}, u32[]{:S(2)}, u32[]{:S(2)}) collective-permute-start(bf16[96,2048]{1,0:T(8,128)(2,1)S(1)} %get-tuple-element.52), channel_id=1, source_target_pairs={{0,96},{16,112},{32,0},{48,16},{64,32},{80,48},{96,64},{112,80},{1... | collective-permute-start | bytes 1179656 | tf_op jit(solution)/shard_map/ppermute | solution.py:177
  185.2 42.9 %collective-permute-start.16 = (bf16[128,1536]{1,0:T(8,128)(2,1)}, bf16[128,1536]{1,0:T(8,128)(2,1)}, u32[]{:S(2)}, u32[]{:S(2)}) collective-permute-start(bf16[128,1536]{1,0:T(8,128)(2,1)} %pad_maximum_fusion.8), channel_id=1, source_target_pairs={{0,96},{16,112},{32,0},{48,16},{64,32},{80,48},{96,64},{112,80},{1... | collective-permute-start | bytes 1179656 | tf_op jit(solution)/shard_map/ppermute | solution.py:181
  190.8 38.2 %collective-permute-start.14 = (bf16[128,1536]{1,0:T(8,128)(2,1)S(1)}, bf16[128,1536]{1,0:T(8,128)(2,1)}, u32[]{:S(2)}, u32[]{:S(2)}) collective-permute-start(bf16[128,1536]{1,0:T(8,128)(2,1)S(1)} %pad_maximum_fusion.7), channel_id=1, source_target_pairs={{0,32},{16,48},{32,64},{48,80},{64,96},{80,112},{96,0},{112,16},{1... | collective-permute-start | bytes 1179656 | tf_op jit(solution)/shard_map/ppermute | solution.py:180
  199.3 58.7 %collective-permute-start.12 = (bf16[128,1536]{1,0:T(8,128)(2,1)}, bf16[128,1536]{1,0:T(8,128)(2,1)S(1)}, u32[]{:S(2)}, u32[]{:S(2)}) collective-permute-start(bf16[128,1536]{1,0:T(8,128)(2,1)} %pad_maximum_fusion.6), channel_id=1, source_target_pairs={{0,96},{16,112},{32,0},{48,16},{64,32},{80,48},{96,64},{112,80},{1... | collective-permute-start | bytes 1179656 | tf_op jit(solution)/shard_map/ppermute | solution.py:181
  202.6 50.4 %collective-permute-start.7 = (bf16[192,2048]{1,0:T(8,128)(2,1)}, bf16[192,2048]{1,0:T(8,128)(2,1)}, u32[]{:S(2)}, u32[]{:S(2)}) collective-permute-start(bf16[192,2048]{1,0:T(8,128)(2,1)} %pad_maximum_fusion.4), channel_id=1, source_target_pairs={{0,96},{16,112},{32,0},{48,16},{64,32},{80,48},{96,64},{112,80},{1... | collective-permute-start | bytes 2359304 | tf_op jit(solution)/shard_map/ppermute | solution.py:181
  204.7 49.2 %collective-permute-start.5 = (bf16[192,2048]{1,0:T(8,128)(2,1)}, bf16[192,2048]{1,0:T(8,128)(2,1)}, u32[]{:S(2)}, u32[]{:S(2)}) collective-permute-start(bf16[192,2048]{1,0:T(8,128)(2,1)} %pad_maximum_fusion.3), channel_id=1, source_target_pairs={{0,32},{16,48},{32,64},{48,80},{64,96},{80,112},{96,0},{112,16},{1... | collective-permute-start | bytes 2359304 | tf_op jit(solution)/shard_map/ppermute | solution.py:180
  211.7 33.7 %all-to-all-start.3 = ((f32[128,1,192]{2,1,0:T(1,128)}), f32[128,1,192]{2,1,0:T(1,128)S(1)}, u32[]{:S(2)}, u32[]{:S(2)}) async-start(f32[128,1,192]{2,1,0:T(1,128)} %all_to_all.25), calls=%async_computation.3 | async-start | bytes 262144 | tf_op jit(solution)/shard_map/all_to_all | solution.py:394
  228.1 38.7 %collective-permute-start.10 = (bf16[128,1536]{1,0:T(8,128)(2,1)}, bf16[128,1536]{1,0:T(8,128)(2,1)S(1)}, u32[]{:S(2)}, u32[]{:S(2)}) collective-permute-start(bf16[128,1536]{1,0:T(8,128)(2,1)} %pad_maximum_fusion.5), channel_id=1, source_target_pairs={{0,32},{16,48},{32,64},{48,80},{64,96},{80,112},{96,0},{112,16},{1... | collective-permute-start | bytes 1179656 | tf_op jit(solution)/shard_map/ppermute | solution.py:180
  229.1 45.4 %collective-permute-start.3 = (bf16[192,2048]{1,0:T(8,128)(2,1)}, bf16[192,2048]{1,0:T(8,128)(2,1)S(1)}, u32[]{:S(2)}, u32[]{:S(2)}) collective-permute-start(bf16[192,2048]{1,0:T(8,128)(2,1)} %pad_maximum_fusion.2), channel_id=1, source_target_pairs={{0,96},{16,112},{32,0},{48,16},{64,32},{80,48},{96,64},{112,80},{1... | collective-permute-start | bytes 2359304 | tf_op jit(solution)/shard_map/ppermute | solution.py:181
  246.2 15.2 %all-to-all-start.4 = ((f32[128,1,192]{2,1,0:T(1,128)}), f32[128,1,192]{2,1,0:T(1,128)S(1)}, u32[]{:S(2)}, u32[]{:S(2)}) async-start(f32[128,1,192]{2,1,0:T(1,128)} %broadcast_in_dim.32), calls=%async_computation.4 | async-start | bytes 262144 | tf_op jit(solution)/shard_map/all_to_all | solution.py:412
  252.9 21.5 %collective-permute-start.1 = (bf16[192,2048]{1,0:T(8,128)(2,1)}, bf16[192,2048]{1,0:T(8,128)(2,1)S(1)}, u32[]{:S(2)}, u32[]{:S(2)}) collective-permute-start(bf16[192,2048]{1,0:T(8,128)(2,1)} %pad_maximum_fusion.1), channel_id=1, source_target_pairs={{0,32},{16,48},{32,64},{48,80},{64,96},{80,112},{96,0},{112,16},{1... | collective-permute-start | bytes 2359304 | tf_op jit(solution)/shard_map/ppermute | solution.py:180
  253.9 12.9 %collective-permute-start.17 = (bf16[128,1536]{1,0:T(8,128)(2,1)}, bf16[128,1536]{1,0:T(8,128)(2,1)}, u32[]{:S(2)}, u32[]{:S(2)}) collective-permute-start(bf16[128,1536]{1,0:T(8,128)(2,1)} %fusion.23), channel_id=1, source_target_pairs={{0,16},{16,0},{32,48},{48,32},{64,80},{80,64},{96,112},{112,96},{1... | collective-permute-start | bytes 1179656 | tf_op jit(solution)/shard_map/ppermute | solution.py:196
  258.0 23.1 %collective-permute-start.8 = (bf16[192,2048]{1,0:T(8,128)(2,1)}, bf16[192,2048]{1,0:T(8,128)(2,1)}, u32[]{:S(2)}, u32[]{:S(2)}) collective-permute-start(bf16[192,2048]{1,0:T(8,128)(2,1)} %fusion.12), channel_id=1, source_target_pairs={{0,16},{16,0},{32,48},{48,32},{64,80},{80,64},{96,112},{112,96},{1... | collective-permute-start | bytes 2359304 | tf_op jit(solution)/shard_map/ppermute | solution.py:196
  261.4 7.6 %copy-start.10 = (s32[4,128]{1,0:T(4,128)S(1)}, s32[4,128]{1,0:T(4,128)}, u32[]{:S(2)}) copy-start(s32[4,128]{1,0:T(4,128)} %eq.41) | copy-start | bytes 6148
  261.4 7.6 %copy-start.11 = (f32[4,128]{1,0:T(4,128)S(1)}, f32[4,128]{1,0:T(4,128)}, u32[]{:S(2)}) copy-start(f32[4,128]{1,0:T(4,128)} %mul.88) | copy-start | bytes 6148
  261.4 41.4 %all-to-all-start.2 = ((bf16[16,32,1536]{2,1,0:T(8,128)(2,1)}), bf16[16,32,1536]{2,1,0:T(8,128)(2,1)}, u32[]{:S(2)}, u32[]{:S(2)}) async-start(bf16[16,32,1536]{2,1,0:T(8,128)(2,1)} %bitcast.29), calls=%async_computation.2 | async-start | bytes 3145728 | tf_op jit(solution)/shard_map/all_to_all | solution.py:397
  284.4 20.1 %copy-start.9 = (bf16[1536,16]{0,1:T(8,128)(2,1)S(1)}, bf16[1536,16]{0,1:T(8,128)(2,1)}, u32[]{:S(2)}) copy-start(bf16[1536,16]{0,1:T(8,128)(2,1)} %param.10) | copy-start | bytes 147460
  (8 other events, 15.4 us)

commit v6 on v4

--- a/solution.py
+++ b/solution.py
@@ -355,6 +355,22 @@
     expert_cot = dispatched[:, slot_width:].reshape(1, -1, model_width)
     back_gate, back_up, back_down = (full_gate, full_up, full_down)
     d_hidden = jnp.einsum("erd,ehd->erh", expert_cot, back_down, preferred_element_type=jnp.float32)
+    position_hits = chosen[:, :, :, None] == jnp.arange(block_rows, dtype=jnp.int32)
+    slot_dots = jnp.sum(cot_rows.astype(jnp.float32) * returned.astype(jnp.float32), axis=2)
+    dgate = jnp.einsum(
+        "bept,ebp->bte",
+        position_hits.astype(jnp.float32),
+        slot_dots.reshape(expert_count, num_blocks, pick_count),
+        precision=lax.Precision.HIGHEST,
+    ).reshape(tok_rows, expert_count)
+    d_logit = (dgate * gate_values * (1.0 - gate_values)).astype(jnp.bfloat16)
+    router_full = jnp.dot(tokens.T, d_logit, preferred_element_type=jnp.float32)
+    devices = n * expert_count_axis
+    router_part = jnp.sum(
+        lax.all_to_all(router_full.reshape(devices, -1), ("dp", "expert"), 0, 0, tiled=True),
+        axis=0,
+    )
+    router_full, d_hidden = lax.optimization_barrier((router_full, d_hidden))
     gate_sigmoid = jax.nn.sigmoid(pre_gate)
     d_pre_gate = (
         d_hidden * pre_up * gate_sigmoid * (1.0 + pre_gate * (1.0 - gate_sigmoid))
@@ -367,7 +383,6 @@
     row_grads = lax.all_to_all(
         d_rows.reshape(expert_count_axis, -1, model_width), "expert", 0, 0, tiled=True
     )
-    position_hits = chosen[:, :, :, None] == jnp.arange(block_rows, dtype=jnp.int32)
     indicator_matrix = position_hits.reshape(num_blocks, expert_count * pick_count, block_rows)
     gate_weighted_rows = to_blocks(slot_gate_values, num_blocks, pick_count)[
         :, :, None
@@ -382,14 +397,6 @@
         .reshape(tok_rows, model_width)
         .astype(jnp.bfloat16)
     )
-    slot_dots = jnp.sum(cot_rows.astype(jnp.float32) * returned.astype(jnp.float32), axis=2)
-    dgate = jnp.einsum(
-        "bept,ebp->bte",
-        position_hits.astype(jnp.float32),
-        slot_dots.reshape(expert_count, num_blocks, pick_count),
-        precision=lax.Precision.HIGHEST,
-    ).reshape(tok_rows, expert_count)
-    d_logit = (dgate * gate_values * (1.0 - gate_values)).astype(jnp.bfloat16)
     gathered_grads = jnp.einsum(
         "wze,wzi->wei",
         indicator_matrix.astype(jnp.bfloat16),
@@ -399,12 +406,6 @@
     grad_tokens = (
         gathered_grads + jnp.dot(d_logit, w_router.T, preferred_element_type=jnp.float32)
     ).astype(jnp.bfloat16)
-    router_full = jnp.dot(tokens.T, d_logit, preferred_element_type=jnp.float32)
-    devices = n * expert_count_axis
-    router_part = jnp.sum(
-        lax.all_to_all(router_full.reshape(devices, -1), ("dp", "expert"), 0, 0, tiled=True),
-        axis=0,
-    )
     grad_gate, grad_up, down_weight_gradient = weight_grads(
         expert_rows, hidden, expert_cot, d_pre_gate, d_pre_up, n
     )

time: 293 us -> 304 us (1.038)
  other arithmetic: 19.3 us -> 28.6 us
  local copies, waits for them, and re-layouts: 21.1 us -> 24.8 us
    ppermute x4, waiting for transfers between devices: 10.7 us -> 0.01 us  [x_ring_scatter(): low = lax.ppermute(blocks[2][:h].astype(jnp.bfloat16), 'dp', _x_shift(n, 1))]
    ppermute x4, waiting for transfers between devices: 0.01 us -> 8.7 us  [x_ring_scatter(): lax.ppermute(to_right.astype(jnp.bfloat16), 'dp', _x_shift(n, 1))]
    ppermute x2, waiting for transfers between devices: 0.01 us -> 7.51 us  [dp_scatter_2d(): sent = lax.ppermute(partner_sum.astype(jnp.bfloat16), 'dp', _y_pair(n))]
    all_to_all x1, waiting for transfers between devices: 0.01 us -> 6.57 us  [body(): lax.all_to_all(expert_out.reshape(expert_count_axis, -1, model_width), 'e...]
    all_to_all x1, waiting for transfers between devices: 8.67 us -> 2.18 us  [body(): lax.all_to_all(d_rows.reshape(expert_count_axis, -1, model_width), 'exper...]
    all_to_all x1, starting transfers between devices: 13.2 us -> 8.41 us  [body(): lax.all_to_all(d_rows.reshape(expert_count_axis, -1, model_width), 'exper...]
    convert_element_type x0 -> x1, other arithmetic: none -> 4.21 us  [body(): d_pre_up = (d_hidden * silu_gate).astype(jnp.bfloat16)]
    all_to_all x1, waiting for transfers between devices: 4.01 us -> 0.07 us  [body(): lax.all_to_all(jnp.broadcast_to(router_part[None], (devices,) + router_pa...]
  transfers between devices with their start and end apart: 23 -> 23, of which waited for: 8 -> 10; matrix products, arithmetic and copies ran while one was open for 13% -> 17% of each run, Pallas kernels for 39% -> 38%
where the time goes in v6:
time: 304 us; the launch traced here: 302 us
  Pallas kernels  114 us (38%)
  starting transfers between devices  60.6 us (20%)
  waiting for transfers between devices  39.1 us (13%)
  matrix products  33.5 us (11%)
  other arithmetic  28.6 us (9%)
  local copies, waits for them, and re-layouts  24.8 us (8%)
    pallas_call x1, Pallas kernels, dp_gather_kernel(): pl.pallas_call(functools.partial(_ring_gather_kernel, n), out_shape=[jax....  114 us
    all_to_all x1, starting transfers between devices, body(): lax.all_to_all(expert_out.reshape(expert_count_axis, -1, model_width), 'e...  8.83 us
    all_to_all x1, starting transfers between devices, body(): lax.all_to_all(jnp.broadcast_to(router_part[None], (devices,) + router_pa...  8.77 us
    ppermute x4, waiting for transfers between devices, x_ring_scatter(): lax.ppermute(to_right.astype(jnp.bfloat16), 'dp', _x_shift(n, 1))  8.7 us
    all_to_all x1, starting transfers between devices, body(): lax.all_to_all(jnp.concatenate([picked, scaled_cot], axis=1), 'expert', 0...  8.64 us
    all_to_all x1, starting transfers between devices, body(): lax.all_to_all(d_rows.reshape(expert_count_axis, -1, model_width), 'exper...  8.41 us
    all_to_all x1, starting transfers between devices, body(): lax.all_to_all(router_full.reshape(devices, -1), ('dp', 'expert'), 0, 0,...  8.3 us
    ppermute x2, waiting for transfers between devices, dp_scatter_2d(): sent = lax.ppermute(partner_sum.astype(jnp.bfloat16), 'dp', _y_pair(n))  7.51 us
  transfers between devices with their start and end apart: 23, of which 10 were waited for; matrix products, arithmetic and copies ran while one was open for 17% of the time, Pallas kernels for 38%

profile of v6, /device:TPU:5, one launch (start us, length us, event | category | flops | bytes accessed | tf_op | source)
XLA Modules:
  0.0 301.5 jit_solution(11347754870953557449)
XLA Ops:
  2.9 4.5 %gather_fusion.2 = f32[512]{0:T(512)S(1)} fusion(f32[16,256]{1,0:T(8,128)S(1)} %bitcast.207, s32[512]{0:T(512)S(1)} %reshape.315), kind=kCustom, calls=%fused_computation.2 | custom fusion | bytes 8192 | tf_op jit(solution)/shard_map/jit(take_along_axis)/gather | solution.py:329
  7.9 2.9 gather_fusion
  10.9 2.1 gather_fusion.1
  16.3 8.6 %all-to-all-start = ((bf16[16,64,1536]{2,1,0:T(8,128)(2,1)}), bf16[16,64,1536]{2,1,0:T(8,128)(2,1)}, u32[]{:S(2)}, u32[]{:S(2)}) async-start(bf16[16,64,1536]{2,1,0:T(8,128)(2,1)} %pad_maximum_fusion), calls=%async_computation | async-start | bytes 6291456 | tf_op jit(solution)/shard_map/all_to_all | solution.py:338
  26.8 113.8 %shard_map.118 = (bf16[8,192,1024]{2,1,0:T(8,128)(2,1)}, bf16[8,192,1024]{2,1,0:T(8,128)(2,1)}, bf16[8,128,1536]{2,1,0:T(8,128)(2,1)}) custom-call(bf16[192,1024]{1,0:T(8,128)(2,1)} %bitcast.226, bf16[192,1024]{1,0:T(8,128)(2,1)} %bitcast.227, bf16[128,1536]{1,0:T(8,128)(2,1)} %bitcast.228), custom_call_target="tpu_custom_call" | custom-call | tf_op jit(solution)/shard_map/pallas_call | solution.py:278
  140.6 2.2 fusion.44
  145.3 3.2 %multiply_convert_fusion = (bf16[512,1024]{1,0:T(8,128)(2,1)S(1)}, f32[512,1024]{1,0:T(8,128)}) fusion(f32[512,1024]{1,0:T(8,128)S(1)} %fusion.45, bf16[512,1536]{1,0:T(8,128)(2,1)S(1)} %bitcast.222, bf16[1536,1024]{1,0:T(8,128)(2,1)S(1)} %bitcast.232), kind=kOutput, calls=%fused_computation.30 | convolution fusion | flops 1613758464 | bytes 9961472 | tf_op jit(solution)/shard_map/erd,edh->erh/dot_general | solution.py:346
  148.6 3.2 %convolution_bitcast_fusion.1 = f32[1,512,1024]{2,1,0:T(8,128)} fusion(bf16[512,1536]{1,0:T(8,128)(2,1)S(1)} %bitcast.224, bf16[1024,1536]{1,0:T(8,128)(2,1)S(1)} %bitcast.235), kind=kOutput, calls=%fused_computation.33 | convolution fusion | flops 1610612736 | bytes 6815744 | tf_op jit(solution)/shard_map/erd,ehd->erh/dot_general | solution.py:357
  154.6 2.1 collective-permute-start.9
  158.2 3.0 convolution_convert_fusion.2
  161.2 8.8 %all-to-all-start.1 = ((bf16[16,32,1536]{2,1,0:T(8,128)(2,1)}), bf16[16,32,1536]{2,1,0:T(8,128)(2,1)}, u32[]{:S(2)}, u32[]{:S(2)}) async-start(bf16[16,32,1536]{2,1,0:T(8,128)(2,1)} %bitcast.220), calls=%async_computation.1 | async-start | bytes 3145728 | tf_op jit(solution)/shard_map/all_to_all | solution.py:352
  171.7 2.4 collective-permute-start.16
  177.2 5.8 %collective-permute-done.16 = bf16[128,1536]{1,0:T(8,128)(2,1)S(1)} collective-permute-done((bf16[128,1536]{1,0:T(8,128)(2,1)S(1)}, bf16[128,1536]{1,0:T(8,128)(2,1)S(1)}, u32[]{:S(2)}, u32[]{:S(2)}) %collective-permute-start.16) | collective-permute-done | bytes 393248 | tf_op jit(solution)/shard_map/ppermute | solution.py:181
  186.4 6.6 %all-to-all-done.1 = bf16[16,32,1536]{2,1,0:T(8,128)(2,1)} async-done(((bf16[16,32,1536]{2,1,0:T(8,128)(2,1)}), bf16[16,32,1536]{2,1,0:T(8,128)(2,1)}, u32[]{:S(2)}, u32[]{:S(2)}) %all-to-all-start.1) | async-done | bytes 1572896 | tf_op jit(solution)/shard_map/all_to_all | solution.py:352
  193.0 1.9 fusion.1
  196.1 4.2 %fusion.9 = (bf16[1,512,1024]{2,1,0:T(8,128)(2,1)S(1)}, bf16[1,512,1024]{2,1,0:T(8,128)(2,1)S(1)}) fusion(f32[1,512,1024]{2,1,0:T(8,128)} %convolution_bitcast_fusion.1, f32[512,1024]{1,0:T(8,128)} %copy-done.6, f32[512,1024]{1,0:T(8,128)} %get-tuple-element.71), kind=kLoop, calls=%fused_computation.25 | loop fusion | flops 6815744 | bytes 8388608 | tf_op jit(solution)/shard_map/convert_element_type | solution.py:378
  200.3 3.5 %fusion.24 = f32[512,1536]{1,0:T(8,128)} fusion(bf16[1536,1024]{1,0:T(8,128)(2,1)S(1)} %bitcast.234, bf16[1,512,1024]{2,1,0:T(8,128)(2,1)S(1)} %get-tuple-element.53), kind=kOutput, calls=%fused_computation.49 | convolution fusion | flops 1610612736 | bytes 7340032 | tf_op jit(solution)/shard_map/erh,edh->erd/dot_general | solution.py:380
  203.8 3.8 %convolution_convert_fusion = bf16[1536,2048]{1,0:T(8,128)(2,1)S(1)} fusion(bf16[512,1536]{1,0:T(8,128)(2,1)S(1)} %bitcast.223, bf16[1,512,1024]{2,1,0:T(8,128)(2,1)S(1)} %get-tuple-element.52, bf16[1,512,1024]{2,1,0:T(8,128)(2,1)S(1)} %get-tuple-element.53), kind=kOutput, calls=%fused_computation.3 | convolution fusion | flops 3228565504 | bytes 9961472 | tf_op jit(solution)/shard_map/erc,erk->ck/dot_general | solution.py:309
  215.7 8.3 %all-to-all-start.3 = ((f32[128,1,192]{2,1,0:T(1,128)}), f32[128,1,192]{2,1,0:T(1,128)S(1)}, u32[]{:S(2)}, u32[]{:S(2)}) async-start(f32[128,1,192]{2,1,0:T(1,128)} %all_to_all.25), calls=%async_computation.3 | async-start | bytes 262144 | tf_op jit(solution)/shard_map/all_to_all | solution.py:370
  224.0 5.8 %fusion.4 = bf16[512,1536]{1,0:T(8,128)(2,1)} fusion(f32[512,1536]{1,0:T(8,128)} %fusion.24, bf16[1536,1024]{1,0:T(8,128)(2,1)} %bitcast.231, bf16[1,512,1024]{2,1,0:T(8,128)(2,1)S(1)} %get-tuple-element.52), kind=kOutput, calls=%fused_computation.15 | convolution fusion | flops 1612185600 | bytes 8912896 | tf_op jit(solution)/shard_map/erh,edh->erd/dot_general | solution.py:381
  229.8 6.7 %all-to-all-done.3 = f32[128,1,192]{2,1,0:T(1,128)S(1)} async-done(((f32[128,1,192]{2,1,0:T(1,128)}), f32[128,1,192]{2,1,0:T(1,128)S(1)}, u32[]{:S(2)}, u32[]{:S(2)}) %all-to-all-start.3) | async-done | bytes 98336 | tf_op jit(solution)/shard_map/all_to_all | solution.py:370
  237.4 8.8 %all-to-all-start.4 = ((f32[128,1,192]{2,1,0:T(1,128)}), f32[128,1,192]{2,1,0:T(1,128)S(1)}, u32[]{:S(2)}, u32[]{:S(2)}) async-start(f32[128,1,192]{2,1,0:T(1,128)} %broadcast_in_dim.32), calls=%async_computation.4 | async-start | bytes 262144 | tf_op jit(solution)/shard_map/all_to_all | solution.py:412
  248.3 2.4 fusion.34
  254.2 8.4 %all-to-all-start.2 = ((bf16[16,32,1536]{2,1,0:T(8,128)(2,1)}), bf16[16,32,1536]{2,1,0:T(8,128)(2,1)S(1)}, u32[]{:S(2)}, u32[]{:S(2)}) async-start(bf16[16,32,1536]{2,1,0:T(8,128)(2,1)} %bitcast.219), calls=%async_computation.2 | async-start | bytes 3145728 | tf_op jit(solution)/shard_map/all_to_all | solution.py:383
  262.6 2.4 fusion.30
  270.1 3.6 %collective-permute-done.5 = bf16[192,2048]{1,0:T(8,128)(2,1)} collective-permute-done((bf16[192,2048]{1,0:T(8,128)(2,1)}, bf16[192,2048]{1,0:T(8,128)(2,1)}, u32[]{:S(2)}, u32[]{:S(2)}) %collective-permute-start.5) | collective-permute-done | bytes 786464 | tf_op jit(solution)/shard_map/ppermute | solution.py:180
  273.8 2.9 fusion.13
  277.8 4.0 %fusion.5 = bf16[4,64,1536]{2,1,0:T(8,128)(2,1)} fusion(f32[4,128]{1,0:T(4,128)S(1)} %copy-done.16, s32[4,128]{1,0:T(4,128)S(1)} %copy-done.15, bf16[16,32,1536]{2,1,0:T(8,128)(2,1)} %all-to-all-done.1), kind=kOutput, calls=%fused_computation.18 | convolution fusion | flops 605978624 | bytes 2363392 | tf_op jit(solution)/shard_map/wze,wzi->wei/dot_general | solution.py:391
  283.3 2.2 all-to-all-done.2
  287.1 3.5 %collective-permute-done.1 = bf16[192,2048]{1,0:T(8,128)(2,1)} collective-permute-done((bf16[192,2048]{1,0:T(8,128)(2,1)}, bf16[192,2048]{1,0:T(8,128)(2,1)}, u32[]{:S(2)}, u32[]{:S(2)}) %collective-permute-start.1) | collective-permute-done | bytes 786464 | tf_op jit(solution)/shard_map/ppermute | solution.py:180
  290.6 7.5 %collective-permute-done.8 = bf16[192,2048]{1,0:T(8,128)(2,1)} collective-permute-done((bf16[192,2048]{1,0:T(8,128)(2,1)}, bf16[192,2048]{1,0:T(8,128)(2,1)}, u32[]{:S(2)}, u32[]{:S(2)}) %collective-permute-start.8) | collective-permute-done | bytes 786464 | tf_op jit(solution)/shard_map/ppermute | solution.py:196
  298.1 2.2 fusion.15
  (126 shorter events, 49.0 us)
Async XLA Ops:
  2.9 4.7 %copy-start.11 = (s32[4,16,8]{1,2,0:T(8,128)S(1)}, s32[4,16,8]{1,2,0:T(8,128)}, u32[]{:S(2)}) copy-start(s32[4,16,8]{1,2,0:T(8,128)} %param.9) | copy-start | bytes 6148
  16.3 124.3 %all-to-all-start = ((bf16[16,64,1536]{2,1,0:T(8,128)(2,1)}), bf16[16,64,1536]{2,1,0:T(8,128)(2,1)}, u32[]{:S(2)}, u32[]{:S(2)}) async-start(bf16[16,64,1536]{2,1,0:T(8,128)(2,1)} %pad_maximum_fusion), calls=%async_computation | async-start | bytes 6291456 | tf_op jit(solution)/shard_map/all_to_all | solution.py:338
  25.1 117.8 %copy-start.13 = (s32[4,16,8]{2,1,0:T(8,128)}, s32[4,16,8]{2,1,0:T(8,128)S(1)}, u32[]{:S(2)}) copy-start(s32[4,16,8]{2,1,0:T(8,128)S(1)} %copy.55) | copy-start | bytes 6148
  153.6 7.6 %copy-start.5 = (bf16[1024,1536]{1,0:T(8,128)(2,1)}, bf16[1024,1536]{1,0:T(8,128)(2,1)S(1)}, u32[]{:S(2)}) copy-start(bf16[1024,1536]{1,0:T(8,128)(2,1)S(1)} %convolution_convert_fusion.1) | copy-start | bytes 9437188
  154.6 15.4 %collective-permute-start.9 = (bf16[64,1536]{1,0:T(8,128)(2,1)}, bf16[64,1536]{1,0:T(8,128)(2,1)S(1)}, u32[]{:S(2)}, u32[]{:S(2)}) collective-permute-start(bf16[64,1536]{1,0:T(8,128)(2,1)} %get-tuple-element.58), channel_id=1, source_target_pairs={{0,32},{16,48},{32,64},{48,80},{64,96},{80,112},{96,0},{112,16},{1... | collective-permute-start | bytes 589832 | tf_op jit(solution)/shard_map/ppermute | solution.py:176
  156.7 13.3 %collective-permute-start.13 = (bf16[64,1536]{1,0:T(8,128)(2,1)}, bf16[64,1536]{1,0:T(8,128)(2,1)}, u32[]{:S(2)}, u32[]{:S(2)}) collective-permute-start(bf16[64,1536]{1,0:T(8,128)(2,1)} %get-tuple-element.60), channel_id=1, source_target_pairs={{0,32},{16,48},{32,64},{48,80},{64,96},{80,112},{96,0},{112,16},{1... | collective-permute-start | bytes 589832 | tf_op jit(solution)/shard_map/ppermute | solution.py:176
  157.3 12.8 %collective-permute-start.15 = (bf16[64,1536]{1,0:T(8,128)(2,1)}, bf16[64,1536]{1,0:T(8,128)(2,1)}, u32[]{:S(2)}, u32[]{:S(2)}) collective-permute-start(bf16[64,1536]{1,0:T(8,128)(2,1)} %get-tuple-element.62), channel_id=1, source_target_pairs={{0,96},{16,112},{32,0},{48,16},{64,32},{80,48},{96,64},{112,80},{1... | collective-permute-start | bytes 589832 | tf_op jit(solution)/shard_map/ppermute | solution.py:177
  158.2 11.9 %collective-permute-start.11 = (bf16[64,1536]{1,0:T(8,128)(2,1)S(1)}, bf16[64,1536]{1,0:T(8,128)(2,1)}, u32[]{:S(2)}, u32[]{:S(2)}) collective-permute-start(bf16[64,1536]{1,0:T(8,128)(2,1)S(1)} %get-tuple-element.64), channel_id=1, source_target_pairs={{0,96},{16,112},{32,0},{48,16},{64,32},{80,48},{96,64},{112,80},{1... | collective-permute-start | bytes 589832 | tf_op jit(solution)/shard_map/ppermute | solution.py:177
  161.2 31.8 %all-to-all-start.1 = ((bf16[16,32,1536]{2,1,0:T(8,128)(2,1)}), bf16[16,32,1536]{2,1,0:T(8,128)(2,1)}, u32[]{:S(2)}, u32[]{:S(2)}) async-start(bf16[16,32,1536]{2,1,0:T(8,128)(2,1)} %bitcast.220), calls=%async_computation.1 | async-start | bytes 3145728 | tf_op jit(solution)/shard_map/all_to_all | solution.py:352
  171.7 11.3 %collective-permute-start.16 = (bf16[128,1536]{1,0:T(8,128)(2,1)S(1)}, bf16[128,1536]{1,0:T(8,128)(2,1)S(1)}, u32[]{:S(2)}, u32[]{:S(2)}) collective-permute-start(bf16[128,1536]{1,0:T(8,128)(2,1)S(1)} %pad_maximum_fusion.8), channel_id=1, source_target_pairs={{0,96},{16,112},{32,0},{48,16},{64,32},{80,48},{96,64},{112,80},{1... | collective-permute-start | bytes 1179656 | tf_op jit(solution)/shard_map/ppermute | solution.py:181
  174.1 10.4 %collective-permute-start.14 = (bf16[128,1536]{1,0:T(8,128)(2,1)S(1)}, bf16[128,1536]{1,0:T(8,128)(2,1)S(1)}, u32[]{:S(2)}, u32[]{:S(2)}) collective-permute-start(bf16[128,1536]{1,0:T(8,128)(2,1)S(1)} %pad_maximum_fusion.7), channel_id=1, source_target_pairs={{0,32},{16,48},{32,64},{48,80},{64,96},{80,112},{96,0},{112,16},{1... | collective-permute-start | bytes 1179656 | tf_op jit(solution)/shard_map/ppermute | solution.py:180
  175.0 87.6 %collective-permute-start.12 = (bf16[128,1536]{1,0:T(8,128)(2,1)}, bf16[128,1536]{1,0:T(8,128)(2,1)}, u32[]{:S(2)}, u32[]{:S(2)}) collective-permute-start(bf16[128,1536]{1,0:T(8,128)(2,1)} %pad_maximum_fusion.6), channel_id=1, source_target_pairs={{0,96},{16,112},{32,0},{48,16},{64,32},{80,48},{96,64},{112,80},{1... | collective-permute-start | bytes 1179656 | tf_op jit(solution)/shard_map/ppermute | solution.py:181
  177.2 17.8 %copy-start.14 = (s32[4,16,8]{2,1,0:T(8,128)S(1)}, s32[4,16,8]{2,1,0:T(8,128)}, u32[]{:S(2)}) copy-start(s32[4,16,8]{2,1,0:T(8,128)} %copy-done.13) | copy-start | bytes 6148
  196.1 4.2 %copy-start.19 = (bf16[8,192,1024]{2,1,0:T(8,128)(2,1)S(1)}, bf16[8,192,1024]{2,1,0:T(8,128)(2,1)}, u32[]{:S(2)}) copy-start(bf16[8,192,1024]{2,1,0:T(8,128)(2,1)} %get-tuple-element.10) | copy-start | bytes 9437188
  210.8 35.4 %collective-permute-start = (bf16[96,2048]{1,0:T(8,128)(2,1)}, bf16[96,2048]{1,0:T(8,128)(2,1)}, u32[]{:S(2)}, u32[]{:S(2)}) collective-permute-start(bf16[96,2048]{1,0:T(8,128)(2,1)} %get-tuple-element.44), channel_id=1, source_target_pairs={{0,32},{16,48},{32,64},{48,80},{64,96},{80,112},{96,0},{112,16},{1... | collective-permute-start | bytes 1179656 | tf_op jit(solution)/shard_map/ppermute | solution.py:176
  212.5 34.6 %collective-permute-start.4 = (bf16[96,2048]{1,0:T(8,128)(2,1)}, bf16[96,2048]{1,0:T(8,128)(2,1)}, u32[]{:S(2)}, u32[]{:S(2)}) collective-permute-start(bf16[96,2048]{1,0:T(8,128)(2,1)} %get-tuple-element.46), channel_id=1, source_target_pairs={{0,32},{16,48},{32,64},{48,80},{64,96},{80,112},{96,0},{112,16},{1... | collective-permute-start | bytes 1179656 | tf_op jit(solution)/shard_map/ppermute | solution.py:176
  214.3 34.1 %collective-permute-start.6 = (bf16[96,2048]{1,0:T(8,128)(2,1)}, bf16[96,2048]{1,0:T(8,128)(2,1)}, u32[]{:S(2)}, u32[]{:S(2)}) collective-permute-start(bf16[96,2048]{1,0:T(8,128)(2,1)} %get-tuple-element.48), channel_id=1, source_target_pairs={{0,96},{16,112},{32,0},{48,16},{64,32},{80,48},{96,64},{112,80},{1... | collective-permute-start | bytes 1179656 | tf_op jit(solution)/shard_map/ppermute | solution.py:177
  214.3 34.1 %collective-permute-start.2 = (bf16[96,2048]{1,0:T(8,128)(2,1)}, bf16[96,2048]{1,0:T(8,128)(2,1)}, u32[]{:S(2)}, u32[]{:S(2)}) collective-permute-start(bf16[96,2048]{1,0:T(8,128)(2,1)} %get-tuple-element.50), channel_id=1, source_target_pairs={{0,96},{16,112},{32,0},{48,16},{64,32},{80,48},{96,64},{112,80},{1... | collective-permute-start | bytes 1179656 | tf_op jit(solution)/shard_map/ppermute | solution.py:177
  215.7 20.8 %all-to-all-start.3 = ((f32[128,1,192]{2,1,0:T(1,128)}), f32[128,1,192]{2,1,0:T(1,128)S(1)}, u32[]{:S(2)}, u32[]{:S(2)}) async-start(f32[128,1,192]{2,1,0:T(1,128)} %all_to_all.25), calls=%async_computation.3 | async-start | bytes 262144 | tf_op jit(solution)/shard_map/all_to_all | solution.py:370
  237.4 16.8 %all-to-all-start.4 = ((f32[128,1,192]{2,1,0:T(1,128)}), f32[128,1,192]{2,1,0:T(1,128)S(1)}, u32[]{:S(2)}, u32[]{:S(2)}) async-start(f32[128,1,192]{2,1,0:T(1,128)} %broadcast_in_dim.32), calls=%async_computation.4 | async-start | bytes 262144 | tf_op jit(solution)/shard_map/all_to_all | solution.py:412
  246.2 16.4 %collective-permute-start.10 = (bf16[128,1536]{1,0:T(8,128)(2,1)}, bf16[128,1536]{1,0:T(8,128)(2,1)}, u32[]{:S(2)}, u32[]{:S(2)}) collective-permute-start(bf16[128,1536]{1,0:T(8,128)(2,1)} %pad_maximum_fusion.5), channel_id=1, source_target_pairs={{0,32},{16,48},{32,64},{48,80},{64,96},{80,112},{96,0},{112,16},{1... | collective-permute-start | bytes 1179656 | tf_op jit(solution)/shard_map/ppermute | solution.py:180
  247.1 15.5 %collective-permute-start.17 = (bf16[128,1536]{1,0:T(8,128)(2,1)}, bf16[128,1536]{1,0:T(8,128)(2,1)}, u32[]{:S(2)}, u32[]{:S(2)}) collective-permute-start(bf16[128,1536]{1,0:T(8,128)(2,1)} %fusion.27), channel_id=1, source_target_pairs={{0,16},{16,0},{32,48},{48,32},{64,80},{80,64},{96,112},{112,96},{1... | collective-permute-start | bytes 1179656 | tf_op jit(solution)/shard_map/ppermute | solution.py:196
  251.7 18.4 %collective-permute-start.7 = (bf16[192,2048]{1,0:T(8,128)(2,1)}, bf16[192,2048]{1,0:T(8,128)(2,1)}, u32[]{:S(2)}, u32[]{:S(2)}) collective-permute-start(bf16[192,2048]{1,0:T(8,128)(2,1)} %pad_maximum_fusion.4), channel_id=1, source_target_pairs={{0,96},{16,112},{32,0},{48,16},{64,32},{80,48},{96,64},{112,80},{1... | collective-permute-start | bytes 2359304 | tf_op jit(solution)/shard_map/ppermute | solution.py:181
  253.2 20.6 %collective-permute-start.5 = (bf16[192,2048]{1,0:T(8,128)(2,1)}, bf16[192,2048]{1,0:T(8,128)(2,1)}, u32[]{:S(2)}, u32[]{:S(2)}) collective-permute-start(bf16[192,2048]{1,0:T(8,128)(2,1)} %pad_maximum_fusion.3), channel_id=1, source_target_pairs={{0,32},{16,48},{32,64},{48,80},{64,96},{80,112},{96,0},{112,16},{1... | collective-permute-start | bytes 2359304 | tf_op jit(solution)/shard_map/ppermute | solution.py:180
  254.2 10.9 %copy-start.9 = (f32[128,1,192]{2,1,0:T(1,128)}, f32[128,1,192]{2,1,0:T(1,128)S(1)}, u32[]{:S(2)}) copy-start(f32[128,1,192]{2,1,0:T(1,128)S(1)} %all-to-all-done.4) | copy-start | bytes 294916
  254.2 31.3 %all-to-all-start.2 = ((bf16[16,32,1536]{2,1,0:T(8,128)(2,1)}), bf16[16,32,1536]{2,1,0:T(8,128)(2,1)S(1)}, u32[]{:S(2)}, u32[]{:S(2)}) async-start(bf16[16,32,1536]{2,1,0:T(8,128)(2,1)} %bitcast.219), calls=%async_computation.2 | async-start | bytes 3145728 | tf_op jit(solution)/shard_map/all_to_all | solution.py:383
  266.0 21.1 %collective-permute-start.3 = (bf16[192,2048]{1,0:T(8,128)(2,1)}, bf16[192,2048]{1,0:T(8,128)(2,1)S(1)}, u32[]{:S(2)}, u32[]{:S(2)}) collective-permute-start(bf16[192,2048]{1,0:T(8,128)(2,1)} %pad_maximum_fusion.2), channel_id=1, source_target_pairs={{0,96},{16,112},{32,0},{48,16},{64,32},{80,48},{96,64},{112,80},{1... | collective-permute-start | bytes 2359304 | tf_op jit(solution)/shard_map/ppermute | solution.py:181
  266.6 11.2 %copy-start.15 = (s32[4,128]{1,0:T(4,128)S(1)}, s32[4,128]{1,0:T(4,128)}, u32[]{:S(2)}) copy-start(s32[4,128]{1,0:T(4,128)} %eq.41) | copy-start | bytes 6148
  266.6 11.2 %copy-start.16 = (f32[4,128]{1,0:T(4,128)S(1)}, f32[4,128]{1,0:T(4,128)}, u32[]{:S(2)}) copy-start(f32[4,128]{1,0:T(4,128)} %mul.86) | copy-start | bytes 6148
  267.6 14.2 %copy-start.10 = (f32[128,1,192]{2,1,0:T(1,128)S(1)}, f32[128,1,192]{2,1,0:T(1,128)}, u32[]{:S(2)}) copy-start(f32[128,1,192]{2,1,0:T(1,128)} %copy-done.9) | copy-start | bytes 294916
  267.6 23.0 %collective-permute-start.1 = (bf16[192,2048]{1,0:T(8,128)(2,1)}, bf16[192,2048]{1,0:T(8,128)(2,1)}, u32[]{:S(2)}, u32[]{:S(2)}) collective-permute-start(bf16[192,2048]{1,0:T(8,128)(2,1)} %pad_maximum_fusion.1), channel_id=1, source_target_pairs={{0,32},{16,48},{32,64},{48,80},{64,96},{80,112},{96,0},{112,16},{1... | collective-permute-start | bytes 2359304 | tf_op jit(solution)/shard_map/ppermute | solution.py:180
  276.6 21.5 %collective-permute-start.8 = (bf16[192,2048]{1,0:T(8,128)(2,1)}, bf16[192,2048]{1,0:T(8,128)(2,1)}, u32[]{:S(2)}, u32[]{:S(2)}) collective-permute-start(bf16[192,2048]{1,0:T(8,128)(2,1)} %fusion.13), channel_id=1, source_target_pairs={{0,16},{16,0},{32,48},{48,32},{64,80},{80,64},{96,112},{112,96},{1... | collective-permute-start | bytes 2359304 | tf_op jit(solution)/shard_map/ppermute | solution.py:196
  (12 other events, 32.7 us)

commit v7 on v4

--- a/solution.py
+++ b/solution.py
@@ -237,20 +237,24 @@
             send(a, 1, shards[a], me, whole, left),
             send(a, 2, shards[a], me, whole, partner),
         ]
-    for copy in first:
-        copy.wait_recv()
     mate = partner
     for a in range(count):
         whole, low, high = spans[a]
+        first[3 * a].wait_recv()
+        to_right = send(a, 3, outs[a].at[left, low], left, low, right)
+        first[3 * a + 1].wait_recv()
+        to_left = send(a, 4, outs[a].at[right, high], right, high, left)
+        second += [to_right, to_left]
+    for a in range(count):
+        whole = spans[a][0]
+        first[3 * a + 2].wait_recv()
         second += [
-            send(a, 3, outs[a].at[left, low], left, low, right),
-            send(a, 4, outs[a].at[right, high], right, high, left),
             send(a, 5, outs[a].at[mate], mate, whole, right),
             send(a, 6, outs[a].at[mate], mate, whole, left),
         ]
-    for a in range(count):
-        second[4 * a + 2].wait_recv()
-        second[4 * a + 3].wait_recv()
+    forwards, mates = second[: 2 * count], second[2 * count :]
+    for copy in mates:
+        copy.wait_recv()
     mate_left, mate_right = lax.rem(mate + n - 2, n), lax.rem(mate + 2, n)
     for a in range(count):
         whole, low, high = spans[a]
@@ -260,9 +264,8 @@
         ]
     for copy in first:
         copy.wait_send()
-    for a in range(count):
-        second[4 * a].wait_recv()
-        second[4 * a + 1].wait_recv()
+    for copy in forwards:
+        copy.wait_recv()
     for copy in second:
         copy.wait_send()
     for copy in third:

time: 293 us -> 263 us (0.90)
  Pallas kernels: 114 us -> 84.4 us
    pallas_call x1, Pallas kernels: 114 us -> 84.4 us  [dp_gather_kernel(): pl.pallas_call(functools.partial(_ring_gather_kernel, n), out_shape=[jax....]
  transfers between devices with their start and end apart: 23 -> 23, of which waited for: 8 -> 8; matrix products, arithmetic and copies ran while one was open for 13% -> 14% of each run, Pallas kernels for 39% -> 32%
where the time goes in v7:
time: 263 us; the launch traced here: 260 us
  Pallas kernels  84.4 us (32%)
  starting transfers between devices  60.4 us (23%)
  waiting for transfers between devices  40 us (15%)
  matrix products  33.5 us (13%)
  local copies, waits for them, and re-layouts  21.1 us (8%)
  other arithmetic  19.3 us (7%)
    pallas_call x1, Pallas kernels, dp_gather_kernel(): pl.pallas_call(functools.partial(_ring_gather_kernel, n), out_shape=[jax....  84.4 us
    all_to_all x1, starting transfers between devices, body(): lax.all_to_all(d_rows.reshape(expert_count_axis, -1, model_width), 'exper...  13.2 us
    ppermute x4, waiting for transfers between devices, x_ring_scatter(): low = lax.ppermute(blocks[2][:h].astype(jnp.bfloat16), 'dp', _x_shift(n, 1))  10.7 us
    all_to_all x1, waiting for transfers between devices, body(): lax.all_to_all(d_rows.reshape(expert_count_axis, -1, model_width), 'exper...  8.67 us
    all_to_all x1, starting transfers between devices, body(): lax.all_to_all(jnp.concatenate([picked, scaled_cot], axis=1), 'expert', 0...  8.63 us
    ppermute x4, waiting for transfers between devices, x_ring_scatter(): lax.ppermute(to_left.astype(jnp.bfloat16), 'dp', _x_shift(n, -1))  8.16 us
    all_to_all x1, waiting for transfers between devices, body(): lax.all_to_all(router_full.reshape(devices, -1), ('dp', 'expert'), 0, 0,...  8.13 us
    all_to_all x1, starting transfers between devices, body(): lax.all_to_all(expert_out.reshape(expert_count_axis, -1, model_width), 'e...  7.99 us
  transfers between devices with their start and end apart: 23, of which 8 were waited for; matrix products, arithmetic and copies ran while one was open for 14% of the time, Pallas kernels for 32%

profile of v7, /device:TPU:5, one launch (start us, length us, event | category | flops | bytes accessed | tf_op | source)
XLA Modules:
  0.0 259.8 jit_solution(13573036934295430294)
XLA Ops:
  2.9 4.5 %gather_fusion.2 = f32[512]{0:T(512)S(1)} fusion(f32[16,256]{1,0:T(8,128)S(1)} %bitcast.187, s32[512]{0:T(512)S(1)} %reshape.317), kind=kCustom, calls=%fused_computation.2 | custom fusion | bytes 8192 | tf_op jit(solution)/shard_map/jit(take_along_axis)/gather | solution.py:332
  7.9 2.9 %gather_fusion = bf16[512,1536]{1,0:T(8,128)(2,1)} fusion(bf16[256,1536]{1,0:T(8,128)(2,1)S(1)} %copy-done, s32[1024]{0:T(1024)S(1)} %pad_clamp_fusion), kind=kCustom, calls=%fused_computation | custom fusion | bytes 3147776 | tf_op jit(solution)/shard_map/gather | solution.py:331
  10.9 2.1 gather_fusion.1
  14.4 1.9 pad_maximum_fusion
  16.4 8.6 %all-to-all-start = ((bf16[16,64,1536]{2,1,0:T(8,128)(2,1)}), bf16[16,64,1536]{2,1,0:T(8,128)(2,1)}, u32[]{:S(2)}, u32[]{:S(2)}) async-start(bf16[16,64,1536]{2,1,0:T(8,128)(2,1)} %pad_maximum_fusion), calls=%async_computation | async-start | bytes 6291456 | tf_op jit(solution)/shard_map/all_to_all | solution.py:341
  26.8 84.4 %shard_map.118 = (bf16[8,192,1024]{2,1,0:T(8,128)(2,1)}, bf16[8,192,1024]{2,1,0:T(8,128)(2,1)}, bf16[8,128,1536]{2,1,0:T(8,128)(2,1)}) custom-call(bf16[192,1024]{1,0:T(8,128)(2,1)} %bitcast.206, bf16[192,1024]{1,0:T(8,128)(2,1)} %bitcast.207, bf16[128,1536]{1,0:T(8,128)(2,1)} %bitcast.208), custom_call_target="tpu_custom_call" | custom-call | tf_op jit(solution)/shard_map/pallas_call | solution.py:281
  111.2 2.2 fusion.39
  117.8 3.5 %multiply_convert_fusion = (bf16[512,1024]{1,0:T(8,128)(2,1)S(1)}, bf16[512,1024]{1,0:T(8,128)(2,1)}, bf16[512,1024]{1,0:T(8,128)(2,1)S(1)}) fusion(f32[512,1024]{1,0:T(8,128)S(1)} %fusion.40, f32[512,1024]{1,0:T(8,128)S(1)} %fusion.41, bf16[512,1536]{1,0:T(8,128)(2,1)S(1)} %bitcast.204, bf16[1024,1536]{1,0:T(8,128)(2,1)S(1)} %bitcast.215), kind=kOutput, calls=%fused_computation.24 | convolution fusion | flops 1618477056 | bytes 12058624 | tf_op jit(solution)/shard_map/erd,ehd->erh/dot_general | solution.py:360
  121.4 3.0 %convolution_convert_fusion.2 = bf16[512,1536]{1,0:T(8,128)(2,1)} fusion(bf16[512,1024]{1,0:T(8,128)(2,1)S(1)} %get-tuple-element.52, bf16[1024,1536]{1,0:T(8,128)(2,1)S(1)} %bitcast.216), kind=kOutput, calls=%fused_computation.16 | convolution fusion | flops 1611399168 | bytes 5767168 | tf_op jit(solution)/shard_map/erh,ehd->erd/dot_general | solution.py:352
  124.3 3.6 %convolution_convert_fusion.1 = bf16[1024,1536]{1,0:T(8,128)(2,1)} fusion(bf16[512,1024]{1,0:T(8,128)(2,1)S(1)} %get-tuple-element.52, bf16[512,1536]{1,0:T(8,128)(2,1)S(1)} %bitcast.205), kind=kOutput, calls=%fused_computation.7 | convolution fusion | flops 1612185600 | bytes 5767168 | tf_op jit(solution)/shard_map/erc,erd->cd/dot_general | solution.py:307
  127.9 8.0 %all-to-all-start.1 = ((bf16[16,32,1536]{2,1,0:T(8,128)(2,1)}), bf16[16,32,1536]{2,1,0:T(8,128)(2,1)}, u32[]{:S(2)}, u32[]{:S(2)}) async-start(bf16[16,32,1536]{2,1,0:T(8,128)(2,1)} %bitcast.200), calls=%async_computation.1 | async-start | bytes 3145728 | tf_op jit(solution)/shard_map/all_to_all | solution.py:355
  135.9 4.2 %fusion.42 = f32[512,1536]{1,0:T(8,128)S(1)} fusion(bf16[512,1024]{1,0:T(8,128)(2,1)} %get-tuple-element.51, bf16[1536,1024]{1,0:T(8,128)(2,1)} %bitcast.213), kind=kOutput, calls=%fused_computation.120 | convolution fusion | flops 1610612736 | bytes 7340032 | tf_op jit(solution)/shard_map/erh,edh->erd/dot_general | solution.py:367
  140.2 2.2 collective-permute-start.9
  143.9 3.1 %fusion.4 = bf16[512,1536]{1,0:T(8,128)(2,1)} fusion(f32[512,1536]{1,0:T(8,128)S(1)} %fusion.42, bf16[512,1024]{1,0:T(8,128)(2,1)S(1)} %get-tuple-element.50, bf16[1536,1024]{1,0:T(8,128)(2,1)S(1)} %bitcast.212), kind=kOutput, calls=%fused_computation.15 | convolution fusion | flops 1612185600 | bytes 8912896 | tf_op jit(solution)/shard_map/erh,edh->erd/dot_general | solution.py:368
  147.0 3.8 %convolution_convert_fusion = bf16[1536,2048]{1,0:T(8,128)(2,1)S(1)} fusion(bf16[512,1536]{1,0:T(8,128)(2,1)S(1)} %bitcast.203, bf16[1,512,1024]{2,1,0:T(8,128)(2,1)S(1)} %bitcast.217, bf16[1,512,1024]{2,1,0:T(8,128)(2,1)S(1)} %bitcast.218), kind=kOutput, calls=%fused_computation.3 | convolution fusion | flops 3228565504 | bytes 9961472 | tf_op jit(solution)/shard_map/erc,erk->ck/dot_general | solution.py:312
  155.0 2.7 %collective-permute-start.16 = (bf16[128,1536]{1,0:T(8,128)(2,1)S(1)}, bf16[128,1536]{1,0:T(8,128)(2,1)S(1)}, u32[]{:S(2)}, u32[]{:S(2)}) collective-permute-start(bf16[128,1536]{1,0:T(8,128)(2,1)S(1)} %pad_maximum_fusion.8), channel_id=1, source_target_pairs={{0,96},{16,112},{32,0},{48,16},{64,32},{80,48},{96,64},{112,80},{1... | collective-permute-start | bytes 1179656 | tf_op jit(solution)/shard_map/ppermute | solution.py:181
  158.5 2.8 %collective-permute-done = bf16[96,2048]{1,0:T(8,128)(2,1)S(1)} collective-permute-done((bf16[96,2048]{1,0:T(8,128)(2,1)S(1)}, bf16[96,2048]{1,0:T(8,128)(2,1)S(1)}, u32[]{:S(2)}, u32[]{:S(2)}) %collective-permute-start) | collective-permute-done | bytes 393248 | tf_op jit(solution)/shard_map/ppermute | solution.py:176
  161.9 7.9 %collective-permute-done.4 = bf16[96,2048]{1,0:T(8,128)(2,1)S(1)} collective-permute-done((bf16[96,2048]{1,0:T(8,128)(2,1)S(1)}, bf16[96,2048]{1,0:T(8,128)(2,1)S(1)}, u32[]{:S(2)}, u32[]{:S(2)}) %collective-permute-start.4) | collective-permute-done | bytes 393248 | tf_op jit(solution)/shard_map/ppermute | solution.py:176
  175.2 4.8 %collective-permute-done.16 = bf16[128,1536]{1,0:T(8,128)(2,1)S(1)} collective-permute-done((bf16[128,1536]{1,0:T(8,128)(2,1)S(1)}, bf16[128,1536]{1,0:T(8,128)(2,1)S(1)}, u32[]{:S(2)}, u32[]{:S(2)}) %collective-permute-start.16) | collective-permute-done | bytes 393248 | tf_op jit(solution)/shard_map/ppermute | solution.py:181
  180.0 2.1 collective-permute-start.5
  184.9 13.2 %all-to-all-start.2 = ((bf16[16,32,1536]{2,1,0:T(8,128)(2,1)}), bf16[16,32,1536]{2,1,0:T(8,128)(2,1)}, u32[]{:S(2)}, u32[]{:S(2)}) async-start(bf16[16,32,1536]{2,1,0:T(8,128)(2,1)} %bitcast.199), calls=%async_computation.2 | async-start | bytes 3145728 | tf_op jit(solution)/shard_map/all_to_all | solution.py:370
  199.7 2.3 fusion.25
  202.0 3.4 %collective-permute-done.7 = bf16[192,2048]{1,0:T(8,128)(2,1)} collective-permute-done((bf16[192,2048]{1,0:T(8,128)(2,1)}, bf16[192,2048]{1,0:T(8,128)(2,1)}, u32[]{:S(2)}, u32[]{:S(2)}) %collective-permute-start.7) | collective-permute-done | bytes 786464 | tf_op jit(solution)/shard_map/ppermute | solution.py:181
  205.4 2.9 %fusion.11 = bf16[192,2048]{1,0:T(8,128)(2,1)} fusion(bf16[192,2048]{1,0:T(8,128)(2,1)} %collective-permute-done.7, bf16[192,2048]{1,0:T(8,128)(2,1)} %collective-permute-done.5, bf16[8,192,2048]{2,1,0:T(8,128)(2,1)} %bitcast.192, s32[]{:T(128)S(6)} %select_n.137), kind=kLoop, calls=%fused_computation.31 | loop fusion | flops 2359296 | bytes 3145732 | tf_op jit(solution)/shard_map/convert_element_type | solution.py:196
  208.3 1.9 fusion.1
  212.5 8.7 %all-to-all-done.2 = bf16[16,32,1536]{2,1,0:T(8,128)(2,1)} async-done(((bf16[16,32,1536]{2,1,0:T(8,128)(2,1)}), bf16[16,32,1536]{2,1,0:T(8,128)(2,1)}, u32[]{:S(2)}, u32[]{:S(2)}) %all-to-all-start.2) | async-done | bytes 1572896 | tf_op jit(solution)/shard_map/all_to_all | solution.py:370
  221.1 7.4 %all-to-all-start.3 = ((f32[128,1,192]{2,1,0:T(1,128)}), f32[128,1,192]{2,1,0:T(1,128)S(1)}, u32[]{:S(2)}, u32[]{:S(2)}) async-start(f32[128,1,192]{2,1,0:T(1,128)} %all_to_all.25), calls=%async_computation.3 | async-start | bytes 262144 | tf_op jit(solution)/shard_map/all_to_all | solution.py:408
  231.6 8.1 %all-to-all-done.3 = f32[128,1,192]{2,1,0:T(1,128)S(1)} async-done(((f32[128,1,192]{2,1,0:T(1,128)}), f32[128,1,192]{2,1,0:T(1,128)S(1)}, u32[]{:S(2)}, u32[]{:S(2)}) %all-to-all-start.3) | async-done | bytes 98336 | tf_op jit(solution)/shard_map/all_to_all | solution.py:408
  240.6 6.4 %all-to-all-start.4 = ((f32[128,1,192]{2,1,0:T(1,128)}), f32[128,1,192]{2,1,0:T(1,128)S(1)}, u32[]{:S(2)}, u32[]{:S(2)}) async-start(f32[128,1,192]{2,1,0:T(1,128)} %broadcast_in_dim.32), calls=%async_computation.4 | async-start | bytes 262144 | tf_op jit(solution)/shard_map/all_to_all | solution.py:414
  247.0 4.0 %fusion.5 = bf16[4,64,1536]{2,1,0:T(8,128)(2,1)} fusion(f32[4,128]{1,0:T(4,128)S(1)} %copy-done.12, s32[4,128]{1,0:T(4,128)S(1)} %copy-done.11, bf16[16,32,1536]{2,1,0:T(8,128)(2,1)} %all-to-all-done.1), kind=kOutput, calls=%fused_computation.18 | convolution fusion | flops 605978624 | bytes 2363392 | tf_op jit(solution)/shard_map/wze,wzi->wei/dot_general | solution.py:379
  251.0 4.0 %all-to-all-done.4 = f32[128,1,192]{2,1,0:T(1,128)S(1)} async-done(((f32[128,1,192]{2,1,0:T(1,128)}), f32[128,1,192]{2,1,0:T(1,128)S(1)}, u32[]{:S(2)}, u32[]{:S(2)}) %all-to-all-start.4) | async-done | bytes 98336 | tf_op jit(solution)/shard_map/all_to_all | solution.py:414
  256.4 2.1 fusion.13
  (119 shorter events, 36.0 us)
Async XLA Ops:
  2.9 4.7 %copy-start.7 = (s32[4,16,8]{1,2,0:T(8,128)S(1)}, s32[4,16,8]{1,2,0:T(8,128)}, u32[]{:S(2)}) copy-start(s32[4,16,8]{1,2,0:T(8,128)} %param.9) | copy-start | bytes 6148
  16.4 94.9 %all-to-all-start = ((bf16[16,64,1536]{2,1,0:T(8,128)(2,1)}), bf16[16,64,1536]{2,1,0:T(8,128)(2,1)}, u32[]{:S(2)}, u32[]{:S(2)}) async-start(bf16[16,64,1536]{2,1,0:T(8,128)(2,1)} %pad_maximum_fusion), calls=%async_computation | async-start | bytes 6291456 | tf_op jit(solution)/shard_map/all_to_all | solution.py:341
  25.2 88.3 %copy-start.9 = (s32[4,16,8]{2,1,0:T(8,128)}, s32[4,16,8]{2,1,0:T(8,128)S(1)}, u32[]{:S(2)}) copy-start(s32[4,16,8]{2,1,0:T(8,128)S(1)} %copy.55) | copy-start | bytes 6148
  127.9 57.1 %all-to-all-start.1 = ((bf16[16,32,1536]{2,1,0:T(8,128)(2,1)}), bf16[16,32,1536]{2,1,0:T(8,128)(2,1)}, u32[]{:S(2)}, u32[]{:S(2)}) async-start(bf16[16,32,1536]{2,1,0:T(8,128)(2,1)} %bitcast.200), calls=%async_computation.1 | async-start | bytes 3145728 | tf_op jit(solution)/shard_map/all_to_all | solution.py:355
  135.9 4.2 %copy-start.4 = (bf16[1024,1536]{1,0:T(8,128)(2,1)S(1)}, bf16[1024,1536]{1,0:T(8,128)(2,1)}, u32[]{:S(2)}) copy-start(bf16[1024,1536]{1,0:T(8,128)(2,1)} %convolution_convert_fusion.1) | copy-start | bytes 9437188
  140.1 3.8 %copy-start.14 = (bf16[8,192,1024]{2,1,0:T(8,128)(2,1)S(1)}, bf16[8,192,1024]{2,1,0:T(8,128)(2,1)}, u32[]{:S(2)}) copy-start(bf16[8,192,1024]{2,1,0:T(8,128)(2,1)} %get-tuple-element.10) | copy-start | bytes 9437188
  140.2 12.4 %collective-permute-start.9 = (bf16[64,1536]{1,0:T(8,128)(2,1)S(1)}, bf16[64,1536]{1,0:T(8,128)(2,1)S(1)}, u32[]{:S(2)}, u32[]{:S(2)}) collective-permute-start(bf16[64,1536]{1,0:T(8,128)(2,1)S(1)} %get-tuple-element.57), channel_id=1, source_target_pairs={{0,32},{16,48},{32,64},{48,80},{64,96},{80,112},{96,0},{112,16},{1... | collective-permute-start | bytes 589832 | tf_op jit(solution)/shard_map/ppermute | solution.py:176
  142.4 12.0 %collective-permute-start.13 = (bf16[64,1536]{1,0:T(8,128)(2,1)S(1)}, bf16[64,1536]{1,0:T(8,128)(2,1)S(1)}, u32[]{:S(2)}, u32[]{:S(2)}) collective-permute-start(bf16[64,1536]{1,0:T(8,128)(2,1)S(1)} %get-tuple-element.59), channel_id=1, source_target_pairs={{0,32},{16,48},{32,64},{48,80},{64,96},{80,112},{96,0},{112,16},{1... | collective-permute-start | bytes 589832 | tf_op jit(solution)/shard_map/ppermute | solution.py:176
  142.9 11.4 %collective-permute-start.15 = (bf16[64,1536]{1,0:T(8,128)(2,1)S(1)}, bf16[64,1536]{1,0:T(8,128)(2,1)S(1)}, u32[]{:S(2)}, u32[]{:S(2)}) collective-permute-start(bf16[64,1536]{1,0:T(8,128)(2,1)S(1)} %get-tuple-element.61), channel_id=1, source_target_pairs={{0,96},{16,112},{32,0},{48,16},{64,32},{80,48},{96,64},{112,80},{1... | collective-permute-start | bytes 589832 | tf_op jit(solution)/shard_map/ppermute | solution.py:177
  143.8 10.9 %collective-permute-start.11 = (bf16[64,1536]{1,0:T(8,128)(2,1)S(1)}, bf16[64,1536]{1,0:T(8,128)(2,1)S(1)}, u32[]{:S(2)}, u32[]{:S(2)}) collective-permute-start(bf16[64,1536]{1,0:T(8,128)(2,1)S(1)} %get-tuple-element.63), channel_id=1, source_target_pairs={{0,96},{16,112},{32,0},{48,16},{64,32},{80,48},{96,64},{112,80},{1... | collective-permute-start | bytes 589832 | tf_op jit(solution)/shard_map/ppermute | solution.py:177
  143.9 3.1 %copy-start.17 = (bf16[512,1024]{1,0:T(8,128)(2,1)S(1)}, bf16[512,1024]{1,0:T(8,128)(2,1)}, u32[]{:S(2)}) copy-start(bf16[512,1024]{1,0:T(8,128)(2,1)} %get-tuple-element.51) | copy-start | bytes 3145732
  150.8 20.8 %copy-start.3 = (bf16[1536,2048]{1,0:T(8,128)(2,1)}, bf16[1536,2048]{1,0:T(8,128)(2,1)S(1)}, u32[]{:S(2)}) copy-start(bf16[1536,2048]{1,0:T(8,128)(2,1)S(1)} %convolution_convert_fusion) | copy-start | bytes 18874372
  151.1 10.3 %collective-permute-start = (bf16[96,2048]{1,0:T(8,128)(2,1)S(1)}, bf16[96,2048]{1,0:T(8,128)(2,1)S(1)}, u32[]{:S(2)}, u32[]{:S(2)}) collective-permute-start(bf16[96,2048]{1,0:T(8,128)(2,1)S(1)} %get-tuple-element.42), channel_id=1, source_target_pairs={{0,32},{16,48},{32,64},{48,80},{64,96},{80,112},{96,0},{112,16},{1... | collective-permute-start | bytes 1179656 | tf_op jit(solution)/shard_map/ppermute | solution.py:176
  152.6 17.2 %collective-permute-start.4 = (bf16[96,2048]{1,0:T(8,128)(2,1)S(1)}, bf16[96,2048]{1,0:T(8,128)(2,1)S(1)}, u32[]{:S(2)}, u32[]{:S(2)}) collective-permute-start(bf16[96,2048]{1,0:T(8,128)(2,1)S(1)} %get-tuple-element.44), channel_id=1, source_target_pairs={{0,32},{16,48},{32,64},{48,80},{64,96},{80,112},{96,0},{112,16},{1... | collective-permute-start | bytes 1179656 | tf_op jit(solution)/shard_map/ppermute | solution.py:176
  154.4 16.6 %collective-permute-start.6 = (bf16[96,2048]{1,0:T(8,128)(2,1)S(1)}, bf16[96,2048]{1,0:T(8,128)(2,1)S(1)}, u32[]{:S(2)}, u32[]{:S(2)}) collective-permute-start(bf16[96,2048]{1,0:T(8,128)(2,1)S(1)} %get-tuple-element.46), channel_id=1, source_target_pairs={{0,96},{16,112},{32,0},{48,16},{64,32},{80,48},{96,64},{112,80},{1... | collective-permute-start | bytes 1179656 | tf_op jit(solution)/shard_map/ppermute | solution.py:177
  154.4 17.2 %collective-permute-start.2 = (bf16[96,2048]{1,0:T(8,128)(2,1)S(1)}, bf16[96,2048]{1,0:T(8,128)(2,1)S(1)}, u32[]{:S(2)}, u32[]{:S(2)}) collective-permute-start(bf16[96,2048]{1,0:T(8,128)(2,1)S(1)} %get-tuple-element.48), channel_id=1, source_target_pairs={{0,96},{16,112},{32,0},{48,16},{64,32},{80,48},{96,64},{112,80},{1... | collective-permute-start | bytes 1179656 | tf_op jit(solution)/shard_map/ppermute | solution.py:177
  155.0 25.0 %collective-permute-start.16 = (bf16[128,1536]{1,0:T(8,128)(2,1)S(1)}, bf16[128,1536]{1,0:T(8,128)(2,1)S(1)}, u32[]{:S(2)}, u32[]{:S(2)}) collective-permute-start(bf16[128,1536]{1,0:T(8,128)(2,1)S(1)} %pad_maximum_fusion.8), channel_id=1, source_target_pairs={{0,96},{16,112},{32,0},{48,16},{64,32},{80,48},{96,64},{112,80},{1... | collective-permute-start | bytes 1179656 | tf_op jit(solution)/shard_map/ppermute | solution.py:181
  161.4 20.8 %collective-permute-start.14 = (bf16[128,1536]{1,0:T(8,128)(2,1)S(1)}, bf16[128,1536]{1,0:T(8,128)(2,1)S(1)}, u32[]{:S(2)}, u32[]{:S(2)}) collective-permute-start(bf16[128,1536]{1,0:T(8,128)(2,1)S(1)} %pad_maximum_fusion.7), channel_id=1, source_target_pairs={{0,32},{16,48},{32,64},{48,80},{64,96},{80,112},{96,0},{112,16},{1... | collective-permute-start | bytes 1179656 | tf_op jit(solution)/shard_map/ppermute | solution.py:180
  169.8 28.4 %collective-permute-start.12 = (bf16[128,1536]{1,0:T(8,128)(2,1)S(1)}, bf16[128,1536]{1,0:T(8,128)(2,1)S(1)}, u32[]{:S(2)}, u32[]{:S(2)}) collective-permute-start(bf16[128,1536]{1,0:T(8,128)(2,1)S(1)} %pad_maximum_fusion.6), channel_id=1, source_target_pairs={{0,96},{16,112},{32,0},{48,16},{64,32},{80,48},{96,64},{112,80},{1... | collective-permute-start | bytes 1179656 | tf_op jit(solution)/shard_map/ppermute | solution.py:181
  171.0 27.3 %collective-permute-start.10 = (bf16[128,1536]{1,0:T(8,128)(2,1)}, bf16[128,1536]{1,0:T(8,128)(2,1)}, u32[]{:S(2)}, u32[]{:S(2)}) collective-permute-start(bf16[128,1536]{1,0:T(8,128)(2,1)} %pad_maximum_fusion.5), channel_id=1, source_target_pairs={{0,32},{16,48},{32,64},{48,80},{64,96},{80,112},{96,0},{112,16},{1... | collective-permute-start | bytes 1179656 | tf_op jit(solution)/shard_map/ppermute | solution.py:180
  173.1 32.3 %collective-permute-start.7 = (bf16[192,2048]{1,0:T(8,128)(2,1)}, bf16[192,2048]{1,0:T(8,128)(2,1)}, u32[]{:S(2)}, u32[]{:S(2)}) collective-permute-start(bf16[192,2048]{1,0:T(8,128)(2,1)} %pad_maximum_fusion.4), channel_id=1, source_target_pairs={{0,96},{16,112},{32,0},{48,16},{64,32},{80,48},{96,64},{112,80},{1... | collective-permute-start | bytes 2359304 | tf_op jit(solution)/shard_map/ppermute | solution.py:181
  180.0 25.4 %collective-permute-start.5 = (bf16[192,2048]{1,0:T(8,128)(2,1)}, bf16[192,2048]{1,0:T(8,128)(2,1)}, u32[]{:S(2)}, u32[]{:S(2)}) collective-permute-start(bf16[192,2048]{1,0:T(8,128)(2,1)} %pad_maximum_fusion.3), channel_id=1, source_target_pairs={{0,32},{16,48},{32,64},{48,80},{64,96},{80,112},{96,0},{112,16},{1... | collective-permute-start | bytes 2359304 | tf_op jit(solution)/shard_map/ppermute | solution.py:180
  183.0 16.7 %collective-permute-start.17 = (bf16[128,1536]{1,0:T(8,128)(2,1)}, bf16[128,1536]{1,0:T(8,128)(2,1)}, u32[]{:S(2)}, u32[]{:S(2)}) collective-permute-start(bf16[128,1536]{1,0:T(8,128)(2,1)} %fusion.22), channel_id=1, source_target_pairs={{0,16},{16,0},{32,48},{48,32},{64,80},{80,64},{96,112},{112,96},{1... | collective-permute-start | bytes 1179656 | tf_op jit(solution)/shard_map/ppermute | solution.py:196
  184.9 36.2 %all-to-all-start.2 = ((bf16[16,32,1536]{2,1,0:T(8,128)(2,1)}), bf16[16,32,1536]{2,1,0:T(8,128)(2,1)}, u32[]{:S(2)}, u32[]{:S(2)}) async-start(bf16[16,32,1536]{2,1,0:T(8,128)(2,1)} %bitcast.199), calls=%async_computation.2 | async-start | bytes 3145728 | tf_op jit(solution)/shard_map/all_to_all | solution.py:370
  198.2 58.3 %collective-permute-start.3 = (bf16[192,2048]{1,0:T(8,128)(2,1)}, bf16[192,2048]{1,0:T(8,128)(2,1)S(1)}, u32[]{:S(2)}, u32[]{:S(2)}) collective-permute-start(bf16[192,2048]{1,0:T(8,128)(2,1)} %pad_maximum_fusion.2), channel_id=1, source_target_pairs={{0,96},{16,112},{32,0},{48,16},{64,32},{80,48},{96,64},{112,80},{1... | collective-permute-start | bytes 2359304 | tf_op jit(solution)/shard_map/ppermute | solution.py:181
  198.3 58.2 %collective-permute-start.1 = (bf16[192,2048]{1,0:T(8,128)(2,1)}, bf16[192,2048]{1,0:T(8,128)(2,1)}, u32[]{:S(2)}, u32[]{:S(2)}) collective-permute-start(bf16[192,2048]{1,0:T(8,128)(2,1)} %pad_maximum_fusion.1), channel_id=1, source_target_pairs={{0,32},{16,48},{32,64},{48,80},{64,96},{80,112},{96,0},{112,16},{1... | collective-permute-start | bytes 2359304 | tf_op jit(solution)/shard_map/ppermute | solution.py:180
  208.3 48.2 %collective-permute-start.8 = (bf16[192,2048]{1,0:T(8,128)(2,1)}, bf16[192,2048]{1,0:T(8,128)(2,1)}, u32[]{:S(2)}, u32[]{:S(2)}) collective-permute-start(bf16[192,2048]{1,0:T(8,128)(2,1)} %fusion.11), channel_id=1, source_target_pairs={{0,16},{16,0},{32,48},{48,32},{64,80},{80,64},{96,112},{112,96},{1... | collective-permute-start | bytes 2359304 | tf_op jit(solution)/shard_map/ppermute | solution.py:196
  210.2 18.3 %copy-start.11 = (s32[4,128]{1,0:T(4,128)S(1)}, s32[4,128]{1,0:T(4,128)}, u32[]{:S(2)}) copy-start(s32[4,128]{1,0:T(4,128)} %eq.41) | copy-start | bytes 6148
  211.4 19.0 %copy-start.8 = (bf16[1536,16]{0,1:T(8,128)(2,1)S(1)}, bf16[1536,16]{0,1:T(8,128)(2,1)}, u32[]{:S(2)}) copy-start(bf16[1536,16]{0,1:T(8,128)(2,1)} %param.10) | copy-start | bytes 147460
  221.1 18.6 %all-to-all-start.3 = ((f32[128,1,192]{2,1,0:T(1,128)}), f32[128,1,192]{2,1,0:T(1,128)S(1)}, u32[]{:S(2)}, u32[]{:S(2)}) async-start(f32[128,1,192]{2,1,0:T(1,128)} %all_to_all.25), calls=%async_computation.3 | async-start | bytes 262144 | tf_op jit(solution)/shard_map/all_to_all | solution.py:408
  230.3 16.7 %copy-start.12 = (f32[4,128]{1,0:T(4,128)S(1)}, f32[4,128]{1,0:T(4,128)}, u32[]{:S(2)}) copy-start(f32[4,128]{1,0:T(4,128)} %mul.88) | copy-start | bytes 6148
  240.6 14.4 %all-to-all-start.4 = ((f32[128,1,192]{2,1,0:T(1,128)}), f32[128,1,192]{2,1,0:T(1,128)S(1)}, u32[]{:S(2)}, u32[]{:S(2)}) async-start(f32[128,1,192]{2,1,0:T(1,128)} %broadcast_in_dim.32), calls=%async_computation.4 | async-start | bytes 262144 | tf_op jit(solution)/shard_map/all_to_all | solution.py:414
  (9 other events, 19.6 us)

commit v8 on v7

--- a/solution.py
+++ b/solution.py
@@ -253,15 +253,13 @@
             send(a, 6, outs[a].at[mate], mate, whole, left),
         ]
     forwards, mates = second[: 2 * count], second[2 * count :]
-    for copy in mates:
-        copy.wait_recv()
     mate_left, mate_right = lax.rem(mate + n - 2, n), lax.rem(mate + 2, n)
     for a in range(count):
         whole, low, high = spans[a]
-        third += [
-            send(a, 7, outs[a].at[mate_left, low], mate_left, low, right),
-            send(a, 8, outs[a].at[mate_right, high], mate_right, high, left),
-        ]
+        mates[2 * a].wait_recv()
+        third.append(send(a, 7, outs[a].at[mate_left, low], mate_left, low, right))
+        mates[2 * a + 1].wait_recv()
+        third.append(send(a, 8, outs[a].at[mate_right, high], mate_right, high, left))
     for copy in first:
         copy.wait_send()
     for copy in forwards:

time: 263 us -> 261 us (level)
  no operation moved by 1% of the time
where the time goes in v8:
time: 261 us; the launch traced here: 258 us
  Pallas kernels  83.6 us (32%)
  starting transfers between devices  58.6 us (22%)
  waiting for transfers between devices  40.6 us (16%)
  matrix products  33.4 us (13%)
  local copies, waits for them, and re-layouts  21.1 us (8%)
  other arithmetic  19.3 us (7%)
    pallas_call x1, Pallas kernels, dp_gather_kernel(): pl.pallas_call(functools.partial(_ring_gather_kernel, n), out_shape=[jax....  83.6 us
    all_to_all x1, starting transfers between devices, body(): lax.all_to_all(d_rows.reshape(expert_count_axis, -1, model_width), 'exper...  12.9 us
    ppermute x4, waiting for transfers between devices, x_ring_scatter(): low = lax.ppermute(blocks[2][:h].astype(jnp.bfloat16), 'dp', _x_shift(n, 1))  10.6 us
    ppermute x4, waiting for transfers between devices, x_ring_scatter(): lax.ppermute(to_left.astype(jnp.bfloat16), 'dp', _x_shift(n, -1))  9.1 us
    all_to_all x1, starting transfers between devices, body(): lax.all_to_all(jnp.concatenate([picked, scaled_cot], axis=1), 'expert', 0...  8.63 us
    all_to_all x1, waiting for transfers between devices, body(): lax.all_to_all(router_full.reshape(devices, -1), ('dp', 'expert'), 0, 0,...  8.13 us
    all_to_all x1, waiting for transfers between devices, body(): lax.all_to_all(d_rows.reshape(expert_count_axis, -1, model_width), 'exper...  7.72 us
    all_to_all x1, starting transfers between devices, body(): lax.all_to_all(expert_out.reshape(expert_count_axis, -1, model_width), 'e...  7.7 us
  transfers between devices with their start and end apart: 23, of which 8 were waited for; matrix products, arithmetic and copies ran while one was open for 14% of the time, Pallas kernels for 32%

profile of v8, /device:TPU:5, one launch (start us, length us, event | category | flops | bytes accessed | tf_op | source)
XLA Modules:
  0.0 257.8 jit_solution(17791781358906495770)
XLA Ops:
  2.9 4.5 %gather_fusion.2 = f32[512]{0:T(512)S(1)} fusion(f32[16,256]{1,0:T(8,128)S(1)} %bitcast.187, s32[512]{0:T(512)S(1)} %reshape.317), kind=kCustom, calls=%fused_computation.2 | custom fusion | bytes 8192 | tf_op jit(solution)/shard_map/jit(take_along_axis)/gather | solution.py:330
  7.9 2.9 %gather_fusion = bf16[512,1536]{1,0:T(8,128)(2,1)} fusion(bf16[256,1536]{1,0:T(8,128)(2,1)S(1)} %copy-done, s32[1024]{0:T(1024)S(1)} %pad_clamp_fusion), kind=kCustom, calls=%fused_computation | custom fusion | bytes 3147776 | tf_op jit(solution)/shard_map/gather | solution.py:329
  10.9 2.1 gather_fusion.1
  14.4 1.9 pad_maximum_fusion
  16.4 8.6 %all-to-all-start = ((bf16[16,64,1536]{2,1,0:T(8,128)(2,1)}), bf16[16,64,1536]{2,1,0:T(8,128)(2,1)}, u32[]{:S(2)}, u32[]{:S(2)}) async-start(bf16[16,64,1536]{2,1,0:T(8,128)(2,1)} %pad_maximum_fusion), calls=%async_computation | async-start | bytes 6291456 | tf_op jit(solution)/shard_map/all_to_all | solution.py:339
  26.8 83.6 %shard_map.118 = (bf16[8,192,1024]{2,1,0:T(8,128)(2,1)}, bf16[8,192,1024]{2,1,0:T(8,128)(2,1)}, bf16[8,128,1536]{2,1,0:T(8,128)(2,1)}) custom-call(bf16[192,1024]{1,0:T(8,128)(2,1)} %bitcast.206, bf16[192,1024]{1,0:T(8,128)(2,1)} %bitcast.207, bf16[128,1536]{1,0:T(8,128)(2,1)} %bitcast.208), custom_call_target="tpu_custom_call" | custom-call | tf_op jit(solution)/shard_map/pallas_call | solution.py:279
  110.5 2.2 fusion.39
  117.1 3.5 %multiply_convert_fusion = (bf16[512,1024]{1,0:T(8,128)(2,1)S(1)}, bf16[512,1024]{1,0:T(8,128)(2,1)}, bf16[512,1024]{1,0:T(8,128)(2,1)S(1)}) fusion(f32[512,1024]{1,0:T(8,128)S(1)} %fusion.40, f32[512,1024]{1,0:T(8,128)S(1)} %fusion.41, bf16[512,1536]{1,0:T(8,128)(2,1)S(1)} %bitcast.204, bf16[1024,1536]{1,0:T(8,128)(2,1)S(1)} %bitcast.215), kind=kOutput, calls=%fused_computation.24 | convolution fusion | flops 1618477056 | bytes 12058624 | tf_op jit(solution)/shard_map/erd,ehd->erh/dot_general | solution.py:358
  120.6 3.0 %convolution_convert_fusion.2 = bf16[512,1536]{1,0:T(8,128)(2,1)} fusion(bf16[512,1024]{1,0:T(8,128)(2,1)S(1)} %get-tuple-element.52, bf16[1024,1536]{1,0:T(8,128)(2,1)S(1)} %bitcast.216), kind=kOutput, calls=%fused_computation.16 | convolution fusion | flops 1611399168 | bytes 5767168 | tf_op jit(solution)/shard_map/erh,ehd->erd/dot_general | solution.py:350
  123.6 3.6 %convolution_convert_fusion.1 = bf16[1024,1536]{1,0:T(8,128)(2,1)} fusion(bf16[512,1024]{1,0:T(8,128)(2,1)S(1)} %get-tuple-element.52, bf16[512,1536]{1,0:T(8,128)(2,1)S(1)} %bitcast.205), kind=kOutput, calls=%fused_computation.7 | convolution fusion | flops 1612185600 | bytes 5767168 | tf_op jit(solution)/shard_map/erc,erd->cd/dot_general | solution.py:305
  127.1 7.7 %all-to-all-start.1 = ((bf16[16,32,1536]{2,1,0:T(8,128)(2,1)}), bf16[16,32,1536]{2,1,0:T(8,128)(2,1)}, u32[]{:S(2)}, u32[]{:S(2)}) async-start(bf16[16,32,1536]{2,1,0:T(8,128)(2,1)} %bitcast.200), calls=%async_computation.1 | async-start | bytes 3145728 | tf_op jit(solution)/shard_map/all_to_all | solution.py:353
  134.8 4.2 %fusion.42 = f32[512,1536]{1,0:T(8,128)S(1)} fusion(bf16[512,1024]{1,0:T(8,128)(2,1)} %get-tuple-element.51, bf16[1536,1024]{1,0:T(8,128)(2,1)} %bitcast.213), kind=kOutput, calls=%fused_computation.120 | convolution fusion | flops 1610612736 | bytes 7340032 | tf_op jit(solution)/shard_map/erh,edh->erd/dot_general | solution.py:365
  139.8 2.1 collective-permute-start.13
  142.2 3.1 %fusion.4 = bf16[512,1536]{1,0:T(8,128)(2,1)} fusion(f32[512,1536]{1,0:T(8,128)S(1)} %fusion.42, bf16[512,1024]{1,0:T(8,128)(2,1)S(1)} %get-tuple-element.50, bf16[1536,1024]{1,0:T(8,128)(2,1)S(1)} %bitcast.212), kind=kOutput, calls=%fused_computation.15 | convolution fusion | flops 1612185600 | bytes 8912896 | tf_op jit(solution)/shard_map/erh,edh->erd/dot_general | solution.py:366
  145.3 3.8 %convolution_convert_fusion = bf16[1536,2048]{1,0:T(8,128)(2,1)S(1)} fusion(bf16[512,1536]{1,0:T(8,128)(2,1)S(1)} %bitcast.203, bf16[1,512,1024]{2,1,0:T(8,128)(2,1)S(1)} %bitcast.217, bf16[1,512,1024]{2,1,0:T(8,128)(2,1)S(1)} %bitcast.218), kind=kOutput, calls=%fused_computation.3 | convolution fusion | flops 3228565504 | bytes 9961472 | tf_op jit(solution)/shard_map/erc,erk->ck/dot_general | solution.py:310
  150.7 2.6 %collective-permute-start.4 = (bf16[96,2048]{1,0:T(8,128)(2,1)S(1)}, bf16[96,2048]{1,0:T(8,128)(2,1)S(1)}, u32[]{:S(2)}, u32[]{:S(2)}) collective-permute-start(bf16[96,2048]{1,0:T(8,128)(2,1)S(1)} %get-tuple-element.44), channel_id=1, source_target_pairs={{0,32},{16,48},{32,64},{48,80},{64,96},{80,112},{96,0},{112,16},{1... | collective-permute-start | bytes 1179656 | tf_op jit(solution)/shard_map/ppermute | solution.py:176
  153.7 2.1 collective-permute-start.16
  156.7 3.0 %collective-permute-done = bf16[96,2048]{1,0:T(8,128)(2,1)S(1)} collective-permute-done((bf16[96,2048]{1,0:T(8,128)(2,1)S(1)}, bf16[96,2048]{1,0:T(8,128)(2,1)S(1)}, u32[]{:S(2)}, u32[]{:S(2)}) %collective-permute-start) | collective-permute-done | bytes 393248 | tf_op jit(solution)/shard_map/ppermute | solution.py:176
  160.4 7.6 %collective-permute-done.4 = bf16[96,2048]{1,0:T(8,128)(2,1)S(1)} collective-permute-done((bf16[96,2048]{1,0:T(8,128)(2,1)S(1)}, bf16[96,2048]{1,0:T(8,128)(2,1)S(1)}, u32[]{:S(2)}, u32[]{:S(2)}) %collective-permute-start.4) | collective-permute-done | bytes 393248 | tf_op jit(solution)/shard_map/ppermute | solution.py:176
  174.2 4.8 %collective-permute-done.16 = bf16[128,1536]{1,0:T(8,128)(2,1)S(1)} collective-permute-done((bf16[128,1536]{1,0:T(8,128)(2,1)S(1)}, bf16[128,1536]{1,0:T(8,128)(2,1)S(1)}, u32[]{:S(2)}, u32[]{:S(2)}) %collective-permute-start.16) | collective-permute-done | bytes 393248 | tf_op jit(solution)/shard_map/ppermute | solution.py:181
  183.2 12.9 %all-to-all-start.2 = ((bf16[16,32,1536]{2,1,0:T(8,128)(2,1)}), bf16[16,32,1536]{2,1,0:T(8,128)(2,1)}, u32[]{:S(2)}, u32[]{:S(2)}) async-start(bf16[16,32,1536]{2,1,0:T(8,128)(2,1)} %bitcast.199), calls=%async_computation.2 | async-start | bytes 3145728 | tf_op jit(solution)/shard_map/all_to_all | solution.py:368
  197.7 2.3 fusion.25
  200.0 4.3 %collective-permute-done.7 = bf16[192,2048]{1,0:T(8,128)(2,1)} collective-permute-done((bf16[192,2048]{1,0:T(8,128)(2,1)}, bf16[192,2048]{1,0:T(8,128)(2,1)}, u32[]{:S(2)}, u32[]{:S(2)}) %collective-permute-start.7) | collective-permute-done | bytes 786464 | tf_op jit(solution)/shard_map/ppermute | solution.py:181
  204.3 2.9 %fusion.11 = bf16[192,2048]{1,0:T(8,128)(2,1)} fusion(bf16[192,2048]{1,0:T(8,128)(2,1)} %collective-permute-done.7, bf16[192,2048]{1,0:T(8,128)(2,1)} %collective-permute-done.5, bf16[8,192,2048]{2,1,0:T(8,128)(2,1)} %bitcast.192, s32[]{:T(128)S(6)} %select_n.137), kind=kLoop, calls=%fused_computation.31 | loop fusion | flops 2359296 | bytes 3145732 | tf_op jit(solution)/shard_map/convert_element_type | solution.py:196
  207.2 1.9 fusion.1
  211.4 7.7 %all-to-all-done.2 = bf16[16,32,1536]{2,1,0:T(8,128)(2,1)} async-done(((bf16[16,32,1536]{2,1,0:T(8,128)(2,1)}), bf16[16,32,1536]{2,1,0:T(8,128)(2,1)}, u32[]{:S(2)}, u32[]{:S(2)}) %all-to-all-start.2) | async-done | bytes 1572896 | tf_op jit(solution)/shard_map/all_to_all | solution.py:368
  219.1 7.4 %all-to-all-start.3 = ((f32[128,1,192]{2,1,0:T(1,128)}), f32[128,1,192]{2,1,0:T(1,128)S(1)}, u32[]{:S(2)}, u32[]{:S(2)}) async-start(f32[128,1,192]{2,1,0:T(1,128)} %all_to_all.25), calls=%async_computation.3 | async-start | bytes 262144 | tf_op jit(solution)/shard_map/all_to_all | solution.py:406
  229.6 8.1 %all-to-all-done.3 = f32[128,1,192]{2,1,0:T(1,128)S(1)} async-done(((f32[128,1,192]{2,1,0:T(1,128)}), f32[128,1,192]{2,1,0:T(1,128)S(1)}, u32[]{:S(2)}, u32[]{:S(2)}) %all-to-all-start.3) | async-done | bytes 98336 | tf_op jit(solution)/shard_map/all_to_all | solution.py:406
  238.6 6.4 %all-to-all-start.4 = ((f32[128,1,192]{2,1,0:T(1,128)}), f32[128,1,192]{2,1,0:T(1,128)S(1)}, u32[]{:S(2)}, u32[]{:S(2)}) async-start(f32[128,1,192]{2,1,0:T(1,128)} %broadcast_in_dim.32), calls=%async_computation.4 | async-start | bytes 262144 | tf_op jit(solution)/shard_map/all_to_all | solution.py:412
  245.0 4.0 %fusion.5 = bf16[4,64,1536]{2,1,0:T(8,128)(2,1)} fusion(f32[4,128]{1,0:T(4,128)S(1)} %copy-done.12, s32[4,128]{1,0:T(4,128)S(1)} %copy-done.11, bf16[16,32,1536]{2,1,0:T(8,128)(2,1)} %all-to-all-done.1), kind=kOutput, calls=%fused_computation.18 | convolution fusion | flops 605978624 | bytes 2363392 | tf_op jit(solution)/shard_map/wze,wzi->wei/dot_general | solution.py:377
  249.0 4.0 %all-to-all-done.4 = f32[128,1,192]{2,1,0:T(1,128)S(1)} async-done(((f32[128,1,192]{2,1,0:T(1,128)}), f32[128,1,192]{2,1,0:T(1,128)S(1)}, u32[]{:S(2)}, u32[]{:S(2)}) %all-to-all-start.4) | async-done | bytes 98336 | tf_op jit(solution)/shard_map/all_to_all | solution.py:412
  254.5 2.1 fusion.13
  (119 shorter events, 35.5 us)
Async XLA Ops:
  2.9 4.7 %copy-start.7 = (s32[4,16,8]{1,2,0:T(8,128)S(1)}, s32[4,16,8]{1,2,0:T(8,128)}, u32[]{:S(2)}) copy-start(s32[4,16,8]{1,2,0:T(8,128)} %param.9) | copy-start | bytes 6148
  16.4 94.1 %all-to-all-start = ((bf16[16,64,1536]{2,1,0:T(8,128)(2,1)}), bf16[16,64,1536]{2,1,0:T(8,128)(2,1)}, u32[]{:S(2)}, u32[]{:S(2)}) async-start(bf16[16,64,1536]{2,1,0:T(8,128)(2,1)} %pad_maximum_fusion), calls=%async_computation | async-start | bytes 6291456 | tf_op jit(solution)/shard_map/all_to_all | solution.py:339
  25.2 87.6 %copy-start.9 = (s32[4,16,8]{2,1,0:T(8,128)}, s32[4,16,8]{2,1,0:T(8,128)S(1)}, u32[]{:S(2)}) copy-start(s32[4,16,8]{2,1,0:T(8,128)S(1)} %copy.55) | copy-start | bytes 6148
  127.1 56.1 %all-to-all-start.1 = ((bf16[16,32,1536]{2,1,0:T(8,128)(2,1)}), bf16[16,32,1536]{2,1,0:T(8,128)(2,1)}, u32[]{:S(2)}, u32[]{:S(2)}) async-start(bf16[16,32,1536]{2,1,0:T(8,128)(2,1)} %bitcast.200), calls=%async_computation.1 | async-start | bytes 3145728 | tf_op jit(solution)/shard_map/all_to_all | solution.py:353
  134.8 4.2 %copy-start.4 = (bf16[1024,1536]{1,0:T(8,128)(2,1)S(1)}, bf16[1024,1536]{1,0:T(8,128)(2,1)}, u32[]{:S(2)}) copy-start(bf16[1024,1536]{1,0:T(8,128)(2,1)} %convolution_convert_fusion.1) | copy-start | bytes 9437188
  139.0 3.2 %copy-start.14 = (bf16[8,192,1024]{2,1,0:T(8,128)(2,1)S(1)}, bf16[8,192,1024]{2,1,0:T(8,128)(2,1)}, u32[]{:S(2)}) copy-start(bf16[8,192,1024]{2,1,0:T(8,128)(2,1)} %get-tuple-element.10) | copy-start | bytes 9437188
  139.2 11.5 %collective-permute-start.9 = (bf16[64,1536]{1,0:T(8,128)(2,1)S(1)}, bf16[64,1536]{1,0:T(8,128)(2,1)S(1)}, u32[]{:S(2)}, u32[]{:S(2)}) collective-permute-start(bf16[64,1536]{1,0:T(8,128)(2,1)S(1)} %get-tuple-element.57), channel_id=1, source_target_pairs={{0,32},{16,48},{32,64},{48,80},{64,96},{80,112},{96,0},{112,16},{1... | collective-permute-start | bytes 589832 | tf_op jit(solution)/shard_map/ppermute | solution.py:176
  139.8 13.6 %collective-permute-start.13 = (bf16[64,1536]{1,0:T(8,128)(2,1)S(1)}, bf16[64,1536]{1,0:T(8,128)(2,1)S(1)}, u32[]{:S(2)}, u32[]{:S(2)}) collective-permute-start(bf16[64,1536]{1,0:T(8,128)(2,1)S(1)} %get-tuple-element.59), channel_id=1, source_target_pairs={{0,32},{16,48},{32,64},{48,80},{64,96},{80,112},{96,0},{112,16},{1... | collective-permute-start | bytes 589832 | tf_op jit(solution)/shard_map/ppermute | solution.py:176
  141.9 11.4 %collective-permute-start.15 = (bf16[64,1536]{1,0:T(8,128)(2,1)S(1)}, bf16[64,1536]{1,0:T(8,128)(2,1)S(1)}, u32[]{:S(2)}, u32[]{:S(2)}) collective-permute-start(bf16[64,1536]{1,0:T(8,128)(2,1)S(1)} %get-tuple-element.61), channel_id=1, source_target_pairs={{0,96},{16,112},{32,0},{48,16},{64,32},{80,48},{96,64},{112,80},{1... | collective-permute-start | bytes 589832 | tf_op jit(solution)/shard_map/ppermute | solution.py:177
  141.9 11.5 %collective-permute-start.11 = (bf16[64,1536]{1,0:T(8,128)(2,1)S(1)}, bf16[64,1536]{1,0:T(8,128)(2,1)S(1)}, u32[]{:S(2)}, u32[]{:S(2)}) collective-permute-start(bf16[64,1536]{1,0:T(8,128)(2,1)S(1)} %get-tuple-element.63), channel_id=1, source_target_pairs={{0,96},{16,112},{32,0},{48,16},{64,32},{80,48},{96,64},{112,80},{1... | collective-permute-start | bytes 589832 | tf_op jit(solution)/shard_map/ppermute | solution.py:177
  142.2 3.1 %copy-start.17 = (bf16[512,1024]{1,0:T(8,128)(2,1)S(1)}, bf16[512,1024]{1,0:T(8,128)(2,1)}, u32[]{:S(2)}) copy-start(bf16[512,1024]{1,0:T(8,128)(2,1)} %get-tuple-element.51) | copy-start | bytes 3145732
  149.1 21.4 %copy-start.3 = (bf16[1536,2048]{1,0:T(8,128)(2,1)}, bf16[1536,2048]{1,0:T(8,128)(2,1)S(1)}, u32[]{:S(2)}) copy-start(bf16[1536,2048]{1,0:T(8,128)(2,1)S(1)} %convolution_convert_fusion) | copy-start | bytes 18874372
  149.4 10.2 %collective-permute-start = (bf16[96,2048]{1,0:T(8,128)(2,1)S(1)}, bf16[96,2048]{1,0:T(8,128)(2,1)S(1)}, u32[]{:S(2)}, u32[]{:S(2)}) collective-permute-start(bf16[96,2048]{1,0:T(8,128)(2,1)S(1)} %get-tuple-element.42), channel_id=1, source_target_pairs={{0,32},{16,48},{32,64},{48,80},{64,96},{80,112},{96,0},{112,16},{1... | collective-permute-start | bytes 1179656 | tf_op jit(solution)/shard_map/ppermute | solution.py:176
  150.7 17.4 %collective-permute-start.4 = (bf16[96,2048]{1,0:T(8,128)(2,1)S(1)}, bf16[96,2048]{1,0:T(8,128)(2,1)S(1)}, u32[]{:S(2)}, u32[]{:S(2)}) collective-permute-start(bf16[96,2048]{1,0:T(8,128)(2,1)S(1)} %get-tuple-element.44), channel_id=1, source_target_pairs={{0,32},{16,48},{32,64},{48,80},{64,96},{80,112},{96,0},{112,16},{1... | collective-permute-start | bytes 1179656 | tf_op jit(solution)/shard_map/ppermute | solution.py:176
  153.3 15.9 %collective-permute-start.6 = (bf16[96,2048]{1,0:T(8,128)(2,1)S(1)}, bf16[96,2048]{1,0:T(8,128)(2,1)S(1)}, u32[]{:S(2)}, u32[]{:S(2)}) collective-permute-start(bf16[96,2048]{1,0:T(8,128)(2,1)S(1)} %get-tuple-element.46), channel_id=1, source_target_pairs={{0,96},{16,112},{32,0},{48,16},{64,32},{80,48},{96,64},{112,80},{1... | collective-permute-start | bytes 1179656 | tf_op jit(solution)/shard_map/ppermute | solution.py:177
  153.3 17.2 %collective-permute-start.2 = (bf16[96,2048]{1,0:T(8,128)(2,1)S(1)}, bf16[96,2048]{1,0:T(8,128)(2,1)S(1)}, u32[]{:S(2)}, u32[]{:S(2)}) collective-permute-start(bf16[96,2048]{1,0:T(8,128)(2,1)S(1)} %get-tuple-element.48), channel_id=1, source_target_pairs={{0,96},{16,112},{32,0},{48,16},{64,32},{80,48},{96,64},{112,80},{1... | collective-permute-start | bytes 1179656 | tf_op jit(solution)/shard_map/ppermute | solution.py:177
  153.7 25.3 %collective-permute-start.16 = (bf16[128,1536]{1,0:T(8,128)(2,1)S(1)}, bf16[128,1536]{1,0:T(8,128)(2,1)S(1)}, u32[]{:S(2)}, u32[]{:S(2)}) collective-permute-start(bf16[128,1536]{1,0:T(8,128)(2,1)S(1)} %pad_maximum_fusion.8), channel_id=1, source_target_pairs={{0,96},{16,112},{32,0},{48,16},{64,32},{80,48},{96,64},{112,80},{1... | collective-permute-start | bytes 1179656 | tf_op jit(solution)/shard_map/ppermute | solution.py:181
  159.6 20.7 %collective-permute-start.14 = (bf16[128,1536]{1,0:T(8,128)(2,1)S(1)}, bf16[128,1536]{1,0:T(8,128)(2,1)S(1)}, u32[]{:S(2)}, u32[]{:S(2)}) collective-permute-start(bf16[128,1536]{1,0:T(8,128)(2,1)S(1)} %pad_maximum_fusion.7), channel_id=1, source_target_pairs={{0,32},{16,48},{32,64},{48,80},{64,96},{80,112},{96,0},{112,16},{1... | collective-permute-start | bytes 1179656 | tf_op jit(solution)/shard_map/ppermute | solution.py:180
  168.1 28.1 %collective-permute-start.12 = (bf16[128,1536]{1,0:T(8,128)(2,1)S(1)}, bf16[128,1536]{1,0:T(8,128)(2,1)S(1)}, u32[]{:S(2)}, u32[]{:S(2)}) collective-permute-start(bf16[128,1536]{1,0:T(8,128)(2,1)S(1)} %pad_maximum_fusion.6), channel_id=1, source_target_pairs={{0,96},{16,112},{32,0},{48,16},{64,32},{80,48},{96,64},{112,80},{1... | collective-permute-start | bytes 1179656 | tf_op jit(solution)/shard_map/ppermute | solution.py:181
  169.2 27.3 %collective-permute-start.10 = (bf16[128,1536]{1,0:T(8,128)(2,1)}, bf16[128,1536]{1,0:T(8,128)(2,1)}, u32[]{:S(2)}, u32[]{:S(2)}) collective-permute-start(bf16[128,1536]{1,0:T(8,128)(2,1)} %pad_maximum_fusion.5), channel_id=1, source_target_pairs={{0,32},{16,48},{32,64},{48,80},{64,96},{80,112},{96,0},{112,16},{1... | collective-permute-start | bytes 1179656 | tf_op jit(solution)/shard_map/ppermute | solution.py:180
  172.0 32.3 %collective-permute-start.7 = (bf16[192,2048]{1,0:T(8,128)(2,1)}, bf16[192,2048]{1,0:T(8,128)(2,1)}, u32[]{:S(2)}, u32[]{:S(2)}) collective-permute-start(bf16[192,2048]{1,0:T(8,128)(2,1)} %pad_maximum_fusion.4), channel_id=1, source_target_pairs={{0,96},{16,112},{32,0},{48,16},{64,32},{80,48},{96,64},{112,80},{1... | collective-permute-start | bytes 2359304 | tf_op jit(solution)/shard_map/ppermute | solution.py:181
  178.9 25.4 %collective-permute-start.5 = (bf16[192,2048]{1,0:T(8,128)(2,1)}, bf16[192,2048]{1,0:T(8,128)(2,1)}, u32[]{:S(2)}, u32[]{:S(2)}) collective-permute-start(bf16[192,2048]{1,0:T(8,128)(2,1)} %pad_maximum_fusion.3), channel_id=1, source_target_pairs={{0,32},{16,48},{32,64},{48,80},{64,96},{80,112},{96,0},{112,16},{1... | collective-permute-start | bytes 2359304 | tf_op jit(solution)/shard_map/ppermute | solution.py:180
  181.3 16.4 %collective-permute-start.17 = (bf16[128,1536]{1,0:T(8,128)(2,1)}, bf16[128,1536]{1,0:T(8,128)(2,1)}, u32[]{:S(2)}, u32[]{:S(2)}) collective-permute-start(bf16[128,1536]{1,0:T(8,128)(2,1)} %fusion.22), channel_id=1, source_target_pairs={{0,16},{16,0},{32,48},{48,32},{64,80},{80,64},{96,112},{112,96},{1... | collective-permute-start | bytes 1179656 | tf_op jit(solution)/shard_map/ppermute | solution.py:196
  183.2 35.9 %all-to-all-start.2 = ((bf16[16,32,1536]{2,1,0:T(8,128)(2,1)}), bf16[16,32,1536]{2,1,0:T(8,128)(2,1)}, u32[]{:S(2)}, u32[]{:S(2)}) async-start(bf16[16,32,1536]{2,1,0:T(8,128)(2,1)} %bitcast.199), calls=%async_computation.2 | async-start | bytes 3145728 | tf_op jit(solution)/shard_map/all_to_all | solution.py:368
  196.2 58.3 %collective-permute-start.3 = (bf16[192,2048]{1,0:T(8,128)(2,1)}, bf16[192,2048]{1,0:T(8,128)(2,1)S(1)}, u32[]{:S(2)}, u32[]{:S(2)}) collective-permute-start(bf16[192,2048]{1,0:T(8,128)(2,1)} %pad_maximum_fusion.2), channel_id=1, source_target_pairs={{0,96},{16,112},{32,0},{48,16},{64,32},{80,48},{96,64},{112,80},{1... | collective-permute-start | bytes 2359304 | tf_op jit(solution)/shard_map/ppermute | solution.py:181
  196.5 57.9 %collective-permute-start.1 = (bf16[192,2048]{1,0:T(8,128)(2,1)}, bf16[192,2048]{1,0:T(8,128)(2,1)}, u32[]{:S(2)}, u32[]{:S(2)}) collective-permute-start(bf16[192,2048]{1,0:T(8,128)(2,1)} %pad_maximum_fusion.1), channel_id=1, source_target_pairs={{0,32},{16,48},{32,64},{48,80},{64,96},{80,112},{96,0},{112,16},{1... | collective-permute-start | bytes 2359304 | tf_op jit(solution)/shard_map/ppermute | solution.py:180
  207.2 47.2 %collective-permute-start.8 = (bf16[192,2048]{1,0:T(8,128)(2,1)}, bf16[192,2048]{1,0:T(8,128)(2,1)}, u32[]{:S(2)}, u32[]{:S(2)}) collective-permute-start(bf16[192,2048]{1,0:T(8,128)(2,1)} %fusion.11), channel_id=1, source_target_pairs={{0,16},{16,0},{32,48},{48,32},{64,80},{80,64},{96,112},{112,96},{1... | collective-permute-start | bytes 2359304 | tf_op jit(solution)/shard_map/ppermute | solution.py:196
  209.1 17.4 %copy-start.11 = (s32[4,128]{1,0:T(4,128)S(1)}, s32[4,128]{1,0:T(4,128)}, u32[]{:S(2)}) copy-start(s32[4,128]{1,0:T(4,128)} %eq.41) | copy-start | bytes 6148
  210.3 18.0 %copy-start.8 = (bf16[1536,16]{0,1:T(8,128)(2,1)S(1)}, bf16[1536,16]{0,1:T(8,128)(2,1)}, u32[]{:S(2)}) copy-start(bf16[1536,16]{0,1:T(8,128)(2,1)} %param.10) | copy-start | bytes 147460
  219.1 18.6 %all-to-all-start.3 = ((f32[128,1,192]{2,1,0:T(1,128)}), f32[128,1,192]{2,1,0:T(1,128)S(1)}, u32[]{:S(2)}, u32[]{:S(2)}) async-start(f32[128,1,192]{2,1,0:T(1,128)} %all_to_all.25), calls=%async_computation.3 | async-start | bytes 262144 | tf_op jit(solution)/shard_map/all_to_all | solution.py:406
  228.3 16.7 %copy-start.12 = (f32[4,128]{1,0:T(4,128)S(1)}, f32[4,128]{1,0:T(4,128)}, u32[]{:S(2)}) copy-start(f32[4,128]{1,0:T(4,128)} %mul.88) | copy-start | bytes 6148
  238.6 14.4 %all-to-all-start.4 = ((f32[128,1,192]{2,1,0:T(1,128)}), f32[128,1,192]{2,1,0:T(1,128)S(1)}, u32[]{:S(2)}, u32[]{:S(2)}) async-start(f32[128,1,192]{2,1,0:T(1,128)} %broadcast_in_dim.32), calls=%async_computation.4 | async-start | bytes 262144 | tf_op jit(solution)/shard_map/all_to_all | solution.py:412
  (9 other events, 19.6 us)

commit v9 on v8

--- a/solution.py
+++ b/solution.py
@@ -231,11 +231,13 @@
         local = pltpu.make_async_copy(shards[a], outs[a].at[me], local_sem.at[a])
         local.start()
         locals_.append(local)
+    across = [send(a, 2, shards[a], me, spans[a][0], partner) for a in range(count)]
+    for a in range(count):
         whole = spans[a][0]
         first += [
             send(a, 0, shards[a], me, whole, right),
             send(a, 1, shards[a], me, whole, left),
-            send(a, 2, shards[a], me, whole, partner),
+            across[a],
         ]
     mate = partner
     for a in range(count):

time: 261 us -> 261 us (level)
  no operation moved by 1% of the time
where the time goes in v9:
time: 261 us; the launch traced here: 258 us
  Pallas kernels  83.6 us (32%)
  starting transfers between devices  58.7 us (22%)
  waiting for transfers between devices  40.6 us (16%)
  matrix products  33.4 us (13%)
  local copies, waits for them, and re-layouts  21.1 us (8%)
  other arithmetic  19.3 us (7%)
    pallas_call x1, Pallas kernels, dp_gather_kernel(): pl.pallas_call(functools.partial(_ring_gather_kernel, n), out_shape=[jax....  83.6 us
    all_to_all x1, starting transfers between devices, body(): lax.all_to_all(d_rows.reshape(expert_count_axis, -1, model_width), 'exper...  13 us
    ppermute x4, waiting for transfers between devices, x_ring_scatter(): low = lax.ppermute(blocks[2][:h].astype(jnp.bfloat16), 'dp', _x_shift(n, 1))  10.6 us
    ppermute x4, waiting for transfers between devices, x_ring_scatter(): lax.ppermute(to_left.astype(jnp.bfloat16), 'dp', _x_shift(n, -1))  9.09 us
    all_to_all x1, starting transfers between devices, body(): lax.all_to_all(jnp.concatenate([picked, scaled_cot], axis=1), 'expert', 0...  8.63 us
    all_to_all x1, waiting for transfers between devices, body(): lax.all_to_all(router_full.reshape(devices, -1), ('dp', 'expert'), 0, 0,...  8.13 us
    all_to_all x1, waiting for transfers between devices, body(): lax.all_to_all(d_rows.reshape(expert_count_axis, -1, model_width), 'exper...  7.73 us
    all_to_all x1, starting transfers between devices, body(): lax.all_to_all(expert_out.reshape(expert_count_axis, -1, model_width), 'e...  7.7 us
  transfers between devices with their start and end apart: 23, of which 8 were waited for; matrix products, arithmetic and copies ran while one was open for 14% of the time, Pallas kernels for 32%

profile of v9, /device:TPU:5, one launch (start us, length us, event | category | flops | bytes accessed | tf_op | source)
XLA Modules:
  0.0 257.8 jit_solution(15245117454326491744)
XLA Ops:
  2.9 4.5 %gather_fusion.2 = f32[512]{0:T(512)S(1)} fusion(f32[16,256]{1,0:T(8,128)S(1)} %bitcast.187, s32[512]{0:T(512)S(1)} %reshape.317), kind=kCustom, calls=%fused_computation.2 | custom fusion | bytes 8192 | tf_op jit(solution)/shard_map/jit(take_along_axis)/gather | solution.py:332
  7.9 2.9 %gather_fusion = bf16[512,1536]{1,0:T(8,128)(2,1)} fusion(bf16[256,1536]{1,0:T(8,128)(2,1)S(1)} %copy-done, s32[1024]{0:T(1024)S(1)} %pad_clamp_fusion), kind=kCustom, calls=%fused_computation | custom fusion | bytes 3147776 | tf_op jit(solution)/shard_map/gather | solution.py:331
  10.9 2.1 gather_fusion.1
  14.4 1.9 pad_maximum_fusion
  16.4 8.6 %all-to-all-start = ((bf16[16,64,1536]{2,1,0:T(8,128)(2,1)}), bf16[16,64,1536]{2,1,0:T(8,128)(2,1)}, u32[]{:S(2)}, u32[]{:S(2)}) async-start(bf16[16,64,1536]{2,1,0:T(8,128)(2,1)} %pad_maximum_fusion), calls=%async_computation | async-start | bytes 6291456 | tf_op jit(solution)/shard_map/all_to_all | solution.py:341
  26.8 83.6 %shard_map.118 = (bf16[8,192,1024]{2,1,0:T(8,128)(2,1)}, bf16[8,192,1024]{2,1,0:T(8,128)(2,1)}, bf16[8,128,1536]{2,1,0:T(8,128)(2,1)}) custom-call(bf16[192,1024]{1,0:T(8,128)(2,1)} %bitcast.206, bf16[192,1024]{1,0:T(8,128)(2,1)} %bitcast.207, bf16[128,1536]{1,0:T(8,128)(2,1)} %bitcast.208), custom_call_target="tpu_custom_call" | custom-call | tf_op jit(solution)/shard_map/pallas_call | solution.py:281
  110.5 2.2 fusion.39
  117.1 3.5 %multiply_convert_fusion = (bf16[512,1024]{1,0:T(8,128)(2,1)S(1)}, bf16[512,1024]{1,0:T(8,128)(2,1)}, bf16[512,1024]{1,0:T(8,128)(2,1)S(1)}) fusion(f32[512,1024]{1,0:T(8,128)S(1)} %fusion.40, f32[512,1024]{1,0:T(8,128)S(1)} %fusion.41, bf16[512,1536]{1,0:T(8,128)(2,1)S(1)} %bitcast.204, bf16[1024,1536]{1,0:T(8,128)(2,1)S(1)} %bitcast.215), kind=kOutput, calls=%fused_computation.24 | convolution fusion | flops 1618477056 | bytes 12058624 | tf_op jit(solution)/shard_map/erd,ehd->erh/dot_general | solution.py:360
  120.6 3.0 %convolution_convert_fusion.2 = bf16[512,1536]{1,0:T(8,128)(2,1)} fusion(bf16[512,1024]{1,0:T(8,128)(2,1)S(1)} %get-tuple-element.52, bf16[1024,1536]{1,0:T(8,128)(2,1)S(1)} %bitcast.216), kind=kOutput, calls=%fused_computation.16 | convolution fusion | flops 1611399168 | bytes 5767168 | tf_op jit(solution)/shard_map/erh,ehd->erd/dot_general | solution.py:352
  123.6 3.6 %convolution_convert_fusion.1 = bf16[1024,1536]{1,0:T(8,128)(2,1)} fusion(bf16[512,1024]{1,0:T(8,128)(2,1)S(1)} %get-tuple-element.52, bf16[512,1536]{1,0:T(8,128)(2,1)S(1)} %bitcast.205), kind=kOutput, calls=%fused_computation.7 | convolution fusion | flops 1612185600 | bytes 5767168 | tf_op jit(solution)/shard_map/erc,erd->cd/dot_general | solution.py:307
  127.1 7.7 %all-to-all-start.1 = ((bf16[16,32,1536]{2,1,0:T(8,128)(2,1)}), bf16[16,32,1536]{2,1,0:T(8,128)(2,1)}, u32[]{:S(2)}, u32[]{:S(2)}) async-start(bf16[16,32,1536]{2,1,0:T(8,128)(2,1)} %bitcast.200), calls=%async_computation.1 | async-start | bytes 3145728 | tf_op jit(solution)/shard_map/all_to_all | solution.py:355
  134.8 4.2 %fusion.42 = f32[512,1536]{1,0:T(8,128)S(1)} fusion(bf16[512,1024]{1,0:T(8,128)(2,1)} %get-tuple-element.51, bf16[1536,1024]{1,0:T(8,128)(2,1)} %bitcast.213), kind=kOutput, calls=%fused_computation.120 | convolution fusion | flops 1610612736 | bytes 7340032 | tf_op jit(solution)/shard_map/erh,edh->erd/dot_general | solution.py:367
  139.8 2.1 collective-permute-start.13
  142.2 3.1 %fusion.4 = bf16[512,1536]{1,0:T(8,128)(2,1)} fusion(f32[512,1536]{1,0:T(8,128)S(1)} %fusion.42, bf16[512,1024]{1,0:T(8,128)(2,1)S(1)} %get-tuple-element.50, bf16[1536,1024]{1,0:T(8,128)(2,1)S(1)} %bitcast.212), kind=kOutput, calls=%fused_computation.15 | convolution fusion | flops 1612185600 | bytes 8912896 | tf_op jit(solution)/shard_map/erh,edh->erd/dot_general | solution.py:368
  145.3 3.8 %convolution_convert_fusion = bf16[1536,2048]{1,0:T(8,128)(2,1)S(1)} fusion(bf16[512,1536]{1,0:T(8,128)(2,1)S(1)} %bitcast.203, bf16[1,512,1024]{2,1,0:T(8,128)(2,1)S(1)} %bitcast.217, bf16[1,512,1024]{2,1,0:T(8,128)(2,1)S(1)} %bitcast.218), kind=kOutput, calls=%fused_computation.3 | convolution fusion | flops 3228565504 | bytes 9961472 | tf_op jit(solution)/shard_map/erc,erk->ck/dot_general | solution.py:312
  150.7 2.6 %collective-permute-start.4 = (bf16[96,2048]{1,0:T(8,128)(2,1)S(1)}, bf16[96,2048]{1,0:T(8,128)(2,1)S(1)}, u32[]{:S(2)}, u32[]{:S(2)}) collective-permute-start(bf16[96,2048]{1,0:T(8,128)(2,1)S(1)} %get-tuple-element.44), channel_id=1, source_target_pairs={{0,32},{16,48},{32,64},{48,80},{64,96},{80,112},{96,0},{112,16},{1... | collective-permute-start | bytes 1179656 | tf_op jit(solution)/shard_map/ppermute | solution.py:176
  153.7 2.1 collective-permute-start.16
  156.6 3.0 %collective-permute-done = bf16[96,2048]{1,0:T(8,128)(2,1)S(1)} collective-permute-done((bf16[96,2048]{1,0:T(8,128)(2,1)S(1)}, bf16[96,2048]{1,0:T(8,128)(2,1)S(1)}, u32[]{:S(2)}, u32[]{:S(2)}) %collective-permute-start) | collective-permute-done | bytes 393248 | tf_op jit(solution)/shard_map/ppermute | solution.py:176
  160.4 7.6 %collective-permute-done.4 = bf16[96,2048]{1,0:T(8,128)(2,1)S(1)} collective-permute-done((bf16[96,2048]{1,0:T(8,128)(2,1)S(1)}, bf16[96,2048]{1,0:T(8,128)(2,1)S(1)}, u32[]{:S(2)}, u32[]{:S(2)}) %collective-permute-start.4) | collective-permute-done | bytes 393248 | tf_op jit(solution)/shard_map/ppermute | solution.py:176
  174.2 4.8 %collective-permute-done.16 = bf16[128,1536]{1,0:T(8,128)(2,1)S(1)} collective-permute-done((bf16[128,1536]{1,0:T(8,128)(2,1)S(1)}, bf16[128,1536]{1,0:T(8,128)(2,1)S(1)}, u32[]{:S(2)}, u32[]{:S(2)}) %collective-permute-start.16) | collective-permute-done | bytes 393248 | tf_op jit(solution)/shard_map/ppermute | solution.py:181
  183.2 13.0 %all-to-all-start.2 = ((bf16[16,32,1536]{2,1,0:T(8,128)(2,1)}), bf16[16,32,1536]{2,1,0:T(8,128)(2,1)}, u32[]{:S(2)}, u32[]{:S(2)}) async-start(bf16[16,32,1536]{2,1,0:T(8,128)(2,1)} %bitcast.199), calls=%async_computation.2 | async-start | bytes 3145728 | tf_op jit(solution)/shard_map/all_to_all | solution.py:370
  197.7 2.3 fusion.25
  200.0 4.3 %collective-permute-done.7 = bf16[192,2048]{1,0:T(8,128)(2,1)} collective-permute-done((bf16[192,2048]{1,0:T(8,128)(2,1)}, bf16[192,2048]{1,0:T(8,128)(2,1)}, u32[]{:S(2)}, u32[]{:S(2)}) %collective-permute-start.7) | collective-permute-done | bytes 786464 | tf_op jit(solution)/shard_map/ppermute | solution.py:181
  204.3 2.9 %fusion.11 = bf16[192,2048]{1,0:T(8,128)(2,1)} fusion(bf16[192,2048]{1,0:T(8,128)(2,1)} %collective-permute-done.7, bf16[192,2048]{1,0:T(8,128)(2,1)} %collective-permute-done.5, bf16[8,192,2048]{2,1,0:T(8,128)(2,1)} %bitcast.192, s32[]{:T(128)S(6)} %select_n.137), kind=kLoop, calls=%fused_computation.31 | loop fusion | flops 2359296 | bytes 3145732 | tf_op jit(solution)/shard_map/convert_element_type | solution.py:196
  207.2 1.9 fusion.1
  211.4 7.7 %all-to-all-done.2 = bf16[16,32,1536]{2,1,0:T(8,128)(2,1)} async-done(((bf16[16,32,1536]{2,1,0:T(8,128)(2,1)}), bf16[16,32,1536]{2,1,0:T(8,128)(2,1)}, u32[]{:S(2)}, u32[]{:S(2)}) %all-to-all-start.2) | async-done | bytes 1572896 | tf_op jit(solution)/shard_map/all_to_all | solution.py:370
  219.1 7.4 %all-to-all-start.3 = ((f32[128,1,192]{2,1,0:T(1,128)}), f32[128,1,192]{2,1,0:T(1,128)S(1)}, u32[]{:S(2)}, u32[]{:S(2)}) async-start(f32[128,1,192]{2,1,0:T(1,128)} %all_to_all.25), calls=%async_computation.3 | async-start | bytes 262144 | tf_op jit(solution)/shard_map/all_to_all | solution.py:408
  229.6 8.1 %all-to-all-done.3 = f32[128,1,192]{2,1,0:T(1,128)S(1)} async-done(((f32[128,1,192]{2,1,0:T(1,128)}), f32[128,1,192]{2,1,0:T(1,128)S(1)}, u32[]{:S(2)}, u32[]{:S(2)}) %all-to-all-start.3) | async-done | bytes 98336 | tf_op jit(solution)/shard_map/all_to_all | solution.py:408
  238.6 6.4 %all-to-all-start.4 = ((f32[128,1,192]{2,1,0:T(1,128)}), f32[128,1,192]{2,1,0:T(1,128)S(1)}, u32[]{:S(2)}, u32[]{:S(2)}) async-start(f32[128,1,192]{2,1,0:T(1,128)} %broadcast_in_dim.32), calls=%async_computation.4 | async-start | bytes 262144 | tf_op jit(solution)/shard_map/all_to_all | solution.py:414
  245.0 4.0 %fusion.5 = bf16[4,64,1536]{2,1,0:T(8,128)(2,1)} fusion(f32[4,128]{1,0:T(4,128)S(1)} %copy-done.12, s32[4,128]{1,0:T(4,128)S(1)} %copy-done.11, bf16[16,32,1536]{2,1,0:T(8,128)(2,1)} %all-to-all-done.1), kind=kOutput, calls=%fused_computation.18 | convolution fusion | flops 605978624 | bytes 2363392 | tf_op jit(solution)/shard_map/wze,wzi->wei/dot_general | solution.py:379
  249.0 4.0 %all-to-all-done.4 = f32[128,1,192]{2,1,0:T(1,128)S(1)} async-done(((f32[128,1,192]{2,1,0:T(1,128)}), f32[128,1,192]{2,1,0:T(1,128)S(1)}, u32[]{:S(2)}, u32[]{:S(2)}) %all-to-all-start.4) | async-done | bytes 98336 | tf_op jit(solution)/shard_map/all_to_all | solution.py:414
  254.5 2.1 fusion.13
  (119 shorter events, 35.5 us)
Async XLA Ops:
  2.9 4.7 %copy-start.7 = (s32[4,16,8]{1,2,0:T(8,128)S(1)}, s32[4,16,8]{1,2,0:T(8,128)}, u32[]{:S(2)}) copy-start(s32[4,16,8]{1,2,0:T(8,128)} %param.9) | copy-start | bytes 6148
  16.4 94.1 %all-to-all-start = ((bf16[16,64,1536]{2,1,0:T(8,128)(2,1)}), bf16[16,64,1536]{2,1,0:T(8,128)(2,1)}, u32[]{:S(2)}, u32[]{:S(2)}) async-start(bf16[16,64,1536]{2,1,0:T(8,128)(2,1)} %pad_maximum_fusion), calls=%async_computation | async-start | bytes 6291456 | tf_op jit(solution)/shard_map/all_to_all | solution.py:341
  25.2 87.6 %copy-start.9 = (s32[4,16,8]{2,1,0:T(8,128)}, s32[4,16,8]{2,1,0:T(8,128)S(1)}, u32[]{:S(2)}) copy-start(s32[4,16,8]{2,1,0:T(8,128)S(1)} %copy.55) | copy-start | bytes 6148
  127.1 56.1 %all-to-all-start.1 = ((bf16[16,32,1536]{2,1,0:T(8,128)(2,1)}), bf16[16,32,1536]{2,1,0:T(8,128)(2,1)}, u32[]{:S(2)}, u32[]{:S(2)}) async-start(bf16[16,32,1536]{2,1,0:T(8,128)(2,1)} %bitcast.200), calls=%async_computation.1 | async-start | bytes 3145728 | tf_op jit(solution)/shard_map/all_to_all | solution.py:355
  134.8 4.2 %copy-start.4 = (bf16[1024,1536]{1,0:T(8,128)(2,1)S(1)}, bf16[1024,1536]{1,0:T(8,128)(2,1)}, u32[]{:S(2)}) copy-start(bf16[1024,1536]{1,0:T(8,128)(2,1)} %convolution_convert_fusion.1) | copy-start | bytes 9437188
  139.0 3.2 %copy-start.14 = (bf16[8,192,1024]{2,1,0:T(8,128)(2,1)S(1)}, bf16[8,192,1024]{2,1,0:T(8,128)(2,1)}, u32[]{:S(2)}) copy-start(bf16[8,192,1024]{2,1,0:T(8,128)(2,1)} %get-tuple-element.10) | copy-start | bytes 9437188
  139.2 11.5 %collective-permute-start.9 = (bf16[64,1536]{1,0:T(8,128)(2,1)S(1)}, bf16[64,1536]{1,0:T(8,128)(2,1)S(1)}, u32[]{:S(2)}, u32[]{:S(2)}) collective-permute-start(bf16[64,1536]{1,0:T(8,128)(2,1)S(1)} %get-tuple-element.57), channel_id=1, source_target_pairs={{0,32},{16,48},{32,64},{48,80},{64,96},{80,112},{96,0},{112,16},{1... | collective-permute-start | bytes 589832 | tf_op jit(solution)/shard_map/ppermute | solution.py:176
  139.8 13.6 %collective-permute-start.13 = (bf16[64,1536]{1,0:T(8,128)(2,1)S(1)}, bf16[64,1536]{1,0:T(8,128)(2,1)S(1)}, u32[]{:S(2)}, u32[]{:S(2)}) collective-permute-start(bf16[64,1536]{1,0:T(8,128)(2,1)S(1)} %get-tuple-element.59), channel_id=1, source_target_pairs={{0,32},{16,48},{32,64},{48,80},{64,96},{80,112},{96,0},{112,16},{1... | collective-permute-start | bytes 589832 | tf_op jit(solution)/shard_map/ppermute | solution.py:176
  141.9 11.4 %collective-permute-start.15 = (bf16[64,1536]{1,0:T(8,128)(2,1)S(1)}, bf16[64,1536]{1,0:T(8,128)(2,1)S(1)}, u32[]{:S(2)}, u32[]{:S(2)}) collective-permute-start(bf16[64,1536]{1,0:T(8,128)(2,1)S(1)} %get-tuple-element.61), channel_id=1, source_target_pairs={{0,96},{16,112},{32,0},{48,16},{64,32},{80,48},{96,64},{112,80},{1... | collective-permute-start | bytes 589832 | tf_op jit(solution)/shard_map/ppermute | solution.py:177
  141.9 11.5 %collective-permute-start.11 = (bf16[64,1536]{1,0:T(8,128)(2,1)S(1)}, bf16[64,1536]{1,0:T(8,128)(2,1)S(1)}, u32[]{:S(2)}, u32[]{:S(2)}) collective-permute-start(bf16[64,1536]{1,0:T(8,128)(2,1)S(1)} %get-tuple-element.63), channel_id=1, source_target_pairs={{0,96},{16,112},{32,0},{48,16},{64,32},{80,48},{96,64},{112,80},{1... | collective-permute-start | bytes 589832 | tf_op jit(solution)/shard_map/ppermute | solution.py:177
  142.2 3.1 %copy-start.17 = (bf16[512,1024]{1,0:T(8,128)(2,1)S(1)}, bf16[512,1024]{1,0:T(8,128)(2,1)}, u32[]{:S(2)}) copy-start(bf16[512,1024]{1,0:T(8,128)(2,1)} %get-tuple-element.51) | copy-start | bytes 3145732
  149.1 21.4 %copy-start.3 = (bf16[1536,2048]{1,0:T(8,128)(2,1)}, bf16[1536,2048]{1,0:T(8,128)(2,1)S(1)}, u32[]{:S(2)}) copy-start(bf16[1536,2048]{1,0:T(8,128)(2,1)S(1)} %convolution_convert_fusion) | copy-start | bytes 18874372
  149.4 10.2 %collective-permute-start = (bf16[96,2048]{1,0:T(8,128)(2,1)S(1)}, bf16[96,2048]{1,0:T(8,128)(2,1)S(1)}, u32[]{:S(2)}, u32[]{:S(2)}) collective-permute-start(bf16[96,2048]{1,0:T(8,128)(2,1)S(1)} %get-tuple-element.42), channel_id=1, source_target_pairs={{0,32},{16,48},{32,64},{48,80},{64,96},{80,112},{96,0},{112,16},{1... | collective-permute-start | bytes 1179656 | tf_op jit(solution)/shard_map/ppermute | solution.py:176
  150.7 17.4 %collective-permute-start.4 = (bf16[96,2048]{1,0:T(8,128)(2,1)S(1)}, bf16[96,2048]{1,0:T(8,128)(2,1)S(1)}, u32[]{:S(2)}, u32[]{:S(2)}) collective-permute-start(bf16[96,2048]{1,0:T(8,128)(2,1)S(1)} %get-tuple-element.44), channel_id=1, source_target_pairs={{0,32},{16,48},{32,64},{48,80},{64,96},{80,112},{96,0},{112,16},{1... | collective-permute-start | bytes 1179656 | tf_op jit(solution)/shard_map/ppermute | solution.py:176
  153.3 15.9 %collective-permute-start.6 = (bf16[96,2048]{1,0:T(8,128)(2,1)S(1)}, bf16[96,2048]{1,0:T(8,128)(2,1)S(1)}, u32[]{:S(2)}, u32[]{:S(2)}) collective-permute-start(bf16[96,2048]{1,0:T(8,128)(2,1)S(1)} %get-tuple-element.46), channel_id=1, source_target_pairs={{0,96},{16,112},{32,0},{48,16},{64,32},{80,48},{96,64},{112,80},{1... | collective-permute-start | bytes 1179656 | tf_op jit(solution)/shard_map/ppermute | solution.py:177
  153.3 17.2 %collective-permute-start.2 = (bf16[96,2048]{1,0:T(8,128)(2,1)S(1)}, bf16[96,2048]{1,0:T(8,128)(2,1)S(1)}, u32[]{:S(2)}, u32[]{:S(2)}) collective-permute-start(bf16[96,2048]{1,0:T(8,128)(2,1)S(1)} %get-tuple-element.48), channel_id=1, source_target_pairs={{0,96},{16,112},{32,0},{48,16},{64,32},{80,48},{96,64},{112,80},{1... | collective-permute-start | bytes 1179656 | tf_op jit(solution)/shard_map/ppermute | solution.py:177
  153.7 25.3 %collective-permute-start.16 = (bf16[128,1536]{1,0:T(8,128)(2,1)S(1)}, bf16[128,1536]{1,0:T(8,128)(2,1)S(1)}, u32[]{:S(2)}, u32[]{:S(2)}) collective-permute-start(bf16[128,1536]{1,0:T(8,128)(2,1)S(1)} %pad_maximum_fusion.8), channel_id=1, source_target_pairs={{0,96},{16,112},{32,0},{48,16},{64,32},{80,48},{96,64},{112,80},{1... | collective-permute-start | bytes 1179656 | tf_op jit(solution)/shard_map/ppermute | solution.py:181
  159.6 20.7 %collective-permute-start.14 = (bf16[128,1536]{1,0:T(8,128)(2,1)S(1)}, bf16[128,1536]{1,0:T(8,128)(2,1)S(1)}, u32[]{:S(2)}, u32[]{:S(2)}) collective-permute-start(bf16[128,1536]{1,0:T(8,128)(2,1)S(1)} %pad_maximum_fusion.7), channel_id=1, source_target_pairs={{0,32},{16,48},{32,64},{48,80},{64,96},{80,112},{96,0},{112,16},{1... | collective-permute-start | bytes 1179656 | tf_op jit(solution)/shard_map/ppermute | solution.py:180
  168.0 28.1 %collective-permute-start.12 = (bf16[128,1536]{1,0:T(8,128)(2,1)S(1)}, bf16[128,1536]{1,0:T(8,128)(2,1)S(1)}, u32[]{:S(2)}, u32[]{:S(2)}) collective-permute-start(bf16[128,1536]{1,0:T(8,128)(2,1)S(1)} %pad_maximum_fusion.6), channel_id=1, source_target_pairs={{0,96},{16,112},{32,0},{48,16},{64,32},{80,48},{96,64},{112,80},{1... | collective-permute-start | bytes 1179656 | tf_op jit(solution)/shard_map/ppermute | solution.py:181
  169.2 27.3 %collective-permute-start.10 = (bf16[128,1536]{1,0:T(8,128)(2,1)}, bf16[128,1536]{1,0:T(8,128)(2,1)}, u32[]{:S(2)}, u32[]{:S(2)}) collective-permute-start(bf16[128,1536]{1,0:T(8,128)(2,1)} %pad_maximum_fusion.5), channel_id=1, source_target_pairs={{0,32},{16,48},{32,64},{48,80},{64,96},{80,112},{96,0},{112,16},{1... | collective-permute-start | bytes 1179656 | tf_op jit(solution)/shard_map/ppermute | solution.py:180
  172.0 32.3 %collective-permute-start.7 = (bf16[192,2048]{1,0:T(8,128)(2,1)}, bf16[192,2048]{1,0:T(8,128)(2,1)}, u32[]{:S(2)}, u32[]{:S(2)}) collective-permute-start(bf16[192,2048]{1,0:T(8,128)(2,1)} %pad_maximum_fusion.4), channel_id=1, source_target_pairs={{0,96},{16,112},{32,0},{48,16},{64,32},{80,48},{96,64},{112,80},{1... | collective-permute-start | bytes 2359304 | tf_op jit(solution)/shard_map/ppermute | solution.py:181
  178.9 25.4 %collective-permute-start.5 = (bf16[192,2048]{1,0:T(8,128)(2,1)}, bf16[192,2048]{1,0:T(8,128)(2,1)}, u32[]{:S(2)}, u32[]{:S(2)}) collective-permute-start(bf16[192,2048]{1,0:T(8,128)(2,1)} %pad_maximum_fusion.3), channel_id=1, source_target_pairs={{0,32},{16,48},{32,64},{48,80},{64,96},{80,112},{96,0},{112,16},{1... | collective-permute-start | bytes 2359304 | tf_op jit(solution)/shard_map/ppermute | solution.py:180
  181.3 16.5 %collective-permute-start.17 = (bf16[128,1536]{1,0:T(8,128)(2,1)}, bf16[128,1536]{1,0:T(8,128)(2,1)}, u32[]{:S(2)}, u32[]{:S(2)}) collective-permute-start(bf16[128,1536]{1,0:T(8,128)(2,1)} %fusion.22), channel_id=1, source_target_pairs={{0,16},{16,0},{32,48},{48,32},{64,80},{80,64},{96,112},{112,96},{1... | collective-permute-start | bytes 1179656 | tf_op jit(solution)/shard_map/ppermute | solution.py:196
  183.2 35.9 %all-to-all-start.2 = ((bf16[16,32,1536]{2,1,0:T(8,128)(2,1)}), bf16[16,32,1536]{2,1,0:T(8,128)(2,1)}, u32[]{:S(2)}, u32[]{:S(2)}) async-start(bf16[16,32,1536]{2,1,0:T(8,128)(2,1)} %bitcast.199), calls=%async_computation.2 | async-start | bytes 3145728 | tf_op jit(solution)/shard_map/all_to_all | solution.py:370
  196.2 58.3 %collective-permute-start.3 = (bf16[192,2048]{1,0:T(8,128)(2,1)}, bf16[192,2048]{1,0:T(8,128)(2,1)S(1)}, u32[]{:S(2)}, u32[]{:S(2)}) collective-permute-start(bf16[192,2048]{1,0:T(8,128)(2,1)} %pad_maximum_fusion.2), channel_id=1, source_target_pairs={{0,96},{16,112},{32,0},{48,16},{64,32},{80,48},{96,64},{112,80},{1... | collective-permute-start | bytes 2359304 | tf_op jit(solution)/shard_map/ppermute | solution.py:181
  196.5 57.9 %collective-permute-start.1 = (bf16[192,2048]{1,0:T(8,128)(2,1)}, bf16[192,2048]{1,0:T(8,128)(2,1)}, u32[]{:S(2)}, u32[]{:S(2)}) collective-permute-start(bf16[192,2048]{1,0:T(8,128)(2,1)} %pad_maximum_fusion.1), channel_id=1, source_target_pairs={{0,32},{16,48},{32,64},{48,80},{64,96},{80,112},{96,0},{112,16},{1... | collective-permute-start | bytes 2359304 | tf_op jit(solution)/shard_map/ppermute | solution.py:180
  207.2 47.2 %collective-permute-start.8 = (bf16[192,2048]{1,0:T(8,128)(2,1)}, bf16[192,2048]{1,0:T(8,128)(2,1)}, u32[]{:S(2)}, u32[]{:S(2)}) collective-permute-start(bf16[192,2048]{1,0:T(8,128)(2,1)} %fusion.11), channel_id=1, source_target_pairs={{0,16},{16,0},{32,48},{48,32},{64,80},{80,64},{96,112},{112,96},{1... | collective-permute-start | bytes 2359304 | tf_op jit(solution)/shard_map/ppermute | solution.py:196
  209.1 17.4 %copy-start.11 = (s32[4,128]{1,0:T(4,128)S(1)}, s32[4,128]{1,0:T(4,128)}, u32[]{:S(2)}) copy-start(s32[4,128]{1,0:T(4,128)} %eq.41) | copy-start | bytes 6148
  210.3 18.0 %copy-start.8 = (bf16[1536,16]{0,1:T(8,128)(2,1)S(1)}, bf16[1536,16]{0,1:T(8,128)(2,1)}, u32[]{:S(2)}) copy-start(bf16[1536,16]{0,1:T(8,128)(2,1)} %param.10) | copy-start | bytes 147460
  219.1 18.6 %all-to-all-start.3 = ((f32[128,1,192]{2,1,0:T(1,128)}), f32[128,1,192]{2,1,0:T(1,128)S(1)}, u32[]{:S(2)}, u32[]{:S(2)}) async-start(f32[128,1,192]{2,1,0:T(1,128)} %all_to_all.25), calls=%async_computation.3 | async-start | bytes 262144 | tf_op jit(solution)/shard_map/all_to_all | solution.py:408
  228.3 16.7 %copy-start.12 = (f32[4,128]{1,0:T(4,128)S(1)}, f32[4,128]{1,0:T(4,128)}, u32[]{:S(2)}) copy-start(f32[4,128]{1,0:T(4,128)} %mul.88) | copy-start | bytes 6148
  238.6 14.4 %all-to-all-start.4 = ((f32[128,1,192]{2,1,0:T(1,128)}), f32[128,1,192]{2,1,0:T(1,128)S(1)}, u32[]{:S(2)}, u32[]{:S(2)}) async-start(f32[128,1,192]{2,1,0:T(1,128)} %broadcast_in_dim.32), calls=%async_computation.4 | async-start | bytes 262144 | tf_op jit(solution)/shard_map/all_to_all | solution.py:414
  (9 other events, 19.6 us)

commit v10 on v8

--- a/solution.py
+++ b/solution.py
@@ -238,21 +238,17 @@
             send(a, 2, shards[a], me, whole, partner),
         ]
     mate = partner
+    forwards, mates = [], []
     for a in range(count):
         whole, low, high = spans[a]
         first[3 * a].wait_recv()
-        to_right = send(a, 3, outs[a].at[left, low], left, low, right)
+        forwards.append(send(a, 3, outs[a].at[left, low], left, low, right))
         first[3 * a + 1].wait_recv()
-        to_left = send(a, 4, outs[a].at[right, high], right, high, left)
-        second += [to_right, to_left]
-    for a in range(count):
-        whole = spans[a][0]
+        forwards.append(send(a, 4, outs[a].at[right, high], right, high, left))
         first[3 * a + 2].wait_recv()
-        second += [
-            send(a, 5, outs[a].at[mate], mate, whole, right),
-            send(a, 6, outs[a].at[mate], mate, whole, left),
-        ]
-    forwards, mates = second[: 2 * count], second[2 * count :]
+        mates.append(send(a, 5, outs[a].at[mate], mate, whole, right))
+        mates.append(send(a, 6, outs[a].at[mate], mate, whole, left))
+    second = forwards + mates
     mate_left, mate_right = lax.rem(mate + n - 2, n), lax.rem(mate + 2, n)
     for a in range(count):
         whole, low, high = spans[a]

time: 261 us -> 270 us (1.034)
  Pallas kernels: 83.6 us -> 91.9 us
    pallas_call x1, Pallas kernels: 83.6 us -> 91.9 us  [dp_gather_kernel(): pl.pallas_call(functools.partial(_ring_gather_kernel, n), out_shape=[jax....]
  transfers between devices with their start and end apart: 23 -> 23, of which waited for: 8 -> 8; matrix products, arithmetic and copies ran while one was open for 14% -> 14% of each run, Pallas kernels for 32% -> 35%
where the time goes in v10:
time: 270 us; the launch traced here: 266 us
  Pallas kernels  91.9 us (34%)
  starting transfers between devices  58.8 us (22%)
  waiting for transfers between devices  40.6 us (15%)
  matrix products  33.5 us (12%)
  local copies, waits for them, and re-layouts  21.1 us (8%)
  other arithmetic  19.3 us (7%)
    pallas_call x1, Pallas kernels, dp_gather_kernel(): pl.pallas_call(functools.partial(_ring_gather_kernel, n), out_shape=[jax....  91.9 us
    all_to_all x1, starting transfers between devices, body(): lax.all_to_all(d_rows.reshape(expert_count_axis, -1, model_width), 'exper...  12.9 us
    ppermute x4, waiting for transfers between devices, x_ring_scatter(): low = lax.ppermute(blocks[2][:h].astype(jnp.bfloat16), 'dp', _x_shift(n, 1))  10.6 us
    ppermute x4, waiting for transfers between devices, x_ring_scatter(): lax.ppermute(to_left.astype(jnp.bfloat16), 'dp', _x_shift(n, -1))  9.1 us
    all_to_all x1, starting transfers between devices, body(): lax.all_to_all(jnp.concatenate([picked, scaled_cot], axis=1), 'expert', 0...  8.63 us
    all_to_all x1, waiting for transfers between devices, body(): lax.all_to_all(router_full.reshape(devices, -1), ('dp', 'expert'), 0, 0,...  8.13 us
    all_to_all x1, starting transfers between devices, body(): lax.all_to_all(expert_out.reshape(expert_count_axis, -1, model_width), 'e...  7.91 us
    all_to_all x1, waiting for transfers between devices, body(): lax.all_to_all(d_rows.reshape(expert_count_axis, -1, model_width), 'exper...  7.73 us
  transfers between devices with their start and end apart: 23, of which 8 were waited for; matrix products, arithmetic and copies ran while one was open for 14% of the time, Pallas kernels for 35%

profile of v10, /device:TPU:5, one launch (start us, length us, event | category | flops | bytes accessed | tf_op | source)
XLA Modules:
  0.0 266.2 jit_solution(5310199521144637807)
XLA Ops:
  2.9 4.5 %gather_fusion.2 = f32[512]{0:T(512)S(1)} fusion(f32[16,256]{1,0:T(8,128)S(1)} %bitcast.187, s32[512]{0:T(512)S(1)} %reshape.317), kind=kCustom, calls=%fused_computation.2 | custom fusion | bytes 8192 | tf_op jit(solution)/shard_map/jit(take_along_axis)/gather | solution.py:326
  7.9 2.9 %gather_fusion = bf16[512,1536]{1,0:T(8,128)(2,1)} fusion(bf16[256,1536]{1,0:T(8,128)(2,1)S(1)} %copy-done, s32[1024]{0:T(1024)S(1)} %pad_clamp_fusion), kind=kCustom, calls=%fused_computation | custom fusion | bytes 3147776 | tf_op jit(solution)/shard_map/gather | solution.py:325
  10.9 2.1 gather_fusion.1
  14.4 1.9 pad_maximum_fusion
  16.4 8.6 %all-to-all-start = ((bf16[16,64,1536]{2,1,0:T(8,128)(2,1)}), bf16[16,64,1536]{2,1,0:T(8,128)(2,1)}, u32[]{:S(2)}, u32[]{:S(2)}) async-start(bf16[16,64,1536]{2,1,0:T(8,128)(2,1)} %pad_maximum_fusion), calls=%async_computation | async-start | bytes 6291456 | tf_op jit(solution)/shard_map/all_to_all | solution.py:335
  26.8 91.9 %shard_map.118 = (bf16[8,192,1024]{2,1,0:T(8,128)(2,1)}, bf16[8,192,1024]{2,1,0:T(8,128)(2,1)}, bf16[8,128,1536]{2,1,0:T(8,128)(2,1)}) custom-call(bf16[192,1024]{1,0:T(8,128)(2,1)} %bitcast.206, bf16[192,1024]{1,0:T(8,128)(2,1)} %bitcast.207, bf16[128,1536]{1,0:T(8,128)(2,1)} %bitcast.208), custom_call_target="tpu_custom_call" | custom-call | tf_op jit(solution)/shard_map/pallas_call | solution.py:275
  118.7 2.2 fusion.39
  125.3 3.5 %multiply_convert_fusion = (bf16[512,1024]{1,0:T(8,128)(2,1)S(1)}, bf16[512,1024]{1,0:T(8,128)(2,1)}, bf16[512,1024]{1,0:T(8,128)(2,1)S(1)}) fusion(f32[512,1024]{1,0:T(8,128)S(1)} %fusion.40, f32[512,1024]{1,0:T(8,128)S(1)} %fusion.41, bf16[512,1536]{1,0:T(8,128)(2,1)S(1)} %bitcast.204, bf16[1024,1536]{1,0:T(8,128)(2,1)S(1)} %bitcast.215), kind=kOutput, calls=%fused_computation.24 | convolution fusion | flops 1618477056 | bytes 12058624 | tf_op jit(solution)/shard_map/erd,ehd->erh/dot_general | solution.py:354
  128.8 3.0 %convolution_convert_fusion.2 = bf16[512,1536]{1,0:T(8,128)(2,1)} fusion(bf16[512,1024]{1,0:T(8,128)(2,1)S(1)} %get-tuple-element.52, bf16[1024,1536]{1,0:T(8,128)(2,1)S(1)} %bitcast.216), kind=kOutput, calls=%fused_computation.16 | convolution fusion | flops 1611399168 | bytes 5767168 | tf_op jit(solution)/shard_map/erh,ehd->erd/dot_general | solution.py:346
  131.8 3.6 %convolution_convert_fusion.1 = bf16[1024,1536]{1,0:T(8,128)(2,1)} fusion(bf16[512,1024]{1,0:T(8,128)(2,1)S(1)} %get-tuple-element.52, bf16[512,1536]{1,0:T(8,128)(2,1)S(1)} %bitcast.205), kind=kOutput, calls=%fused_computation.7 | convolution fusion | flops 1612185600 | bytes 5767168 | tf_op jit(solution)/shard_map/erc,erd->cd/dot_general | solution.py:301
  135.3 7.9 %all-to-all-start.1 = ((bf16[16,32,1536]{2,1,0:T(8,128)(2,1)}), bf16[16,32,1536]{2,1,0:T(8,128)(2,1)}, u32[]{:S(2)}, u32[]{:S(2)}) async-start(bf16[16,32,1536]{2,1,0:T(8,128)(2,1)} %bitcast.200), calls=%async_computation.1 | async-start | bytes 3145728 | tf_op jit(solution)/shard_map/all_to_all | solution.py:349
  143.3 4.2 %fusion.42 = f32[512,1536]{1,0:T(8,128)S(1)} fusion(bf16[512,1024]{1,0:T(8,128)(2,1)} %get-tuple-element.51, bf16[1536,1024]{1,0:T(8,128)(2,1)} %bitcast.213), kind=kOutput, calls=%fused_computation.120 | convolution fusion | flops 1610612736 | bytes 7340032 | tf_op jit(solution)/shard_map/erh,edh->erd/dot_general | solution.py:361
  148.2 2.1 collective-permute-start.13
  150.6 3.1 %fusion.4 = bf16[512,1536]{1,0:T(8,128)(2,1)} fusion(f32[512,1536]{1,0:T(8,128)S(1)} %fusion.42, bf16[512,1024]{1,0:T(8,128)(2,1)S(1)} %get-tuple-element.50, bf16[1536,1024]{1,0:T(8,128)(2,1)S(1)} %bitcast.212), kind=kOutput, calls=%fused_computation.15 | convolution fusion | flops 1612185600 | bytes 8912896 | tf_op jit(solution)/shard_map/erh,edh->erd/dot_general | solution.py:362
  153.7 3.8 %convolution_convert_fusion = bf16[1536,2048]{1,0:T(8,128)(2,1)S(1)} fusion(bf16[512,1536]{1,0:T(8,128)(2,1)S(1)} %bitcast.203, bf16[1,512,1024]{2,1,0:T(8,128)(2,1)S(1)} %bitcast.217, bf16[1,512,1024]{2,1,0:T(8,128)(2,1)S(1)} %bitcast.218), kind=kOutput, calls=%fused_computation.3 | convolution fusion | flops 3228565504 | bytes 9961472 | tf_op jit(solution)/shard_map/erc,erk->ck/dot_general | solution.py:306
  159.1 2.6 collective-permute-start.4
  162.1 2.1 collective-permute-start.16
  165.1 3.0 %collective-permute-done = bf16[96,2048]{1,0:T(8,128)(2,1)S(1)} collective-permute-done((bf16[96,2048]{1,0:T(8,128)(2,1)S(1)}, bf16[96,2048]{1,0:T(8,128)(2,1)S(1)}, u32[]{:S(2)}, u32[]{:S(2)}) %collective-permute-start) | collective-permute-done | bytes 393248 | tf_op jit(solution)/shard_map/ppermute | solution.py:176
  168.9 7.6 %collective-permute-done.4 = bf16[96,2048]{1,0:T(8,128)(2,1)S(1)} collective-permute-done((bf16[96,2048]{1,0:T(8,128)(2,1)S(1)}, bf16[96,2048]{1,0:T(8,128)(2,1)S(1)}, u32[]{:S(2)}, u32[]{:S(2)}) %collective-permute-start.4) | collective-permute-done | bytes 393248 | tf_op jit(solution)/shard_map/ppermute | solution.py:176
  182.6 4.8 %collective-permute-done.16 = bf16[128,1536]{1,0:T(8,128)(2,1)S(1)} collective-permute-done((bf16[128,1536]{1,0:T(8,128)(2,1)S(1)}, bf16[128,1536]{1,0:T(8,128)(2,1)S(1)}, u32[]{:S(2)}, u32[]{:S(2)}) %collective-permute-start.16) | collective-permute-done | bytes 393248 | tf_op jit(solution)/shard_map/ppermute | solution.py:181
  191.7 12.9 %all-to-all-start.2 = ((bf16[16,32,1536]{2,1,0:T(8,128)(2,1)}), bf16[16,32,1536]{2,1,0:T(8,128)(2,1)}, u32[]{:S(2)}, u32[]{:S(2)}) async-start(bf16[16,32,1536]{2,1,0:T(8,128)(2,1)} %bitcast.199), calls=%async_computation.2 | async-start | bytes 3145728 | tf_op jit(solution)/shard_map/all_to_all | solution.py:364
  206.1 2.3 fusion.25
  208.4 4.3 %collective-permute-done.7 = bf16[192,2048]{1,0:T(8,128)(2,1)} collective-permute-done((bf16[192,2048]{1,0:T(8,128)(2,1)}, bf16[192,2048]{1,0:T(8,128)(2,1)}, u32[]{:S(2)}, u32[]{:S(2)}) %collective-permute-start.7) | collective-permute-done | bytes 786464 | tf_op jit(solution)/shard_map/ppermute | solution.py:181
  212.8 2.9 %fusion.11 = bf16[192,2048]{1,0:T(8,128)(2,1)} fusion(bf16[192,2048]{1,0:T(8,128)(2,1)} %collective-permute-done.7, bf16[192,2048]{1,0:T(8,128)(2,1)} %collective-permute-done.5, bf16[8,192,2048]{2,1,0:T(8,128)(2,1)} %bitcast.192, s32[]{:T(128)S(6)} %select_n.137), kind=kLoop, calls=%fused_computation.31 | loop fusion | flops 2359296 | bytes 3145732 | tf_op jit(solution)/shard_map/convert_element_type | solution.py:196
  215.7 1.9 fusion.1
  219.8 7.7 %all-to-all-done.2 = bf16[16,32,1536]{2,1,0:T(8,128)(2,1)} async-done(((bf16[16,32,1536]{2,1,0:T(8,128)(2,1)}), bf16[16,32,1536]{2,1,0:T(8,128)(2,1)}, u32[]{:S(2)}, u32[]{:S(2)}) %all-to-all-start.2) | async-done | bytes 1572896 | tf_op jit(solution)/shard_map/all_to_all | solution.py:364
  227.6 7.4 %all-to-all-start.3 = ((f32[128,1,192]{2,1,0:T(1,128)}), f32[128,1,192]{2,1,0:T(1,128)S(1)}, u32[]{:S(2)}, u32[]{:S(2)}) async-start(f32[128,1,192]{2,1,0:T(1,128)} %all_to_all.25), calls=%async_computation.3 | async-start | bytes 262144 | tf_op jit(solution)/shard_map/all_to_all | solution.py:402
  238.0 8.1 %all-to-all-done.3 = f32[128,1,192]{2,1,0:T(1,128)S(1)} async-done(((f32[128,1,192]{2,1,0:T(1,128)}), f32[128,1,192]{2,1,0:T(1,128)S(1)}, u32[]{:S(2)}, u32[]{:S(2)}) %all-to-all-start.3) | async-done | bytes 98336 | tf_op jit(solution)/shard_map/all_to_all | solution.py:402
  247.0 6.4 %all-to-all-start.4 = ((f32[128,1,192]{2,1,0:T(1,128)}), f32[128,1,192]{2,1,0:T(1,128)S(1)}, u32[]{:S(2)}, u32[]{:S(2)}) async-start(f32[128,1,192]{2,1,0:T(1,128)} %broadcast_in_dim.32), calls=%async_computation.4 | async-start | bytes 262144 | tf_op jit(solution)/shard_map/all_to_all | solution.py:408
  253.4 4.0 %fusion.5 = bf16[4,64,1536]{2,1,0:T(8,128)(2,1)} fusion(f32[4,128]{1,0:T(4,128)S(1)} %copy-done.12, s32[4,128]{1,0:T(4,128)S(1)} %copy-done.11, bf16[16,32,1536]{2,1,0:T(8,128)(2,1)} %all-to-all-done.1), kind=kOutput, calls=%fused_computation.18 | convolution fusion | flops 605978624 | bytes 2363392 | tf_op jit(solution)/shard_map/wze,wzi->wei/dot_general | solution.py:373
  257.4 4.0 %all-to-all-done.4 = f32[128,1,192]{2,1,0:T(1,128)S(1)} async-done(((f32[128,1,192]{2,1,0:T(1,128)}), f32[128,1,192]{2,1,0:T(1,128)S(1)}, u32[]{:S(2)}, u32[]{:S(2)}) %all-to-all-start.4) | async-done | bytes 98336 | tf_op jit(solution)/shard_map/all_to_all | solution.py:408
  262.9 2.1 fusion.13
  (119 shorter events, 35.5 us)
Async XLA Ops:
  2.9 4.7 %copy-start.7 = (s32[4,16,8]{1,2,0:T(8,128)S(1)}, s32[4,16,8]{1,2,0:T(8,128)}, u32[]{:S(2)}) copy-start(s32[4,16,8]{1,2,0:T(8,128)} %param.9) | copy-start | bytes 6148
  16.4 102.3 %all-to-all-start = ((bf16[16,64,1536]{2,1,0:T(8,128)(2,1)}), bf16[16,64,1536]{2,1,0:T(8,128)(2,1)}, u32[]{:S(2)}, u32[]{:S(2)}) async-start(bf16[16,64,1536]{2,1,0:T(8,128)(2,1)} %pad_maximum_fusion), calls=%async_computation | async-start | bytes 6291456 | tf_op jit(solution)/shard_map/all_to_all | solution.py:335
  25.2 95.8 %copy-start.9 = (s32[4,16,8]{2,1,0:T(8,128)}, s32[4,16,8]{2,1,0:T(8,128)S(1)}, u32[]{:S(2)}) copy-start(s32[4,16,8]{2,1,0:T(8,128)S(1)} %copy.55) | copy-start | bytes 6148
  135.3 56.3 %all-to-all-start.1 = ((bf16[16,32,1536]{2,1,0:T(8,128)(2,1)}), bf16[16,32,1536]{2,1,0:T(8,128)(2,1)}, u32[]{:S(2)}, u32[]{:S(2)}) async-start(bf16[16,32,1536]{2,1,0:T(8,128)(2,1)} %bitcast.200), calls=%async_computation.1 | async-start | bytes 3145728 | tf_op jit(solution)/shard_map/all_to_all | solution.py:349
  143.3 4.2 %copy-start.4 = (bf16[1024,1536]{1,0:T(8,128)(2,1)S(1)}, bf16[1024,1536]{1,0:T(8,128)(2,1)}, u32[]{:S(2)}) copy-start(bf16[1024,1536]{1,0:T(8,128)(2,1)} %convolution_convert_fusion.1) | copy-start | bytes 9437188
  147.5 3.2 %copy-start.14 = (bf16[8,192,1024]{2,1,0:T(8,128)(2,1)S(1)}, bf16[8,192,1024]{2,1,0:T(8,128)(2,1)}, u32[]{:S(2)}) copy-start(bf16[8,192,1024]{2,1,0:T(8,128)(2,1)} %get-tuple-element.10) | copy-start | bytes 9437188
  147.6 11.5 %collective-permute-start.9 = (bf16[64,1536]{1,0:T(8,128)(2,1)S(1)}, bf16[64,1536]{1,0:T(8,128)(2,1)S(1)}, u32[]{:S(2)}, u32[]{:S(2)}) collective-permute-start(bf16[64,1536]{1,0:T(8,128)(2,1)S(1)} %get-tuple-element.57), channel_id=1, source_target_pairs={{0,32},{16,48},{32,64},{48,80},{64,96},{80,112},{96,0},{112,16},{1... | collective-permute-start | bytes 589832 | tf_op jit(solution)/shard_map/ppermute | solution.py:176
  148.2 13.6 %collective-permute-start.13 = (bf16[64,1536]{1,0:T(8,128)(2,1)S(1)}, bf16[64,1536]{1,0:T(8,128)(2,1)S(1)}, u32[]{:S(2)}, u32[]{:S(2)}) collective-permute-start(bf16[64,1536]{1,0:T(8,128)(2,1)S(1)} %get-tuple-element.59), channel_id=1, source_target_pairs={{0,32},{16,48},{32,64},{48,80},{64,96},{80,112},{96,0},{112,16},{1... | collective-permute-start | bytes 589832 | tf_op jit(solution)/shard_map/ppermute | solution.py:176
  150.3 11.4 %collective-permute-start.15 = (bf16[64,1536]{1,0:T(8,128)(2,1)S(1)}, bf16[64,1536]{1,0:T(8,128)(2,1)S(1)}, u32[]{:S(2)}, u32[]{:S(2)}) collective-permute-start(bf16[64,1536]{1,0:T(8,128)(2,1)S(1)} %get-tuple-element.61), channel_id=1, source_target_pairs={{0,96},{16,112},{32,0},{48,16},{64,32},{80,48},{96,64},{112,80},{1... | collective-permute-start | bytes 589832 | tf_op jit(solution)/shard_map/ppermute | solution.py:177
  150.3 11.5 %collective-permute-start.11 = (bf16[64,1536]{1,0:T(8,128)(2,1)S(1)}, bf16[64,1536]{1,0:T(8,128)(2,1)S(1)}, u32[]{:S(2)}, u32[]{:S(2)}) collective-permute-start(bf16[64,1536]{1,0:T(8,128)(2,1)S(1)} %get-tuple-element.63), channel_id=1, source_target_pairs={{0,96},{16,112},{32,0},{48,16},{64,32},{80,48},{96,64},{112,80},{1... | collective-permute-start | bytes 589832 | tf_op jit(solution)/shard_map/ppermute | solution.py:177
  150.6 3.1 %copy-start.17 = (bf16[512,1024]{1,0:T(8,128)(2,1)S(1)}, bf16[512,1024]{1,0:T(8,128)(2,1)}, u32[]{:S(2)}) copy-start(bf16[512,1024]{1,0:T(8,128)(2,1)} %get-tuple-element.51) | copy-start | bytes 3145732
  157.5 21.4 %copy-start.3 = (bf16[1536,2048]{1,0:T(8,128)(2,1)}, bf16[1536,2048]{1,0:T(8,128)(2,1)S(1)}, u32[]{:S(2)}) copy-start(bf16[1536,2048]{1,0:T(8,128)(2,1)S(1)} %convolution_convert_fusion) | copy-start | bytes 18874372
  157.8 10.3 %collective-permute-start = (bf16[96,2048]{1,0:T(8,128)(2,1)S(1)}, bf16[96,2048]{1,0:T(8,128)(2,1)S(1)}, u32[]{:S(2)}, u32[]{:S(2)}) collective-permute-start(bf16[96,2048]{1,0:T(8,128)(2,1)S(1)} %get-tuple-element.42), channel_id=1, source_target_pairs={{0,32},{16,48},{32,64},{48,80},{64,96},{80,112},{96,0},{112,16},{1... | collective-permute-start | bytes 1179656 | tf_op jit(solution)/shard_map/ppermute | solution.py:176
  159.1 17.4 %collective-permute-start.4 = (bf16[96,2048]{1,0:T(8,128)(2,1)S(1)}, bf16[96,2048]{1,0:T(8,128)(2,1)S(1)}, u32[]{:S(2)}, u32[]{:S(2)}) collective-permute-start(bf16[96,2048]{1,0:T(8,128)(2,1)S(1)} %get-tuple-element.44), channel_id=1, source_target_pairs={{0,32},{16,48},{32,64},{48,80},{64,96},{80,112},{96,0},{112,16},{1... | collective-permute-start | bytes 1179656 | tf_op jit(solution)/shard_map/ppermute | solution.py:176
  161.8 15.9 %collective-permute-start.6 = (bf16[96,2048]{1,0:T(8,128)(2,1)S(1)}, bf16[96,2048]{1,0:T(8,128)(2,1)S(1)}, u32[]{:S(2)}, u32[]{:S(2)}) collective-permute-start(bf16[96,2048]{1,0:T(8,128)(2,1)S(1)} %get-tuple-element.46), channel_id=1, source_target_pairs={{0,96},{16,112},{32,0},{48,16},{64,32},{80,48},{96,64},{112,80},{1... | collective-permute-start | bytes 1179656 | tf_op jit(solution)/shard_map/ppermute | solution.py:177
  161.8 17.2 %collective-permute-start.2 = (bf16[96,2048]{1,0:T(8,128)(2,1)S(1)}, bf16[96,2048]{1,0:T(8,128)(2,1)S(1)}, u32[]{:S(2)}, u32[]{:S(2)}) collective-permute-start(bf16[96,2048]{1,0:T(8,128)(2,1)S(1)} %get-tuple-element.48), channel_id=1, source_target_pairs={{0,96},{16,112},{32,0},{48,16},{64,32},{80,48},{96,64},{112,80},{1... | collective-permute-start | bytes 1179656 | tf_op jit(solution)/shard_map/ppermute | solution.py:177
  162.1 25.3 %collective-permute-start.16 = (bf16[128,1536]{1,0:T(8,128)(2,1)S(1)}, bf16[128,1536]{1,0:T(8,128)(2,1)S(1)}, u32[]{:S(2)}, u32[]{:S(2)}) collective-permute-start(bf16[128,1536]{1,0:T(8,128)(2,1)S(1)} %pad_maximum_fusion.8), channel_id=1, source_target_pairs={{0,96},{16,112},{32,0},{48,16},{64,32},{80,48},{96,64},{112,80},{1... | collective-permute-start | bytes 1179656 | tf_op jit(solution)/shard_map/ppermute | solution.py:181
  168.1 20.7 %collective-permute-start.14 = (bf16[128,1536]{1,0:T(8,128)(2,1)S(1)}, bf16[128,1536]{1,0:T(8,128)(2,1)S(1)}, u32[]{:S(2)}, u32[]{:S(2)}) collective-permute-start(bf16[128,1536]{1,0:T(8,128)(2,1)S(1)} %pad_maximum_fusion.7), channel_id=1, source_target_pairs={{0,32},{16,48},{32,64},{48,80},{64,96},{80,112},{96,0},{112,16},{1... | collective-permute-start | bytes 1179656 | tf_op jit(solution)/shard_map/ppermute | solution.py:180
  176.5 28.1 %collective-permute-start.12 = (bf16[128,1536]{1,0:T(8,128)(2,1)S(1)}, bf16[128,1536]{1,0:T(8,128)(2,1)S(1)}, u32[]{:S(2)}, u32[]{:S(2)}) collective-permute-start(bf16[128,1536]{1,0:T(8,128)(2,1)S(1)} %pad_maximum_fusion.6), channel_id=1, source_target_pairs={{0,96},{16,112},{32,0},{48,16},{64,32},{80,48},{96,64},{112,80},{1... | collective-permute-start | bytes 1179656 | tf_op jit(solution)/shard_map/ppermute | solution.py:181
  177.7 27.3 %collective-permute-start.10 = (bf16[128,1536]{1,0:T(8,128)(2,1)}, bf16[128,1536]{1,0:T(8,128)(2,1)}, u32[]{:S(2)}, u32[]{:S(2)}) collective-permute-start(bf16[128,1536]{1,0:T(8,128)(2,1)} %pad_maximum_fusion.5), channel_id=1, source_target_pairs={{0,32},{16,48},{32,64},{48,80},{64,96},{80,112},{96,0},{112,16},{1... | collective-permute-start | bytes 1179656 | tf_op jit(solution)/shard_map/ppermute | solution.py:180
  180.5 32.3 %collective-permute-start.7 = (bf16[192,2048]{1,0:T(8,128)(2,1)}, bf16[192,2048]{1,0:T(8,128)(2,1)}, u32[]{:S(2)}, u32[]{:S(2)}) collective-permute-start(bf16[192,2048]{1,0:T(8,128)(2,1)} %pad_maximum_fusion.4), channel_id=1, source_target_pairs={{0,96},{16,112},{32,0},{48,16},{64,32},{80,48},{96,64},{112,80},{1... | collective-permute-start | bytes 2359304 | tf_op jit(solution)/shard_map/ppermute | solution.py:181
  187.4 25.4 %collective-permute-start.5 = (bf16[192,2048]{1,0:T(8,128)(2,1)}, bf16[192,2048]{1,0:T(8,128)(2,1)}, u32[]{:S(2)}, u32[]{:S(2)}) collective-permute-start(bf16[192,2048]{1,0:T(8,128)(2,1)} %pad_maximum_fusion.3), channel_id=1, source_target_pairs={{0,32},{16,48},{32,64},{48,80},{64,96},{80,112},{96,0},{112,16},{1... | collective-permute-start | bytes 2359304 | tf_op jit(solution)/shard_map/ppermute | solution.py:180
  189.7 16.4 %collective-permute-start.17 = (bf16[128,1536]{1,0:T(8,128)(2,1)}, bf16[128,1536]{1,0:T(8,128)(2,1)}, u32[]{:S(2)}, u32[]{:S(2)}) collective-permute-start(bf16[128,1536]{1,0:T(8,128)(2,1)} %fusion.22), channel_id=1, source_target_pairs={{0,16},{16,0},{32,48},{48,32},{64,80},{80,64},{96,112},{112,96},{1... | collective-permute-start | bytes 1179656 | tf_op jit(solution)/shard_map/ppermute | solution.py:196
  191.7 35.9 %all-to-all-start.2 = ((bf16[16,32,1536]{2,1,0:T(8,128)(2,1)}), bf16[16,32,1536]{2,1,0:T(8,128)(2,1)}, u32[]{:S(2)}, u32[]{:S(2)}) async-start(bf16[16,32,1536]{2,1,0:T(8,128)(2,1)} %bitcast.199), calls=%async_computation.2 | async-start | bytes 3145728 | tf_op jit(solution)/shard_map/all_to_all | solution.py:364
  204.6 58.3 %collective-permute-start.3 = (bf16[192,2048]{1,0:T(8,128)(2,1)}, bf16[192,2048]{1,0:T(8,128)(2,1)S(1)}, u32[]{:S(2)}, u32[]{:S(2)}) collective-permute-start(bf16[192,2048]{1,0:T(8,128)(2,1)} %pad_maximum_fusion.2), channel_id=1, source_target_pairs={{0,96},{16,112},{32,0},{48,16},{64,32},{80,48},{96,64},{112,80},{1... | collective-permute-start | bytes 2359304 | tf_op jit(solution)/shard_map/ppermute | solution.py:181
  205.0 57.9 %collective-permute-start.1 = (bf16[192,2048]{1,0:T(8,128)(2,1)}, bf16[192,2048]{1,0:T(8,128)(2,1)}, u32[]{:S(2)}, u32[]{:S(2)}) collective-permute-start(bf16[192,2048]{1,0:T(8,128)(2,1)} %pad_maximum_fusion.1), channel_id=1, source_target_pairs={{0,32},{16,48},{32,64},{48,80},{64,96},{80,112},{96,0},{112,16},{1... | collective-permute-start | bytes 2359304 | tf_op jit(solution)/shard_map/ppermute | solution.py:180
  215.6 47.2 %collective-permute-start.8 = (bf16[192,2048]{1,0:T(8,128)(2,1)}, bf16[192,2048]{1,0:T(8,128)(2,1)}, u32[]{:S(2)}, u32[]{:S(2)}) collective-permute-start(bf16[192,2048]{1,0:T(8,128)(2,1)} %fusion.11), channel_id=1, source_target_pairs={{0,16},{16,0},{32,48},{48,32},{64,80},{80,64},{96,112},{112,96},{1... | collective-permute-start | bytes 2359304 | tf_op jit(solution)/shard_map/ppermute | solution.py:196
  217.5 17.4 %copy-start.11 = (s32[4,128]{1,0:T(4,128)S(1)}, s32[4,128]{1,0:T(4,128)}, u32[]{:S(2)}) copy-start(s32[4,128]{1,0:T(4,128)} %eq.41) | copy-start | bytes 6148
  218.7 18.0 %copy-start.8 = (bf16[1536,16]{0,1:T(8,128)(2,1)S(1)}, bf16[1536,16]{0,1:T(8,128)(2,1)}, u32[]{:S(2)}) copy-start(bf16[1536,16]{0,1:T(8,128)(2,1)} %param.10) | copy-start | bytes 147460
  227.6 18.6 %all-to-all-start.3 = ((f32[128,1,192]{2,1,0:T(1,128)}), f32[128,1,192]{2,1,0:T(1,128)S(1)}, u32[]{:S(2)}, u32[]{:S(2)}) async-start(f32[128,1,192]{2,1,0:T(1,128)} %all_to_all.25), calls=%async_computation.3 | async-start | bytes 262144 | tf_op jit(solution)/shard_map/all_to_all | solution.py:402
  236.7 16.7 %copy-start.12 = (f32[4,128]{1,0:T(4,128)S(1)}, f32[4,128]{1,0:T(4,128)}, u32[]{:S(2)}) copy-start(f32[4,128]{1,0:T(4,128)} %mul.88) | copy-start | bytes 6148
  247.0 14.4 %all-to-all-start.4 = ((f32[128,1,192]{2,1,0:T(1,128)}), f32[128,1,192]{2,1,0:T(1,128)S(1)}, u32[]{:S(2)}, u32[]{:S(2)}) async-start(f32[128,1,192]{2,1,0:T(1,128)} %broadcast_in_dim.32), calls=%async_computation.4 | async-start | bytes 262144 | tf_op jit(solution)/shard_map/all_to_all | solution.py:408
  (9 other events, 19.6 us)
